TPU v7x, 32 devices: a whole 2x2x4 slice. The times are simulated.
32 devices in a mesh: dp: 8 (over y, x, core), ctx: 4 (over z).
Axes of the slice: x: 2, y: 2, z: 4, core: 2. Of those that a mesh axis runs over, the one named last changes fastest.
Arguments:
- queries: bfloat16 [6144, 2048], P(('dp', 'ctx')), parts along dimension 0, may hold values from -6 to 6
- keys: bfloat16 [6144, 2048], P(('dp', 'ctx')), parts along dimension 0, may hold values from -6 to 6
- values: bfloat16 [6144, 2048], P(('dp', 'ctx')), parts along dimension 0, may hold values from -6 to 6
- beta: float32 [6144, 16], P(('dp', 'ctx')), parts along dimension 0, may hold values from 0.01 to 0.1
- log_decay: bfloat16 [6144, 2048], P(('dp', 'ctx')), parts along dimension 0, may hold values from -0.6 to 0
- out_gain: float32 [2048], replicated, may hold values from 0.25 to 1.75
- doc_lengths: int32 [128], P('dp'), parts along dimension 0, may hold values from 1 to 384, 768 in all
Outputs:
- mixed: bfloat16 [6144, 2048], P(('dp', 'ctx')), parts along dimension 0
There are 8 independent parts, one for each index of `dp`. A program takes and returns all parts, laid end to end along the dimension named above; an argument that names none is the same for every part. Nothing has to cross between parts.
All inputs are finite; a program needn't handle non-finite values.
Results may differ from a plain program's by a relative error of at most 0.001.
Values sent between devices are 32-bit elements; how exact they have to be, the bound alone decides.
No kernel may reach another device: no remote copies, remote signals or barrier semaphores. Data moves between devices by JAX's collectives and lax.ppermute only.
A program may use at most 128 MiB of HBM per device.

v0:
```python
import jax
import jax.numpy as jnp
from jax import lax
from jax.sharding import PartitionSpec as P

BLOCK = 64


HIGHEST_ACCURACY = lax.Precision.HIGHEST


def shifted(array, axis, by):
    devices = lax.axis_size(axis)
    pairs = [(i, i + by) for i in range(devices) if 0 <= i + by < devices]
    return lax.ppermute(array, axis, pairs)


def unit_rows(x):
    return x / jnp.sqrt(jnp.sum(x * x, axis=-1, keepdims=True) + 1e-06)


def head_matmul(left, right):
    return jnp.einsum("hij,hjk->hik", left, right, precision=HIGHEST_ACCURACY)


def lower_solve(system, right_side):
    return lax.linalg.triangular_solve(
        system, right_side, left_side=True, lower=True, unit_diagonal=True
    )


def local(queries, keys, values, beta, log_decay, out_gain, doc_lengths):
    count_rows = queries.shape[0]
    heads = beta.shape[1]
    width = queries.shape[1] // heads
    blocks = count_rows // BLOCK

    def split(x):
        return x.astype(jnp.float32).reshape(blocks, BLOCK, heads, width).transpose(0, 2, 1, 3)

    qn = unit_rows(split(queries))
    kn = unit_rows(split(keys))
    vals = split(values)
    logs = split(log_decay)
    strength = beta.reshape(blocks, BLOCK, heads).transpose(0, 2, 1)[..., None]
    order = jnp.arange(BLOCK)
    lower = (order[:, None] >= order[None, :]).astype(jnp.float32)
    strict = (order[:, None] > order[None, :]).astype(jnp.float32)
    cumul = jnp.einsum("ts,bhsc->bhtc", lower, logs, precision=HIGHEST_ACCURACY)
    starts = jnp.cumsum(doc_lengths) - doc_lengths
    place = lax.axis_index("ctx") * count_rows + jnp.arange(count_rows, dtype=jnp.int32)
    resets = jnp.sum((place[:, None] == starts[None, :]).astype(jnp.float32), axis=1).reshape(
        blocks, BLOCK
    )
    seen = jnp.einsum("ts,bs->bt", lower, resets, precision=HIGHEST_ACCURACY)
    same_doc = (seen[:, :, None] == seen[:, None, :]).astype(jnp.float32)[:, None]
    fresh = (seen == 0.0).astype(jnp.float32)[:, None, :, None]
    kpos = kn * jnp.exp(cumul)
    kneg = kn * jnp.exp(-cumul)
    qpos = qn * jnp.exp(cumul)
    inner = (
        jnp.einsum("bhtc,bhsc->bhts", kpos, kneg, precision=HIGHEST_ACCURACY)
        * same_doc
        * strict
        * strength
    )
    scores = (
        jnp.einsum("bhtc,bhsc->bhts", qpos, kneg, precision=HIGHEST_ACCURACY) * same_doc * lower
    )
    eye_block = jnp.eye(BLOCK, dtype=jnp.float32)
    system = eye_block + inner
    plain_upd = lower_solve(system, strength * vals)
    state_upd = lower_solve(system, strength * kpos * fresh)
    last_cumul = cumul[:, :, -1:, :]
    tail_same = same_doc[:, :, -1, :][..., None]
    khat = kneg * jnp.exp(last_cumul) * tail_same
    eye_width = jnp.eye(width, dtype=jnp.float32)
    keep_diag = jnp.exp(last_cumul[:, :, 0, :]) * fresh[:, :, -1, :]
    trans_a = keep_diag[..., :, None] * eye_width - jnp.einsum(
        "bhsc,bhsd->bhcd", khat, state_upd, precision=HIGHEST_ACCURACY
    )
    trans_b = jnp.einsum("bhsc,bhsv->bhcv", khat, plain_upd, precision=HIGHEST_ACCURACY)
    local_out = jnp.einsum("bhts,bhsv->bhtv", scores, plain_upd, precision=HIGHEST_ACCURACY)
    reach = qpos * fresh - jnp.einsum(
        "bhts,bhsc->bhtc", scores, state_upd, precision=HIGHEST_ACCURACY
    )

    def compose(carry, item):
        return ((head_matmul(item[0], carry[0]), head_matmul(item[0], carry[1]) + item[1]), None)

    eye_heads = jnp.broadcast_to(eye_width, (heads, width, width))
    empty = jnp.zeros((heads, width, width), jnp.float32)
    (span_a, span_b), _ = lax.scan(compose, (eye_heads, empty), (trans_a, trans_b))

    def hop(step, memory_state):
        sent = head_matmul(span_a, memory_state) + span_b
        return shifted(sent, "ctx", 1)

    incoming = lax.fori_loop(0, lax.axis_size("ctx") - 1, hop, empty)

    def advance(memory_state, item):
        return (head_matmul(item[0], memory_state) + item[1], memory_state)

    _, block_states = lax.scan(advance, incoming, (trans_a, trans_b))
    outs = local_out + jnp.einsum(
        "bhtc,bhcv->bhtv", reach, block_states, precision=HIGHEST_ACCURACY
    )
    scale = jnp.sqrt(jnp.mean(outs * outs, axis=-1, keepdims=True) + 1e-06)
    normed = outs / scale * out_gain.reshape(heads, width)[None, :, None, :]
    return normed.transpose(0, 2, 1, 3).reshape(count_rows, heads * width).astype(jnp.bfloat16)


def solution(mesh):
    return jax.shard_map(
        local,
        mesh=mesh,
        in_specs=(
            P(("dp", "ctx"), None),
            P(("dp", "ctx"), None),
            P(("dp", "ctx"), None),
            P(("dp", "ctx"), None),
            P(("dp", "ctx"), None),
            P(),
            P("dp"),
        ),
        out_specs=P(("dp", "ctx"), None),
        check_vma=False,
    )
```

profile of v0, /device:TPU:0, one launch (start us, length us, event | category | flops | bytes accessed | tf_op | source)
XLA Modules:
  0.0 410.8 jit_solution(5222230204377554510)
XLA Ops:
  11.0 4.7 %add_bitcast_fusion = f32[3,16,1,64,64]{4,3,2,1,0:T(8,128)} fusion(f32[64,64]{1,0:T(8,128)S(1)} %get-tuple-element.142, f32[3,16,64]{2,1,0:T(8,128)S(1)} %copy.31, f32[64,64]{1,0:T(8,128)S(1)} %get-tuple-element.141, f32[64,64]{1,0:T(8,128)S(1)} %get-tuple-element.140, f32[3,64,64]{2,1,0:T(8,128)S(1)} %compare_convert_fusion, ...), kind=kOutput, calls=%fused_computation.35 | convolution fusion | flops 305135616 | bytes 4059136 | tf_op jit(solution)/shard_map/bhtc,bhsc->bhts/dot_general | solution.py:62
  15.7 237.3 %custom-call.5 = f32[3,16,1,64,64]{3,4,2,1,0:T(8,128)} custom-call(f32[3,16,1,64,64]{4,3,2,1,0:T(8,128)} %add_bitcast_fusion), custom_call_target="InvertDiagBlocksLowerTriangular" | custom-call | tf_op jit(solution)/shard_map/triangular_solve/custom-call.1 | solution.py:27
  253.0 5.8 %multiply_multiply_fusion.1 = f32[3,16,64,64]{3,2,1,0:T(8,128)S(1)} fusion(f32[64,64]{1,0:T(8,128)S(1)} %fusion.44, f32[3,64,64]{2,1,0:T(8,128)S(1)} %compare_convert_fusion, f32[3,64,16,128]{3,2,1,0:T(8,128)} %bitcast.143, f32[3,16,64,128]{3,2,1,0:T(8,128)} %copy-done.3, f32[3,16,64]{2,1,0:T(8,128)S(1)} %get-tuple-element.138, ...), kind=kOutput, calls=%fused_computation.46 | convolution fusion | flops 304349184 | bytes 5595136 | tf_op jit(solution)/shard_map/bhtc,bhsc->bhts/dot_general | solution.py:68
  258.8 4.0 fusion.17
  262.9 3.0 fusion.55
  265.8 7.9 %multiply_subtract_fusion = f32[3,16,128,128]{3,2,1,0:T(8,128)} fusion(f32[3,16,64,128]{3,2,1,0:T(8,128)S(1)} %fusion.17, f32[128,128]{1,0:T(8,128)S(1)} %fusion.43, f32[3,16,128]{2,1,0:T(8,128)S(1)} %broadcast_multiply_fusion, f32[3,64]{1,0:T(4,128)S(1)} %convert_bitcast_fusion.3, f32[3,16,128]{2,1,0:T(8,128)S(1)} %bitcast.157, ...), kind=kOutput, calls=%fused_computation.18 | convolution fusion | flops 607518720 | bytes 7992064 | tf_op jit(solution)/shard_map/bhsc,bhsd->bhcd/dot_general | solution.py:79
  274.2 3.2 fusion.16
  277.4 2.9 fusion.54
  280.3 7.7 %fusion.32 = f32[3,16,128,128]{3,2,1,0:T(8,128)} fusion(f32[3,16,64,128]{3,2,1,0:T(8,128)S(1)} %fusion.16, f32[3,64]{1,0:T(4,128)S(1)} %convert_bitcast_fusion.3, f32[3,16,128]{2,1,0:T(8,128)S(1)} %bitcast.158, f32[3,16,64,128]{3,2,1,0:T(8,128)S(1)} %copy-done.5, f32[3,16,64]{2,1,0:T(8,128)S(1)} %get-tuple-element.137, f32[3,64,16,128]{3,2,1,0:T(8,128)S(1)} %bitcast.150), kind=kOutput, calls=%fused_computation.51 | convolution fusion | flops 605945856 | bytes 7901952 | tf_op jit(solution)/shard_map/bhsc,bhsv->bhcv/dot_general | solution.py:82
  288.0 16.4 %while.37 = (s32[]{:T(128)}, f32[16,128,128]{2,1,0:T(8,128)S(1)}, f32[16,128,128]{2,1,0:T(8,128)S(1)}, f32[3,16,128,128]{3,2,1,0:T(8,128)}, f32[3,16,128,128]{3,2,1,0:T(8,128)}, /*index=5*/s32[]{:T(128)}, s32[]{:T(128)}) while((s32[]{:T(128)}, f32[16,128,128]{2,1,0:T(8,128)S(1)}, f32[16,128,128]{2,1,0:T(8,128)S(1)}, ...), condition=%wide.region_5.7_spmd.clone, body=%wide.region_4.6_spmd.clone.sunk | while | flops 805830656 | bytes 24118908 | solution.py:93
  289.8 2.4 convolution_add_fusion.8
  300.8 2.4 convolution_add_fusion.8
  304.5 85.4 %while.35 = (s32[]{:T(128)}, f32[16,128,128]{2,1,0:T(8,128)S(1)}, f32[16,128,128]{2,1,0:T(8,128)S(1)}, f32[16,128,128]{2,1,0:T(8,128)S(1)}, s32[]{:T(128)}) while((s32[]{:T(128)}, f32[16,128,128]{2,1,0:T(8,128)S(1)}, f32[16,128,128]{2,1,0:T(8,128)S(1)}, f32[16,128,128]{2,1,0:T(8,128)S(1)}, s32[]{:T(128)}) %tuple.57), condition=%wide.region_7.9_spmd, body=%wide.region_6.8_spmd.sunk | while | flops 402915328 | bytes 8388709 | solution.py:99
  306.7 5.0 %collective-permute-start = (f32[16,128,128]{2,1,0:T(8,128)}, f32[16,128,128]{2,1,0:T(8,128)S(1)}, u32[]{:S(2)}, u32[]{:S(2)}) collective-permute-start(f32[16,128,128]{2,1,0:T(8,128)} %convolution_add_fusion.6), channel_id=1, source_target_pairs={{0,1},{1,2},{2,3},{4,5},{5,6},{6,7},{8,9},{9,10},{10,11},{12,13},{... | collective-permute-start | bytes 3145736 | tf_op jit(solution)/shard_map/while/body/eval_jaxpr/ppermute | solution.py:15
  311.7 22.6 %collective-permute-done = f32[16,128,128]{2,1,0:T(8,128)S(1)} collective-permute-done((f32[16,128,128]{2,1,0:T(8,128)}, f32[16,128,128]{2,1,0:T(8,128)S(1)}, u32[]{:S(2)}, u32[]{:S(2)}) %collective-permute-start) | collective-permute-done | bytes 1048608 | tf_op jit(solution)/shard_map/while/body/eval_jaxpr/ppermute | solution.py:15
  336.5 4.3 %collective-permute-start = (f32[16,128,128]{2,1,0:T(8,128)}, f32[16,128,128]{2,1,0:T(8,128)S(1)}, u32[]{:S(2)}, u32[]{:S(2)}) collective-permute-start(f32[16,128,128]{2,1,0:T(8,128)} %convolution_add_fusion.6), channel_id=1, source_target_pairs={{0,1},{1,2},{2,3},{4,5},{5,6},{6,7},{8,9},{9,10},{10,11},{12,13},{... | collective-permute-start | bytes 3145736 | tf_op jit(solution)/shard_map/while/body/eval_jaxpr/ppermute | solution.py:15
  340.8 21.8 %collective-permute-done = f32[16,128,128]{2,1,0:T(8,128)S(1)} collective-permute-done((f32[16,128,128]{2,1,0:T(8,128)}, f32[16,128,128]{2,1,0:T(8,128)S(1)}, u32[]{:S(2)}, u32[]{:S(2)}) %collective-permute-start) | collective-permute-done | bytes 1048608 | tf_op jit(solution)/shard_map/while/body/eval_jaxpr/ppermute | solution.py:15
  364.7 4.3 %collective-permute-start = (f32[16,128,128]{2,1,0:T(8,128)}, f32[16,128,128]{2,1,0:T(8,128)S(1)}, u32[]{:S(2)}, u32[]{:S(2)}) collective-permute-start(f32[16,128,128]{2,1,0:T(8,128)} %convolution_add_fusion.6), channel_id=1, source_target_pairs={{0,1},{1,2},{2,3},{4,5},{5,6},{6,7},{8,9},{9,10},{10,11},{12,13},{... | collective-permute-start | bytes 3145736 | tf_op jit(solution)/shard_map/while/body/eval_jaxpr/ppermute | solution.py:15
  369.1 20.8 %collective-permute-done = f32[16,128,128]{2,1,0:T(8,128)S(1)} collective-permute-done((f32[16,128,128]{2,1,0:T(8,128)}, f32[16,128,128]{2,1,0:T(8,128)S(1)}, u32[]{:S(2)}, u32[]{:S(2)}) %collective-permute-start) | collective-permute-done | bytes 1048608 | tf_op jit(solution)/shard_map/while/body/eval_jaxpr/ppermute | solution.py:15
  389.9 11.8 %while.36 = (s32[]{:T(128)}, f32[16,128,128]{2,1,0:T(8,128)S(1)}, f32[3,16,128,128]{3,2,1,0:T(8,128)}, f32[3,16,128,128]{3,2,1,0:T(8,128)}, f32[3,16,128,128]{3,2,1,0:T(8,128)}, /*index=5*/s32[]{:T(128)}) while((s32[]{:T(128)}, f32[16,128,128]{2,1,0:T(8,128)S(1)}, f32[3,16,128,128]{3,2,1,0:T(8,128)}, f32[3,16,128,128]{3,2,1,0:T(8,128)}, ...), condition=%wide.region_9.11_spmd, body=%wide.region_8.10_spmd.sunk | while | flops 402915328 | bytes 8389713 | solution.py:104
  391.1 2.7 convolution_add_fusion.7
  395.0 2.7 convolution_add_fusion.7
  399.0 2.7 convolution_add_fusion.7
  401.8 6.9 %multiply_reduce_fusion = (f32[3,16,64]{2,1,0:T(8,128)S(1)}, f32[3,16,64,128]{3,2,1,0:T(8,128)S(1)}) fusion(f32[3,16,64,128]{3,2,1,0:T(8,128)} %fusion.54, f32[3,16,128,128]{3,2,1,0:T(8,128)} %get-tuple-element.86, f32[3,16,64,128]{3,2,1,0:T(8,128)} %fusion.55, f32[3,64]{1,0:T(4,128)S(1)} %get-tuple-element.134, f32[3,16,64,128]{3,2,1,0:T(8,128)} %copy-done.3, ...), kind=kOutput, calls=%fused_computation.39 | convolution fusion | flops 606729216 | bytes 11035392 | tf_op jit(solution)/shard_map/bhtc,bhcv->bhtv/dot_general | solution.py:105
  (91 shorter events, 35.0 us)
Async XLA Ops:
  4.6 1.7 copy-start.9
  5.0 1.2 copy-start.3
  6.8 1.9 copy-start.1
  6.8 1.7 copy-start.10
  9.0 1.2 copy-start.6
  9.0 2.0 copy-start.4
  253.0 5.8 %copy-start.5 = (f32[3,16,64,128]{3,2,1,0:T(8,128)S(1)}, f32[3,16,64,128]{3,2,1,0:T(8,128)}, u32[]{:S(2)}) copy-start(f32[3,16,64,128]{3,2,1,0:T(8,128)} %copy-done.3) | copy-start | bytes 4718596
  253.0 5.8 %copy-start.7 = (f32[24,8,16,128]{3,2,1,0:T(8,128)S(1)}, f32[24,8,16,128]{3,2,1,0:T(8,128)}, u32[]{:S(2)}) copy-start(f32[24,8,16,128]{3,2,1,0:T(8,128)} %copy-done.6) | copy-start | bytes 4718596
  253.0 5.8 %copy-start.8 = (f32[3,16,1,64,64]{3,4,2,1,0:T(8,128)S(1)}, f32[3,16,1,64,64]{3,4,2,1,0:T(8,128)}, u32[]{:S(2)}) copy-start(f32[3,16,1,64,64]{3,4,2,1,0:T(8,128)} %custom-call.5) | copy-start | bytes 2359300
  265.8 7.9 %copy-start.11 = (bf16[192,2048]{1,0:T(8,128)(2,1)S(1)}, bf16[192,2048]{1,0:T(8,128)(2,1)}, u32[]{:S(2)}) copy-start(bf16[192,2048]{1,0:T(8,128)(2,1)} %param.17) | copy-start | bytes 2359300
  288.0 1.9 copy-start
  293.4 1.9 copy-start
  298.9 1.9 copy-start
  306.7 27.6 %collective-permute-start = (f32[16,128,128]{2,1,0:T(8,128)}, f32[16,128,128]{2,1,0:T(8,128)S(1)}, u32[]{:S(2)}, u32[]{:S(2)}) collective-permute-start(f32[16,128,128]{2,1,0:T(8,128)} %convolution_add_fusion.6), channel_id=1, source_target_pairs={{0,1},{1,2},{2,3},{4,5},{5,6},{6,7},{8,9},{9,10},{10,11},{12,13},{... | collective-permute-start | bytes 3145736 | tf_op jit(solution)/shard_map/while/body/eval_jaxpr/ppermute | solution.py:15
  336.5 26.1 %collective-permute-start = (f32[16,128,128]{2,1,0:T(8,128)}, f32[16,128,128]{2,1,0:T(8,128)S(1)}, u32[]{:S(2)}, u32[]{:S(2)}) collective-permute-start(f32[16,128,128]{2,1,0:T(8,128)} %convolution_add_fusion.6), channel_id=1, source_target_pairs={{0,1},{1,2},{2,3},{4,5},{5,6},{6,7},{8,9},{9,10},{10,11},{12,13},{... | collective-permute-start | bytes 3145736 | tf_op jit(solution)/shard_map/while/body/eval_jaxpr/ppermute | solution.py:15
  364.7 25.2 %collective-permute-start = (f32[16,128,128]{2,1,0:T(8,128)}, f32[16,128,128]{2,1,0:T(8,128)S(1)}, u32[]{:S(2)}, u32[]{:S(2)}) collective-permute-start(f32[16,128,128]{2,1,0:T(8,128)} %convolution_add_fusion.6), channel_id=1, source_target_pairs={{0,1},{1,2},{2,3},{4,5},{5,6},{6,7},{8,9},{9,10},{10,11},{12,13},{... | collective-permute-start | bytes 3145736 | tf_op jit(solution)/shard_map/while/body/eval_jaxpr/ppermute | solution.py:15
  389.9 11.8 %copy-start.2 = (f32[24,8,16,128]{3,2,1,0:T(8,128)S(1)}, f32[24,8,16,128]{3,2,1,0:T(8,128)}, u32[]{:S(2)}) copy-start(f32[24,8,16,128]{3,2,1,0:T(8,128)} %copy-done.1) | copy-start | bytes 4718596
  401.7 7.0 %copy-start.12 = (f32[2048]{0:T(1024)S(1)}, f32[2048]{0:T(1024)}, u32[]{:S(2)}) copy-start(f32[2048]{0:T(1024)} %param.20) | copy-start | bytes 24580
where the time goes:
time: 412 us; the launch traced here: 411 us
  other arithmetic  241 us (58%)
  matrix products  71.9 us (17%)
  waiting for transfers between devices  65.3 us (16%)
  local copies, waits for them, and re-layouts  18.6 us (5%)
  starting transfers between devices  13.7 us (3%)
    another operation x3, other arithmetic, lower_solve(): lax.linalg.triangular_solve(system, right_side, left_side=True, lower=Tru...  237 us
    ppermute x3, waiting for transfers between devices, shifted(): return lax.ppermute(array, axis, pairs)  65.3 us
    dot_general x12, matrix products, head_matmul(): return jnp.einsum('hij,hjk->hik', left, right, precision=HIGHEST_ACCURACY)  25.3 us
    ppermute x3, starting transfers between devices, shifted(): return lax.ppermute(array, axis, pairs)  13.7 us
  transfers between devices with their start and end apart: 3, of which 3 were waited for; matrix products, arithmetic and copies ran while one was open for 0% of the time, Pallas kernels for 0%

commit v1 on v0

v1 whole, which is shorter than its diff:
```python
import functools

import jax
import jax.numpy as jnp
from jax import lax
from jax.experimental import pallas as pl
from jax.experimental.pallas import tpu as pltpu
from jax.sharding import PartitionSpec as P

F32 = jnp.float32
BF16 = jnp.bfloat16
TILE = 32
BLOCK = 64
TOGETHER = 2


def halves(x):
    high = x.astype(BF16)
    return high, (x - high.astype(F32)).astype(BF16)


def dot(a, b, dims=((1,), (0,))):
    return lax.dot_general(a, b, (dims, ((), ())), preferred_element_type=F32)


def dot3(a, b, dims=((1,), (0,))):
    return dot(a[0], b[0], dims) + (dot(a[0], b[1], dims) + dot(a[1], b[0], dims))


def rows_of(pair, low, high):
    return pair[0][low:high], pair[1][low:high]


def unit_rows(x):
    return x * lax.rsqrt(jnp.sum(x * x, axis=-1, keepdims=True) + 1e-06)


def doc_ids(lengths_ref, first, shape, dim):
    docs = lengths_ref.shape[0]
    place = first + lax.broadcasted_iota(jnp.int32, shape, dim)
    ids = jnp.zeros(shape, jnp.int32)
    before = jnp.int32(0)
    start = jnp.int32(0)
    for d in range(docs):
        ids = ids + (place >= start).astype(jnp.int32)
        before = before + (first > start).astype(jnp.int32)
        start = start + lengths_ref[d]
    return ids, before


def tile_inverse(system, count):
    lane = lax.broadcasted_iota(jnp.int32, (TILE, count), 1)
    row = lax.broadcasted_iota(jnp.int32, (TILE, count), 0)
    side = jnp.zeros((TILE, count), F32)
    for b in range(count // TILE):
        side = jnp.where(lane // TILE == b, system[b * TILE : (b + 1) * TILE, :], side)
    parts = []
    for low in range(0, count, 128):
        high = min(low + 128, count)
        piece = side[:, low:high]
        if high - low < 128:
            piece = jnp.concatenate([piece, jnp.zeros((TILE, 128 - high + low), F32)], axis=1)
        lanes = lax.broadcasted_iota(jnp.int32, (TILE, 128), 1)
        home = lanes - lanes % TILE
        inverse = (lanes % TILE == lax.broadcasted_iota(jnp.int32, (TILE, 128), 0)).astype(F32)
        for j in range(TILE - 1):
            top = (j + 1) // 8 * 8
            column = jnp.take_along_axis(piece[top:], (home + j)[top:], axis=1, mode="promise_in_bounds")
            lower = inverse[top:] - column * inverse[j : j + 1, :]
            inverse = lower if top == 0 else jnp.concatenate([inverse[:top], lower], axis=0)
        parts.append(inverse[:, : high - low])
    return jnp.concatenate(parts, axis=1)


def spread(side, count, height, column_of):
    lane = lax.broadcasted_iota(jnp.int32, side.shape, 1)
    return jnp.concatenate(
        [jnp.where(column_of(lane) == b, side, 0.0) for b in range(count // height)], axis=0
    )


def block_inverses(system, count):
    small = tile_inverse(system, count)
    lane = lax.broadcasted_iota(jnp.int32, small.shape, 1)
    even = lane // TILE % 2 == 0
    below = jnp.zeros(small.shape, F32)
    for b in range(1, count // TILE, 2):
        below = jnp.where(lane // TILE == b - 1, system[b * TILE : (b + 1) * TILE, :], below)
    wide = spread(small, count, TILE, lambda x: x // TILE)
    middle = dot3(halves(below), halves(wide))
    tall = spread(middle, count, TILE, lambda x: jnp.where(x // TILE % 2 == 0, x // TILE + 1, -1))
    odd = jnp.where(even, 0.0, small)
    corner = dot3(halves(odd), halves(tall))
    return jnp.concatenate([jnp.where(even, small, 0.0), jnp.where(even, -corner, small)], axis=0)


def solve(system, right, count):
    inverses = block_inverses(system, count)
    split_system = halves(system)
    done = None
    for b in range(count // BLOCK):
        low, high = b * BLOCK, (b + 1) * BLOCK
        part = right[low:high]
        if b:
            left = tuple(x[low:high, :low] for x in split_system)
            part = part - dot3(left, done)
        result = halves(dot3(halves(inverses[:, low:high]), halves(part)))
        done = result if b == 0 else tuple(jnp.concatenate(x, axis=0) for x in zip(done, result))
    return done


def span_kernel(lengths_ref, q_ref, k_ref, v_ref, beta_ref, g_ref, a_ref, b_ref, out_ref, reach_ref):
    count = q_ref.shape[0]
    width = q_ref.shape[1] // TOGETHER
    first = lax.axis_index("ctx") * count
    ids_col, before = doc_ids(lengths_ref, first, (count, 1), 0)
    ids_row, _ = doc_ids(lengths_ref, first, (1, count), 1)
    row = lax.broadcasted_iota(jnp.int32, (count, count), 0)
    col = lax.broadcasted_iota(jnp.int32, (count, count), 1)
    same = ids_col == ids_row
    lower = same & (row >= col)
    strict = same & (row > col)
    sums = (row >= col).astype(F32).astype(BF16)
    fresh = (ids_col == before).astype(F32)
    last_id = ids_col[count - 1 :, :]
    tail = (ids_col == last_id).astype(F32)
    kept = (last_id == before).astype(F32)
    cumul_all = dot(sums, g_ref[...])
    head_lane = lax.broadcasted_iota(jnp.int32, beta_ref.shape, 1)
    eye = (
        lax.broadcasted_iota(jnp.int32, (width, width), 0)
        == lax.broadcasted_iota(jnp.int32, (width, width), 1)
    )
    for h in range(TOGETHER):
        here = slice(h * width, (h + 1) * width)
        head = pl.program_id(0) * TOGETHER + h
        strength = jnp.sum(jnp.where(head_lane == head, beta_ref[...], 0.0), axis=1, keepdims=True)
        cumul = cumul_all[:, here]
        total = cumul[count - 1 :, :]
        middle = total * 0.5
        up = jnp.exp(cumul - middle)
        kn = unit_rows(k_ref[:, here].astype(F32))
        qn = unit_rows(q_ref[:, here].astype(F32))
        kneg = kn * jnp.exp(middle - cumul)
        kpos = kn * up * strength
        qpos = qn * up
        half = jnp.exp(middle)
        products = dot3(halves(jnp.concatenate([kpos, qpos], axis=0)), halves(kneg), ((1,), (1,)))
        system = jnp.where(strict, products[:count], 0.0)
        scores = jnp.where(lower, products[count:], 0.0)
        right = jnp.concatenate(
            [strength * v_ref[:, here].astype(F32), kpos * (half * fresh)], axis=1
        )
        updates = solve(system, right, count)
        khat = kneg * (half * tail)
        left = halves(jnp.concatenate([khat.T, scores], axis=0))
        found = dot3(left, updates)
        b_ref[h] = found[:width, :width]
        a_ref[h] = jnp.where(eye, jnp.exp(total) * kept, 0.0) - found[:width, width:]
        out_ref[:, here] = found[width:, :width]
        reach_ref[:, here] = qpos * (half * fresh) - found[width:, width:]


def span(lengths, queries, keys, values, beta, log_decay):
    count, total = queries.shape
    heads = beta.shape[1]
    width = total // heads
    cols = TOGETHER * width
    rows = pl.BlockSpec((count, cols), lambda i: (0, i))
    squares = pl.BlockSpec((TOGETHER, width, width), lambda i: (i, 0, 0))
    return pl.pallas_call(
        span_kernel,
        grid=(heads // TOGETHER,),
        in_specs=[
            pl.BlockSpec(memory_space=pltpu.SMEM),
            rows,
            rows,
            rows,
            pl.BlockSpec(beta.shape, lambda i: (0, 0)),
            rows,
        ],
        out_specs=[squares, squares, rows, rows],
        out_shape=[
            jax.ShapeDtypeStruct((heads, width, width), F32),
            jax.ShapeDtypeStruct((heads, width, width), F32),
            jax.ShapeDtypeStruct((count, total), F32),
            jax.ShapeDtypeStruct((count, total), F32),
        ],
        compiler_params=pltpu.CompilerParams(vmem_limit_bytes=48 << 20),
        name="span",
    )(lengths, queries, keys, values, beta, log_decay)


def pass_kernel(a_ref, b_ref, state_ref, out_ref):
    for h in range(a_ref.shape[0]):
        out_ref[h] = b_ref[h] + dot3(halves(a_ref[h]), halves(state_ref[h]))


def passed(trans_a, trans_b, state):
    heads, width, _ = trans_a.shape
    squares = pl.BlockSpec((4, width, width), lambda i: (i, 0, 0))
    return pl.pallas_call(
        pass_kernel,
        grid=(heads // 4,),
        in_specs=[squares] * 3,
        out_specs=squares,
        out_shape=jax.ShapeDtypeStruct(trans_a.shape, F32),
        name="pass_on",
    )(trans_a, trans_b, state)


def finish_kernel(out_ref, reach_ref, state_ref, gain_ref, mixed_ref):
    width = state_ref.shape[1]
    for h in range(state_ref.shape[0]):
        here = slice(h * width, (h + 1) * width)
        outs = out_ref[:, here] + dot3(halves(reach_ref[:, here]), halves(state_ref[h]))
        scale = lax.rsqrt(jnp.mean(outs * outs, axis=-1, keepdims=True) + 1e-06)
        mixed_ref[:, here] = (outs * scale * gain_ref[:, here]).astype(BF16)


def finished(outs, reach, state, gain):
    count, total = outs.shape
    heads, width, _ = state.shape
    rows = pl.BlockSpec((count, 4 * width), lambda i: (0, i))
    return pl.pallas_call(
        finish_kernel,
        grid=(heads // 4,),
        in_specs=[
            rows,
            rows,
            pl.BlockSpec((4, width, width), lambda i: (i, 0, 0)),
            pl.BlockSpec((1, 4 * width), lambda i: (0, i)),
        ],
        out_specs=rows,
        out_shape=jax.ShapeDtypeStruct((count, total), BF16),
        name="finish",
    )(outs, reach, state, gain)


def local(queries, keys, values, beta, log_decay, out_gain, doc_lengths):
    devices = lax.axis_size("ctx")
    pairs = [(i, i + 1) for i in range(devices - 1)]
    trans_a, trans_b, outs, reach = span(doc_lengths, queries, keys, values, beta, log_decay)
    state = lax.ppermute(trans_b, "ctx", pairs)
    for _ in range(devices // 2 - 1):
        state = lax.ppermute(passed(trans_a, trans_b, state), "ctx", pairs)
    return finished(outs, reach, state, out_gain.reshape(1, -1))


def solution(mesh):
    rows = P(("dp", "ctx"), None)
    return jax.shard_map(
        local,
        mesh=mesh,
        in_specs=(rows, rows, rows, rows, rows, P(), P("dp")),
        out_specs=rows,
        check_vma=False,
    )
```

time: 412 us -> 113 us (0.27)
  other arithmetic: 241 us -> 0 us
  matrix products: 71.9 us -> 0 us
  Pallas kernels: 0 us -> 49.6 us
  waiting for transfers between devices: 65.3 us -> 44.1 us
  local copies, waits for them, and re-layouts: 18.6 us -> 8.99 us
  starting transfers between devices: 13.7 us -> 9.42 us
    another operation x5 -> x0, other arithmetic: 238 us -> none  [the longest x3 237 us: lower_solve(): lax.linalg.triangular_solve(system, right_side, left_side=True, lower=Tru...]
    dot_general x21 -> x0, matrix products: 64.6 us -> none  [the longest x12 25.3 us: head_matmul(): return jnp.einsum('hij,hjk->hik', left, right, precision=HIGHEST_ACCURACY)]
    pallas_call x0 -> x3, Pallas kernels: none -> 49.6 us  [the longest x1 40.7 us: span(): pl.pallas_call(span_kernel, grid=(heads // TOGETHER,), in_specs=[pl.Block...]
    ppermute x3 -> x2, waiting for transfers between devices: 65.3 us -> 44.1 us  [the longest x1 22.3 us: local(): state = lax.ppermute(trans_b, 'ctx', pairs)]
    another operation x2 -> x0, matrix products: 7.25 us -> none  [lower_solve(): lax.linalg.triangular_solve(system, right_side, left_side=True, lower=Tru...]
    while x15 -> x0, local copies, waits for them, and re-layouts: 5.82 us -> none
    ppermute x3 -> x2, starting transfers between devices: 13.7 us -> 9.42 us  [the longest x1 4.98 us: local(): state = lax.ppermute(trans_b, 'ctx', pairs)]
    unnamed x30 -> x19, local copies, waits for them, and re-layouts: 6.83 us -> 8.99 us
  transfers between devices with their start and end apart: 3 -> 2, of which waited for: 3 -> 2; matrix products, arithmetic and copies ran while one was open for 0% -> 0% of each run, Pallas kernels for 0% -> 0%
where the time goes in v1:
time: 113 us; the launch traced here: 112 us
  Pallas kernels  49.6 us (44%)
  waiting for transfers between devices  44.1 us (39%)
  starting transfers between devices  9.42 us (8%)
  local copies, waits for them, and re-layouts  8.99 us (8%)
    pallas_call x1, Pallas kernels, span(): pl.pallas_call(span_kernel, grid=(heads // TOGETHER,), in_specs=[pl.Block...  40.7 us
    ppermute x1, waiting for transfers between devices, local(): state = lax.ppermute(trans_b, 'ctx', pairs)  22.3 us
    ppermute x1, waiting for transfers between devices, local(): state = lax.ppermute(passed(trans_a, trans_b, state), 'ctx', pairs)  21.8 us
    unnamed x19, local copies, waits for them, and re-layouts  8.99 us
    ppermute x1, starting transfers between devices, local(): state = lax.ppermute(trans_b, 'ctx', pairs)  4.98 us
    pallas_call x1, Pallas kernels, finished(): pl.pallas_call(finish_kernel, grid=(heads // 4,), in_specs=[rows, rows, p...  4.67 us
    ppermute x1, starting transfers between devices, local(): state = lax.ppermute(passed(trans_a, trans_b, state), 'ctx', pairs)  4.44 us
    pallas_call x1, Pallas kernels, passed(): pl.pallas_call(pass_kernel, grid=(heads // 4,), in_specs=[squares] * 3, o...  4.2 us
  transfers between devices with their start and end apart: 2, of which 2 were waited for; matrix products, arithmetic and copies ran while one was open for 0% of the time, Pallas kernels for 0%

profile of v1, /device:TPU:0, one launch (start us, length us, event | category | flops | bytes accessed | tf_op | source)
XLA Modules:
  0.0 112.1 jit_solution(17217270539595203450)
XLA Ops:
  0.0 0.8 copy.8.beta_ref
  0.8 0.0 copy-start.2
  0.8 1.1 %copy-done.2 = bf16[192,2048]{1,0:T(8,128)(2,1)S(1)} copy-done((bf16[192,2048]{1,0:T(8,128)(2,1)S(1)}, bf16[192,2048]{1,0:T(8,128)(2,1)}, u32[]{:S(2)}) %copy-start.2) | copy-done | bytes 786456
  2.0 0.0 copy-start.3
  2.0 1.1 %copy-done.3 = bf16[192,2048]{1,0:T(8,128)(2,1)S(1)} copy-done((bf16[192,2048]{1,0:T(8,128)(2,1)S(1)}, bf16[192,2048]{1,0:T(8,128)(2,1)}, u32[]{:S(2)}) %copy-start.3) | copy-done | bytes 786456
  3.1 0.0 copy-start.4
  3.1 1.1 %copy-done.4 = bf16[192,2048]{1,0:T(8,128)(2,1)S(1)} copy-done((bf16[192,2048]{1,0:T(8,128)(2,1)S(1)}, bf16[192,2048]{1,0:T(8,128)(2,1)}, u32[]{:S(2)}) %copy-start.4) | copy-done | bytes 786456
  4.2 0.0 copy-start.5
  4.2 1.1 %copy-done.5 = bf16[192,2048]{1,0:T(8,128)(2,1)S(1)} copy-done((bf16[192,2048]{1,0:T(8,128)(2,1)S(1)}, bf16[192,2048]{1,0:T(8,128)(2,1)}, u32[]{:S(2)}) %copy-start.5) | copy-done | bytes 786456
  5.4 0.0 copy-start.6
  5.4 0.7 copy-done.6
  6.0 40.7 %span.1 = (f32[16,128,128]{2,1,0:T(8,128)S(1)}, f32[16,128,128]{2,1,0:T(8,128)S(1)}, f32[192,2048]{1,0:T(8,128)}, f32[192,2048]{1,0:T(8,128)}) custom-call(s32[16]{0:T(128)S(1)} %copy-done.6, bf16[192,2048]{1,0:T(8,128)(2,1)S(1)} %copy-done.2, bf16[192,2048]{1,0:T(8,128)(2,1)S(1)} %copy-done.3, bf16[192,2048]{1,0:T(8,128)(2,1)S(1)} %copy-done.4, ...), custom_call_target="tpu_custom_call" | custom-call | tf_op jit(solution)/shard_map/span/pallas_call | solution.py:171
  46.7 0.0 copy-start
  46.7 1.0 copy-done
  47.7 0.0 copy-start.1
  47.7 5.0 %collective-permute-start = (f32[16,128,128]{2,1,0:T(8,128)S(1)}, f32[16,128,128]{2,1,0:T(8,128)S(1)}, u32[]{:S(2)}, u32[]{:S(2)}) collective-permute-start(f32[16,128,128]{2,1,0:T(8,128)S(1)} %get-tuple-element.12.b_ref), channel_id=1, source_target_pairs={{0,1},{1,2},{2,3},{4,5},{5,6},{6,7},{8,9},{9,10},{10,11},{12,13},{... | collective-permute-start | bytes 3145736 | tf_op jit(solution)/shard_map/ppermute | solution.py:244
  52.7 22.3 %collective-permute-done.state_ref = f32[16,128,128]{2,1,0:T(8,128)S(1)} collective-permute-done((f32[16,128,128]{2,1,0:T(8,128)S(1)}, f32[16,128,128]{2,1,0:T(8,128)S(1)}, u32[]{:S(2)}, u32[]{:S(2)}) %collective-permute-start) | collective-permute-done | bytes 1048608 | tf_op jit(solution)/shard_map/ppermute | solution.py:244
  75.0 0.0 copy-done.1
  75.0 1.0 copy-done.8
  76.0 4.2 %pass_on.1 = f32[16,128,128]{2,1,0:T(8,128)} custom-call(f32[16,128,128]{2,1,0:T(8,128)} %copy-done, f32[16,128,128]{2,1,0:T(8,128)} %copy-done.1, f32[16,128,128]{2,1,0:T(8,128)} %copy-done.8), custom_call_target="tpu_custom_call" | custom-call | tf_op jit(solution)/shard_map/pass_on/pallas_call | solution.py:202
  80.2 4.4 %collective-permute-start.1 = (f32[16,128,128]{2,1,0:T(8,128)}, f32[16,128,128]{2,1,0:T(8,128)S(1)}, u32[]{:S(2)}, u32[]{:S(2)}) collective-permute-start(f32[16,128,128]{2,1,0:T(8,128)} %pass_on.1), channel_id=1, source_target_pairs={{0,1},{1,2},{2,3},{4,5},{5,6},{6,7},{8,9},{9,10},{10,11},{12,13},{... | collective-permute-start | bytes 3145736 | tf_op jit(solution)/shard_map/ppermute | solution.py:246
  84.7 21.8 %collective-permute-done.1.state_ref = f32[16,128,128]{2,1,0:T(8,128)S(1)} collective-permute-done((f32[16,128,128]{2,1,0:T(8,128)}, f32[16,128,128]{2,1,0:T(8,128)S(1)}, u32[]{:S(2)}, u32[]{:S(2)}) %collective-permute-start.1) | collective-permute-done | bytes 1048608 | tf_op jit(solution)/shard_map/ppermute | solution.py:246
  106.5 1.0 copy-done.7
  107.5 4.7 %finish.1 = bf16[192,2048]{1,0:T(8,128)(2,1)} custom-call(f32[192,2048]{1,0:T(8,128)} %get-tuple-element.9.out_ref, f32[192,2048]{1,0:T(8,128)} %get-tuple-element.10.reach_ref, f32[16,128,128]{2,1,0:T(8,128)} %copy-done.7, f32[1,2048]{1,0:T(1,128)} %bitcast.1), custom_call_target="tpu_custom_call" | custom-call | tf_op jit(solution)/shard_map/finish/pallas_call | solution.py:225
  (2 shorter events, 0.0 us)
Async XLA Ops:
  0.8 1.1 %copy-start.2 = (bf16[192,2048]{1,0:T(8,128)(2,1)S(1)}, bf16[192,2048]{1,0:T(8,128)(2,1)}, u32[]{:S(2)}) copy-start(bf16[192,2048]{1,0:T(8,128)(2,1)} %q_ref.1) | copy-start | bytes 2359300
  2.0 1.1 %copy-start.3 = (bf16[192,2048]{1,0:T(8,128)(2,1)S(1)}, bf16[192,2048]{1,0:T(8,128)(2,1)}, u32[]{:S(2)}) copy-start(bf16[192,2048]{1,0:T(8,128)(2,1)} %k_ref.1) | copy-start | bytes 2359300
  3.1 1.1 %copy-start.4 = (bf16[192,2048]{1,0:T(8,128)(2,1)S(1)}, bf16[192,2048]{1,0:T(8,128)(2,1)}, u32[]{:S(2)}) copy-start(bf16[192,2048]{1,0:T(8,128)(2,1)} %v_ref.1) | copy-start | bytes 2359300
  4.2 1.1 %copy-start.5 = (bf16[192,2048]{1,0:T(8,128)(2,1)S(1)}, bf16[192,2048]{1,0:T(8,128)(2,1)}, u32[]{:S(2)}) copy-start(bf16[192,2048]{1,0:T(8,128)(2,1)} %g_ref.1) | copy-start | bytes 2359300
  5.4 0.7 copy-start.6
  46.7 1.0 copy-start
  47.7 27.3 %copy-start.1 = (f32[16,128,128]{2,1,0:T(8,128)}, f32[16,128,128]{2,1,0:T(8,128)S(1)}, u32[]{:S(2)}) copy-start(f32[16,128,128]{2,1,0:T(8,128)S(1)} %get-tuple-element.12.b_ref) | copy-start | bytes 3145732
  47.7 27.3 %collective-permute-start = (f32[16,128,128]{2,1,0:T(8,128)S(1)}, f32[16,128,128]{2,1,0:T(8,128)S(1)}, u32[]{:S(2)}, u32[]{:S(2)}) collective-permute-start(f32[16,128,128]{2,1,0:T(8,128)S(1)} %get-tuple-element.12.b_ref), channel_id=1, source_target_pairs={{0,1},{1,2},{2,3},{4,5},{5,6},{6,7},{8,9},{9,10},{10,11},{12,13},{... | collective-permute-start | bytes 3145736 | tf_op jit(solution)/shard_map/ppermute | solution.py:244
  75.0 1.0 copy-start.8
  80.2 26.2 %collective-permute-start.1 = (f32[16,128,128]{2,1,0:T(8,128)}, f32[16,128,128]{2,1,0:T(8,128)S(1)}, u32[]{:S(2)}, u32[]{:S(2)}) collective-permute-start(f32[16,128,128]{2,1,0:T(8,128)} %pass_on.1), channel_id=1, source_target_pairs={{0,1},{1,2},{2,3},{4,5},{5,6},{6,7},{8,9},{9,10},{10,11},{12,13},{... | collective-permute-start | bytes 3145736 | tf_op jit(solution)/shard_map/ppermute | solution.py:246
  106.5 1.0 copy-start.7

commit v2 on v0

v2 whole, which is shorter than its diff:
```python
import functools

import jax
import jax.numpy as jnp
from jax import lax
from jax.experimental import pallas as pl
from jax.experimental.pallas import tpu as pltpu
from jax.sharding import PartitionSpec as P

F32 = jnp.float32
BF16 = jnp.bfloat16
TILE = 16
BLOCK = 64
GROUP = 4
LAG = 2


def halves(x):
    high = x.astype(BF16)
    return high, (x - high.astype(F32)).astype(BF16)


def dot(a, b, dims=((1,), (0,))):
    return lax.dot_general(a, b, (dims, ((), ())), preferred_element_type=F32)


def dot3(a, b, dims=((1,), (0,))):
    return dot(a[0], b[0], dims) + (dot(a[0], b[1], dims) + dot(a[1], b[0], dims))


def rows_of(pair, low, high):
    return pair[0][low:high], pair[1][low:high]


def unit_rows(x):
    return x * lax.rsqrt(jnp.sum(x * x, axis=-1, keepdims=True) + 1e-06)


def doc_ids(lengths_ref, first, shape, dim):
    place = first + lax.broadcasted_iota(jnp.int32, shape, dim)
    ids = jnp.zeros(shape, jnp.int32)
    before = jnp.int32(0)
    start = jnp.int32(0)
    for d in range(lengths_ref.shape[0]):
        ids = ids + (place >= start).astype(jnp.int32)
        before = before + (first > start).astype(jnp.int32)
        start = start + lengths_ref[d]
    return ids, before


def lanes_of(shape):
    return lax.broadcasted_iota(jnp.int32, shape, 1)


def side_by_side(system, count, size):
    lane = lanes_of((size, count)) // size
    side = system[:size]
    for b in range(1, count // size):
        side = jnp.where(lane == b, system[b * size : (b + 1) * size], side)
    return side


def tile_inverses(systems, count):
    sides = [side_by_side(s, count, TILE) for s in systems]
    whole = count // 128 * 128
    pieces = [s[:, low : low + 128] for s in sides for low in range(0, whole, 128)]
    rest = [s[:, whole:] for s in sides]
    if count > whole:
        for i in range(0, len(rest), 128 // (count - whole)):
            group = rest[i : i + 128 // (count - whole)]
            wide = sum(x.shape[1] for x in group)
            if wide < 128:
                group = group + [jnp.zeros((TILE, 128 - wide), F32)]
            pieces.append(jnp.concatenate(group, axis=1))
    lane = lanes_of((TILE, 128))
    home = lane - lane % TILE
    eye = (lane % TILE == lax.broadcasted_iota(jnp.int32, (TILE, 128), 0)).astype(F32)
    found = [[eye[8 * i : 8 * i + 8] for i in range(TILE // 8)] for _ in pieces]
    for j in range(TILE - 1):
        for p, piece in enumerate(pieces):
            line = found[p][j // 8][j % 8 : j % 8 + 1, :]
            for i in range((j + 1) // 8, TILE // 8):
                column = jnp.take_along_axis(
                    piece[8 * i : 8 * i + 8], home[:8] + j, axis=1, mode="promise_in_bounds"
                )
                found[p][i] = found[p][i] - column * line
    found = [jnp.concatenate(x, axis=0) for x in found]
    each = whole // 128
    results = []
    for h in range(len(systems)):
        parts = found[h * each : (h + 1) * each]
        if count > whole:
            per = 128 // (count - whole)
            at = h % per * (count - whole)
            parts = parts + [found[each * len(systems) + h // per][:, at : at + count - whole]]
        results.append(jnp.concatenate(parts, axis=1))
    return results


def spread(side, count, height, column_of):
    block = column_of(lanes_of(side.shape) // height)
    return jnp.concatenate([jnp.where(block == b, side, 0.0) for b in range(count // height)], axis=0)


def merged(system, side, count, size):
    lane = lanes_of(side.shape) // size
    even = lane % 2 == 0
    below = jnp.zeros(side.shape, F32)
    for b in range(1, count // size, 2):
        below = jnp.where(lane == b - 1, system[b * size : (b + 1) * size, :], below)
    wide = spread(side, count, size, lambda x: x)
    middle = dot3(halves(below), halves(wide))
    tall = spread(middle, count, size, lambda x: jnp.where(x % 2 == 0, x + 1, -1))
    corner = dot3(halves(jnp.where(even, 0.0, side)), halves(tall))
    return jnp.concatenate([jnp.where(even, side, 0.0), jnp.where(even, -corner, side)], axis=0)


def solve(systems, rights, count):
    sides = tile_inverses(systems, count)
    size = TILE
    while size < BLOCK:
        sides = [merged(s, x, count, size) for s, x in zip(systems, sides)]
        size = 2 * size
    wides = [halves(spread(x, count, BLOCK, lambda x: x)) for x in sides]
    row = lax.broadcasted_iota(jnp.int32, (count, count), 0) // BLOCK
    outside = row > lanes_of((count, count)) // BLOCK
    splits = [halves(jnp.where(outside, s, 0.0)) for s in systems]
    firsts = [dot3(w, r) for w, r in zip(wides, rights)]
    links = [halves(dot3(rows_of(w, BLOCK, count), s)) for w, s in zip(wides, splits)]
    done = [halves(x[:BLOCK]) for x in firsts]
    for b in range(1, count // BLOCK):
        low, high = b * BLOCK, (b + 1) * BLOCK
        for h in range(len(systems)):
            link = tuple(x[low - BLOCK : low, :low] for x in links[h])
            part = halves(firsts[h][low:high] - dot3(link, done[h]))
            done[h] = tuple(jnp.concatenate(x, axis=0) for x in zip(done[h], part))
    return done


def span_kernel(
    group, lengths_ref, q_ref, k_ref, v_ref, beta_ref, g_ref, a_ref, b_ref, out_ref, reach_ref
):
    count = q_ref.shape[0]
    width = a_ref.shape[1]
    first = lax.axis_index("ctx") * count
    ids_col, before = doc_ids(lengths_ref, first, (count, 1), 0)
    ids_row, _ = doc_ids(lengths_ref, first, (1, count), 1)
    row = lax.broadcasted_iota(jnp.int32, (count, count), 0)
    col = lanes_of((count, count))
    same = ids_col == ids_row
    lower = same & (row >= col)
    strict = same & (row > col)
    sums = (row >= col).astype(F32).astype(BF16)
    fresh = ids_col == before
    tail = (ids_row == ids_row[:, count - 1 :]).astype(F32)
    kept = (ids_row[:, count - 1 :] == before).astype(F32)
    cumul_all = dot(sums, g_ref[...])
    eye = lax.broadcasted_iota(jnp.int32, (width, width), 0) == lanes_of((width, width))
    heads = range(a_ref.shape[0])
    here = [slice(h * width, (h + 1) * width) for h in heads]
    strength = [beta_ref[group * len(heads) + h :][:1] for h in heads]
    total, half, kneg, kpos, qpos = [], [], [], [], []
    for h in heads:
        cumul = cumul_all[:, here[h]]
        total.append(cumul[count - 1 :, :])
        middle = total[h] * 0.5
        half.append(jnp.exp(middle))
        up = jnp.exp(cumul - middle)
        kn = unit_rows(k_ref[:, here[h]].astype(F32))
        kneg.append(kn * jnp.exp(middle - cumul))
        kpos.append(kn * up)
        qpos.append(unit_rows(q_ref[:, here[h]].astype(F32)) * up)
    products = [
        dot3(halves(jnp.concatenate([kpos[h], qpos[h]], axis=0)), halves(kneg[h]), ((1,), (1,)))
        * strength[h]
        for h in heads
    ]
    systems = [jnp.where(strict, x[:count], 0.0) for x in products]
    rights = []
    for h in heads:
        high, low = halves(kpos[h] * half[h])
        value = v_ref[:, here[h]]
        rights.append(
            (
                jnp.concatenate([value, high], axis=1),
                jnp.concatenate([jnp.zeros_like(value), low], axis=1),
            )
        )
    updates = solve(systems, rights, count)
    for h in heads:
        scores = jnp.where(lower, products[h][count:], 0.0)
        khat = (kneg[h] * half[h]).T * (strength[h] * tail)
        found = dot3(halves(jnp.concatenate([khat, scores], axis=0)), updates[h])
        b_ref[h] = found[:width, :width]
        a_ref[h] = (jnp.where(eye, jnp.exp(total[h]), 0.0) - found[:width, width:]) * kept
        out_ref[:, here[h]] = found[width:, :width]
        reach_ref[:, here[h]] = jnp.where(fresh, qpos[h] * half[h] - found[width:, width:], 0.0)


VMEM = pl.BlockSpec(memory_space=pltpu.VMEM)
SMEM = pl.BlockSpec(memory_space=pltpu.SMEM)


def span(group, lengths, queries, keys, values, strength, log_decay):
    count, total = queries.shape
    heads = strength.shape[0]
    width = total // heads
    cols = GROUP * width
    rows = pl.BlockSpec((count, cols), lambda i: (0, group))
    square = jax.ShapeDtypeStruct((GROUP, width, width), F32)
    part = jax.ShapeDtypeStruct((count, cols), F32)
    return pl.pallas_call(
        functools.partial(span_kernel, group),
        grid=(1,),
        in_specs=[SMEM, rows, rows, rows, VMEM, rows],
        out_specs=[VMEM] * 4,
        out_shape=[square, square, part, part],
        compiler_params=pltpu.CompilerParams(vmem_limit_bytes=32 << 20),
        name="span",
    )(lengths, queries, keys, values, strength, log_decay)


def spans_back(lengths_ref, count, most):
    first = lax.axis_index("ctx") * count
    start = jnp.int32(0)
    latest = jnp.int32(0)
    fresh = jnp.int32(0)
    for d in range(lengths_ref.shape[0]):
        latest = jnp.where(start < first, start, latest)
        fresh = jnp.where((start >= first) & (start < first + count), 1, fresh)
        start = start + lengths_ref[d]
    back = jnp.int32(0)
    for i in range(1, most):
        back = back + jnp.where(latest < first - i * count, 1, 0)
    return back, fresh


def pass_kernel(count, most, own, low, late, lengths_ref, state_ref, *refs):
    out_ref = refs[-1]
    before, fresh = spans_back(lengths_ref, count, most)
    for h in range(out_ref.shape[0]):
        trans_a, trans_b = refs[own][h], refs[own + 1][h]
        for i in range(1, late):
            here = before == low + i
            trans_a = jnp.where(here, refs[own + 2 * i][h], trans_a)
            trans_b = jnp.where(here, refs[own + 2 * i + 1][h], trans_b)
        sent = trans_b + dot3(halves(trans_a), halves(state_ref[h]))
        out_ref[h] = jnp.where(fresh == 1, refs[0][h], sent) if own else sent


def message(step, count, most, lengths, trans_a, trans_b, received):
    own = [trans_b[step]] if step < len(trans_b) else []
    if step < LAG:
        return own[0]
    late = [step - LAG * i for i in range(1, most)]
    low = next(i for i, x in enumerate(late) if x < len(trans_b))
    late = [x for x in late if 0 <= x < len(trans_b)]
    carried = [x for g in late for x in (trans_a[g], trans_b[g])]
    return pl.pallas_call(
        functools.partial(pass_kernel, count, most, len(own), low, len(late)),
        in_specs=[SMEM] + [VMEM] * (1 + len(own) + len(carried)),
        out_specs=VMEM,
        out_shape=jax.ShapeDtypeStruct(trans_b[0].shape, F32),
        compiler_params=pltpu.CompilerParams(vmem_limit_bytes=8 << 20),
        name="pass_on",
    )(lengths, received[step - LAG], *own, *carried)


def finish_kernel(lengths_ref, out_ref, reach_ref, gain_ref, *refs):
    states = refs[:-2]
    mixed_ref = refs[-1]
    heads, width, _ = states[0].shape
    before, _ = spans_back(lengths_ref, out_ref.shape[0], len(states))
    for h in range(heads):
        here = slice(h * width, (h + 1) * width)
        state = states[0][h]
        for i in range(1, len(states)):
            state = jnp.where(before == i, states[i][h], state)
        outs = out_ref[:, here] + dot3(halves(reach_ref[:, here]), halves(state))
        scale = lax.rsqrt(jnp.mean(outs * outs, axis=-1, keepdims=True) + 1e-06)
        mixed_ref[:, here] = (outs * scale * gain_ref[:, here]).astype(BF16)


def finished(group, mixed, lengths, outs, reach, states, gain):
    count, cols = outs.shape
    return pl.pallas_call(
        finish_kernel,
        grid=(1,),
        in_specs=[SMEM, VMEM, VMEM, pl.BlockSpec((1, cols), lambda i: (0, group))]
        + [VMEM] * len(states)
        + [pl.BlockSpec(memory_space=pl.ANY)],
        out_specs=pl.BlockSpec((count, cols), lambda i: (0, group)),
        out_shape=jax.ShapeDtypeStruct(mixed.shape, BF16),
        input_output_aliases={4 + len(states): 0},
        compiler_params=pltpu.CompilerParams(vmem_limit_bytes=8 << 20),
        name="finish",
    )(lengths, outs, reach, gain, *states, mixed)


def local(queries, keys, values, beta, log_decay, out_gain, doc_lengths):
    devices = lax.axis_size("ctx")
    pairs = [(i, i + 1) for i in range(devices - 1)]
    count = queries.shape[0]
    groups = beta.shape[1] // GROUP
    most = devices // 2
    queries, keys, values, log_decay = (
        pltpu.with_memory_space_constraint(x, pltpu.HBM)
        for x in (queries, keys, values, log_decay)
    )
    strength = beta.T
    trans_a, trans_b, outs, reach = zip(
        *(
            span(g, doc_lengths, queries, keys, values, strength, log_decay)
            for g in range(groups)
        )
    )
    received = []
    for step in range(groups + LAG * (most - 1)):
        sent = message(step, count, most, doc_lengths, trans_a, trans_b, received)
        received.append(lax.ppermute(sent, "ctx", pairs))
    mixed = jnp.zeros(queries.shape, BF16)
    gain = out_gain.reshape(1, -1)
    for g in range(groups):
        states = [received[g + LAG * i] for i in range(most)]
        mixed = finished(g, mixed, doc_lengths, outs[g], reach[g], states, gain)
    return mixed


def solution(mesh):
    rows = P(("dp", "ctx"), None)
    return jax.shard_map(
        local,
        mesh=mesh,
        in_specs=(rows, rows, rows, rows, rows, P(), P("dp")),
        out_specs=rows,
        check_vma=False,
    )
```

time: 412 us -> 59.7 us (0.14)
  other arithmetic: 241 us -> 0 us
  matrix products: 71.9 us -> 0 us
  waiting for transfers between devices: 65.3 us -> 4.37 us
  Pallas kernels: 0 us -> 29.7 us
  local copies, waits for them, and re-layouts: 18.6 us -> 2.34 us
  starting transfers between devices: 13.7 us -> 22.8 us
    another operation x5 -> x0, other arithmetic: 238 us -> none  [the longest x3 237 us: lower_solve(): lax.linalg.triangular_solve(system, right_side, left_side=True, lower=Tru...]
    dot_general x21 -> x0, matrix products: 64.6 us -> none  [the longest x12 25.3 us: head_matmul(): return jnp.einsum('hij,hjk->hik', left, right, precision=HIGHEST_ACCURACY)]
    ppermute x3 -> x6, waiting for transfers between devices: 65.3 us -> 4.37 us  [local(): received.append(lax.ppermute(sent, 'ctx', pairs))]
    pallas_call x0 -> x12, Pallas kernels: none -> 29.7 us  [the longest x4 19.7 us: span(): pl.pallas_call(functools.partial(span_kernel, group), grid=(1,), in_specs...]
    ppermute x3 -> x6, starting transfers between devices: 13.7 us -> 22.8 us  [local(): received.append(lax.ppermute(sent, 'ctx', pairs))]
    another operation x2 -> x0, matrix products: 7.25 us -> none  [lower_solve(): lax.linalg.triangular_solve(system, right_side, left_side=True, lower=Tru...]
    while x15 -> x0, local copies, waits for them, and re-layouts: 5.82 us -> none
    unnamed x30 -> x6, local copies, waits for them, and re-layouts: 6.83 us -> 1.38 us
  transfers between devices with their start and end apart: 3 -> 6, of which waited for: 3 -> 2; matrix products, arithmetic and copies ran while one was open for 0% -> 2% of each run, Pallas kernels for 0% -> 39%
where the time goes in v2:
time: 59.7 us; the launch traced here: 59.4 us
  Pallas kernels  29.7 us (50%)
  starting transfers between devices  22.8 us (38%)
  waiting for transfers between devices  4.37 us (7%)
  local copies, waits for them, and re-layouts  2.34 us (4%)
    ppermute x6, starting transfers between devices, local(): received.append(lax.ppermute(sent, 'ctx', pairs))  22.8 us
    pallas_call x4, Pallas kernels, span(): pl.pallas_call(functools.partial(span_kernel, group), grid=(1,), in_specs...  19.7 us
    pallas_call x4, Pallas kernels, finished(): pl.pallas_call(finish_kernel, grid=(1,), in_specs=[SMEM, VMEM, VMEM, pl.B...  6.73 us
    ppermute x6, waiting for transfers between devices, local(): received.append(lax.ppermute(sent, 'ctx', pairs))  4.37 us
    pallas_call x4, Pallas kernels, message(): pl.pallas_call(functools.partial(pass_kernel, count, most, len(own), low,...  3.23 us
    unnamed x6, local copies, waits for them, and re-layouts  1.38 us
  transfers between devices with their start and end apart: 6, of which 2 were waited for; matrix products, arithmetic and copies ran while one was open for 2% of the time, Pallas kernels for 39%

profile of v2, /device:TPU:0, one launch (start us, length us, event | category | flops | bytes accessed | tf_op | source)
XLA Modules:
  0.0 59.4 jit_solution(8529980031556264556)
XLA Ops:
  0.0 0.7 %copy-done.2 = s32[16]{0:T(128)S(1)} copy-done((s32[16]{0:T(128)S(1)}, s32[16]{0:T(128)}, u32[]{:S(2)}) %copy-start.2) | copy-done | bytes 88
  0.7 0.7 %copy-done = f32[192,16]{0,1:T(8,128)S(1)} copy-done((f32[192,16]{0,1:T(8,128)S(1)}, f32[192,16]{0,1:T(8,128)}, u32[]{:S(2)}) %copy-start) | copy-done | bytes 12312
  1.4 4.9 %span.7 = (f32[4,128,128]{2,1,0:T(8,128)S(1)}, f32[4,128,128]{2,1,0:T(8,128)S(1)}, f32[192,512]{1,0:T(8,128)S(1)}, f32[192,512]{1,0:T(8,128)S(1)}) custom-call(s32[16]{0:T(128)S(1)} %copy-done.2, bf16[192,2048]{1,0:T(8,128)(2,1)} %q_ref.7, bf16[192,2048]{1,0:T(8,128)(2,1)} %k_ref.7, bf16[192,2048]{1,0:T(8,128)(2,1)} %v_ref.7, f32[16,192]{1,0:T(8,128)S(1)} %bitcast.2, ...), custom_call_target="tpu_custom_call" | custom-call | tf_op jit(solution)/shard_map/span/pallas_call | solution.py:212
  6.3 4.9 %collective-permute-start.3 = (f32[4,128,128]{2,1,0:T(8,128)S(1)}, f32[4,128,128]{2,1,0:T(8,128)S(1)}, u32[]{:S(2)}, u32[]{:S(2)}) collective-permute-start(f32[4,128,128]{2,1,0:T(8,128)S(1)} %get-tuple-element.29.refs_2_), channel_id=1, source_target_pairs={{0,1},{1,2},{2,3},{4,5},{5,6},{6,7},{8,9},{9,10},{10,11},{12,13},{... | collective-permute-start | bytes 786440 | tf_op jit(solution)/shard_map/ppermute | solution.py:320
  11.3 4.9 %span.5 = (f32[4,128,128]{2,1,0:T(8,128)S(1)}, f32[4,128,128]{2,1,0:T(8,128)S(1)}, f32[192,512]{1,0:T(8,128)S(1)}, f32[192,512]{1,0:T(8,128)S(1)}) custom-call(s32[16]{0:T(128)S(1)} %copy-done.2, bf16[192,2048]{1,0:T(8,128)(2,1)} %q_ref.7, bf16[192,2048]{1,0:T(8,128)(2,1)} %k_ref.7, bf16[192,2048]{1,0:T(8,128)(2,1)} %v_ref.7, f32[16,192]{1,0:T(8,128)S(1)} %bitcast.3, ...), custom_call_target="tpu_custom_call" | custom-call | tf_op jit(solution)/shard_map/span/pallas_call | solution.py:212
  16.2 3.7 %collective-permute-start = (f32[4,128,128]{2,1,0:T(8,128)S(1)}, f32[4,128,128]{2,1,0:T(8,128)S(1)}, u32[]{:S(2)}, u32[]{:S(2)}) collective-permute-start(f32[4,128,128]{2,1,0:T(8,128)S(1)} %get-tuple-element.23.refs_2_), channel_id=1, source_target_pairs={{0,1},{1,2},{2,3},{4,5},{5,6},{6,7},{8,9},{9,10},{10,11},{12,13},{... | collective-permute-start | bytes 786440 | tf_op jit(solution)/shard_map/ppermute | solution.py:320
  19.9 4.9 %span.6 = (f32[4,128,128]{2,1,0:T(8,128)S(1)}, f32[4,128,128]{2,1,0:T(8,128)S(1)}, f32[192,512]{1,0:T(8,128)S(1)}, f32[192,512]{1,0:T(8,128)S(1)}) custom-call(s32[16]{0:T(128)S(1)} %copy-done.2, bf16[192,2048]{1,0:T(8,128)(2,1)} %q_ref.7, bf16[192,2048]{1,0:T(8,128)(2,1)} %k_ref.7, bf16[192,2048]{1,0:T(8,128)(2,1)} %v_ref.7, f32[16,192]{1,0:T(8,128)S(1)} %bitcast.4, ...), custom_call_target="tpu_custom_call" | custom-call | tf_op jit(solution)/shard_map/span/pallas_call | solution.py:212
  24.8 4.9 %span.4 = (f32[4,128,128]{2,1,0:T(8,128)S(1)}, f32[4,128,128]{2,1,0:T(8,128)S(1)}, f32[192,512]{1,0:T(8,128)S(1)}, f32[192,512]{1,0:T(8,128)S(1)}) custom-call(s32[16]{0:T(128)S(1)} %copy-done.2, bf16[192,2048]{1,0:T(8,128)(2,1)} %q_ref.7, bf16[192,2048]{1,0:T(8,128)(2,1)} %k_ref.7, bf16[192,2048]{1,0:T(8,128)(2,1)} %v_ref.7, f32[16,192]{1,0:T(8,128)S(1)} %bitcast.5, ...), custom_call_target="tpu_custom_call" | custom-call | tf_op jit(solution)/shard_map/span/pallas_call | solution.py:212
  29.8 0.8 %pass_on.6 = f32[4,128,128]{2,1,0:T(8,128)S(1)} custom-call(s32[16]{0:T(128)S(1)} %copy-done.2, f32[4,128,128]{2,1,0:T(8,128)S(1)} %collective-permute-done.3.state_ref.refs_0_, f32[4,128,128]{2,1,0:T(8,128)S(1)} %get-tuple-element.30.refs_0_.refs_1_, f32[4,128,128]{2,1,0:T(8,128)S(1)} %get-tuple-element.31.refs_1_, f32[4,128,128]{2,1,0:T(8,128)S(1)} %get-tuple-element.29.refs_2_), custom_call_target="tpu_custom_call" | custom-call | tf_op jit(solution)/shard_map/pass_on/pallas_call | solution.py:259
  30.6 3.5 %collective-permute-start.4 = (f32[4,128,128]{2,1,0:T(8,128)S(1)}, f32[4,128,128]{2,1,0:T(8,128)S(1)}, u32[]{:S(2)}, u32[]{:S(2)}) collective-permute-start(f32[4,128,128]{2,1,0:T(8,128)S(1)} %pass_on.6), channel_id=1, source_target_pairs={{0,1},{1,2},{2,3},{4,5},{5,6},{6,7},{8,9},{9,10},{10,11},{12,13},{... | collective-permute-start | bytes 786440 | tf_op jit(solution)/shard_map/ppermute | solution.py:320
  34.1 0.8 %pass_on.4 = f32[4,128,128]{2,1,0:T(8,128)S(1)} custom-call(s32[16]{0:T(128)S(1)} %copy-done.2, f32[4,128,128]{2,1,0:T(8,128)S(1)} %collective-permute-done.state_ref.refs_0_, f32[4,128,128]{2,1,0:T(8,128)S(1)} %get-tuple-element.24.refs_0_.refs_1_, f32[4,128,128]{2,1,0:T(8,128)S(1)} %get-tuple-element.25.refs_1_, f32[4,128,128]{2,1,0:T(8,128)S(1)} %get-tuple-element.23.refs_2_), custom_call_target="tpu_custom_call" | custom-call | tf_op jit(solution)/shard_map/pass_on/pallas_call | solution.py:259
  34.9 1.9 %collective-permute-start.1 = (f32[4,128,128]{2,1,0:T(8,128)S(1)}, f32[4,128,128]{2,1,0:T(8,128)S(1)}, u32[]{:S(2)}, u32[]{:S(2)}) collective-permute-start(f32[4,128,128]{2,1,0:T(8,128)S(1)} %pass_on.4), channel_id=1, source_target_pairs={{0,1},{1,2},{2,3},{4,5},{5,6},{6,7},{8,9},{9,10},{10,11},{12,13},{... | collective-permute-start | bytes 786440 | tf_op jit(solution)/shard_map/ppermute | solution.py:320
  36.8 4.0 %collective-permute-done.4.state_ref.refs_1_.refs_0_ = f32[4,128,128]{2,1,0:T(8,128)S(1)} collective-permute-done((f32[4,128,128]{2,1,0:T(8,128)S(1)}, f32[4,128,128]{2,1,0:T(8,128)S(1)}, u32[]{:S(2)}, u32[]{:S(2)}) %collective-permute-start.4) | collective-permute-done | bytes 262176 | tf_op jit(solution)/shard_map/ppermute | solution.py:320
  40.8 0.8 %pass_on.7 = f32[4,128,128]{2,1,0:T(8,128)S(1)} custom-call(s32[16]{0:T(128)S(1)} %copy-done.2, f32[4,128,128]{2,1,0:T(8,128)S(1)} %collective-permute-done.4.state_ref.refs_1_.refs_0_, f32[4,128,128]{2,1,0:T(8,128)S(1)} %get-tuple-element.32.refs_0_, f32[4,128,128]{2,1,0:T(8,128)S(1)} %get-tuple-element.30.refs_0_.refs_1_), custom_call_target="tpu_custom_call" | custom-call | tf_op jit(solution)/shard_map/pass_on/pallas_call | solution.py:259
  41.6 4.4 %collective-permute-start.5 = (f32[4,128,128]{2,1,0:T(8,128)S(1)}, f32[4,128,128]{2,1,0:T(8,128)S(1)}, u32[]{:S(2)}, u32[]{:S(2)}) collective-permute-start(f32[4,128,128]{2,1,0:T(8,128)S(1)} %pass_on.7), channel_id=1, source_target_pairs={{0,1},{1,2},{2,3},{4,5},{5,6},{6,7},{8,9},{9,10},{10,11},{12,13},{... | collective-permute-start | bytes 786440 | tf_op jit(solution)/shard_map/ppermute | solution.py:320
  46.0 0.4 collective-permute-done.1.state_ref.refs_1_.refs_0_
  46.4 0.8 %pass_on.5 = f32[4,128,128]{2,1,0:T(8,128)S(1)} custom-call(s32[16]{0:T(128)S(1)} %copy-done.2, f32[4,128,128]{2,1,0:T(8,128)S(1)} %collective-permute-done.1.state_ref.refs_1_.refs_0_, f32[4,128,128]{2,1,0:T(8,128)S(1)} %get-tuple-element.26.refs_0_, f32[4,128,128]{2,1,0:T(8,128)S(1)} %get-tuple-element.24.refs_0_.refs_1_), custom_call_target="tpu_custom_call" | custom-call | tf_op jit(solution)/shard_map/pass_on/pallas_call | solution.py:259
  47.2 4.4 %collective-permute-start.2 = (f32[4,128,128]{2,1,0:T(8,128)S(1)}, f32[4,128,128]{2,1,0:T(8,128)S(1)}, u32[]{:S(2)}, u32[]{:S(2)}) collective-permute-start(f32[4,128,128]{2,1,0:T(8,128)S(1)} %pass_on.5), channel_id=1, source_target_pairs={{0,1},{1,2},{2,3},{4,5},{5,6},{6,7},{8,9},{9,10},{10,11},{12,13},{... | collective-permute-start | bytes 786440 | tf_op jit(solution)/shard_map/ppermute | solution.py:320
  51.6 0.0 copy-start.1
  51.6 1.0 %broadcast_in_dim.3.refs_2_ = bf16[192,2048]{1,0:T(8,128)(2,1)} broadcast(bf16[]{:T(256)} %constant.0.clone.1), dimensions={} | broadcast | bytes 786434 | tf_op jit(solution)/shard_map/broadcast_in_dim | solution.py:321
  52.6 1.7 %finish.4.refs_2_ = bf16[192,2048]{1,0:T(8,128)(2,1)} custom-call(s32[16]{0:T(128)S(1)} %copy-done.2, f32[192,512]{1,0:T(8,128)S(1)} %get-tuple-element.35.out_ref, f32[192,512]{1,0:T(8,128)S(1)} %get-tuple-element.36.reach_ref, f32[1,2048]{1,0:T(1,128)S(1)} %bitcast.6, ...), custom_call_target="tpu_custom_call", output_to_operand_aliasing={{}: (6, {})} | custom-call | tf_op jit(solution)/shard_map/finish/pallas_call | solution.py:286
  54.3 1.7 %finish.5.refs_2_ = bf16[192,2048]{1,0:T(8,128)(2,1)} custom-call(s32[16]{0:T(128)S(1)} %copy-done.2, f32[192,512]{1,0:T(8,128)S(1)} %get-tuple-element.33.out_ref, f32[192,512]{1,0:T(8,128)S(1)} %get-tuple-element.34.reach_ref, f32[1,2048]{1,0:T(1,128)S(1)} %bitcast.7, ...), custom_call_target="tpu_custom_call", output_to_operand_aliasing={{}: (6, {})} | custom-call | tf_op jit(solution)/shard_map/finish/pallas_call | solution.py:286
  56.0 1.7 %finish.6.refs_2_ = bf16[192,2048]{1,0:T(8,128)(2,1)} custom-call(s32[16]{0:T(128)S(1)} %copy-done.2, f32[192,512]{1,0:T(8,128)S(1)} %get-tuple-element.27.out_ref, f32[192,512]{1,0:T(8,128)S(1)} %get-tuple-element.28.reach_ref, f32[1,2048]{1,0:T(1,128)S(1)} %bitcast.8, ...), custom_call_target="tpu_custom_call", output_to_operand_aliasing={{}: (6, {})} | custom-call | tf_op jit(solution)/shard_map/finish/pallas_call | solution.py:286
  57.7 1.7 %finish.7 = bf16[192,2048]{1,0:T(8,128)(2,1)} custom-call(s32[16]{0:T(128)S(1)} %copy-done.2, f32[192,512]{1,0:T(8,128)S(1)} %get-tuple-element.21.out_ref, f32[192,512]{1,0:T(8,128)S(1)} %get-tuple-element.22.reach_ref, f32[1,2048]{1,0:T(1,128)S(1)} %bitcast.9, ...), custom_call_target="tpu_custom_call", output_to_operand_aliasing={{}: (6, {})} | custom-call | tf_op jit(solution)/shard_map/finish/pallas_call | solution.py:286
  (7 shorter events, 0.0 us)
Async XLA Ops:
  0.0 0.7 %copy-start.2 = (s32[16]{0:T(128)S(1)}, s32[16]{0:T(128)}, u32[]{:S(2)}) copy-start(s32[16]{0:T(128)} %lengths_ref.23) | copy-start | bytes 196
  0.7 0.7 %copy-start = (f32[192,16]{0,1:T(8,128)S(1)}, f32[192,16]{0,1:T(8,128)}, u32[]{:S(2)}) copy-start(f32[192,16]{0,1:T(8,128)} %param.10) | copy-start | bytes 36868
  6.3 23.4 %collective-permute-start.3 = (f32[4,128,128]{2,1,0:T(8,128)S(1)}, f32[4,128,128]{2,1,0:T(8,128)S(1)}, u32[]{:S(2)}, u32[]{:S(2)}) collective-permute-start(f32[4,128,128]{2,1,0:T(8,128)S(1)} %get-tuple-element.29.refs_2_), channel_id=1, source_target_pairs={{0,1},{1,2},{2,3},{4,5},{5,6},{6,7},{8,9},{9,10},{10,11},{12,13},{... | collective-permute-start | bytes 786440 | tf_op jit(solution)/shard_map/ppermute | solution.py:320
  16.2 17.9 %collective-permute-start = (f32[4,128,128]{2,1,0:T(8,128)S(1)}, f32[4,128,128]{2,1,0:T(8,128)S(1)}, u32[]{:S(2)}, u32[]{:S(2)}) collective-permute-start(f32[4,128,128]{2,1,0:T(8,128)S(1)} %get-tuple-element.23.refs_2_), channel_id=1, source_target_pairs={{0,1},{1,2},{2,3},{4,5},{5,6},{6,7},{8,9},{9,10},{10,11},{12,13},{... | collective-permute-start | bytes 786440 | tf_op jit(solution)/shard_map/ppermute | solution.py:320
  30.6 10.2 %collective-permute-start.4 = (f32[4,128,128]{2,1,0:T(8,128)S(1)}, f32[4,128,128]{2,1,0:T(8,128)S(1)}, u32[]{:S(2)}, u32[]{:S(2)}) collective-permute-start(f32[4,128,128]{2,1,0:T(8,128)S(1)} %pass_on.6), channel_id=1, source_target_pairs={{0,1},{1,2},{2,3},{4,5},{5,6},{6,7},{8,9},{9,10},{10,11},{12,13},{... | collective-permute-start | bytes 786440 | tf_op jit(solution)/shard_map/ppermute | solution.py:320
  34.9 11.5 %collective-permute-start.1 = (f32[4,128,128]{2,1,0:T(8,128)S(1)}, f32[4,128,128]{2,1,0:T(8,128)S(1)}, u32[]{:S(2)}, u32[]{:S(2)}) collective-permute-start(f32[4,128,128]{2,1,0:T(8,128)S(1)} %pass_on.4), channel_id=1, source_target_pairs={{0,1},{1,2},{2,3},{4,5},{5,6},{6,7},{8,9},{9,10},{10,11},{12,13},{... | collective-permute-start | bytes 786440 | tf_op jit(solution)/shard_map/ppermute | solution.py:320
  41.6 14.4 %collective-permute-start.5 = (f32[4,128,128]{2,1,0:T(8,128)S(1)}, f32[4,128,128]{2,1,0:T(8,128)S(1)}, u32[]{:S(2)}, u32[]{:S(2)}) collective-permute-start(f32[4,128,128]{2,1,0:T(8,128)S(1)} %pass_on.7), channel_id=1, source_target_pairs={{0,1},{1,2},{2,3},{4,5},{5,6},{6,7},{8,9},{9,10},{10,11},{12,13},{... | collective-permute-start | bytes 786440 | tf_op jit(solution)/shard_map/ppermute | solution.py:320
  47.2 10.4 %collective-permute-start.2 = (f32[4,128,128]{2,1,0:T(8,128)S(1)}, f32[4,128,128]{2,1,0:T(8,128)S(1)}, u32[]{:S(2)}, u32[]{:S(2)}) collective-permute-start(f32[4,128,128]{2,1,0:T(8,128)S(1)} %pass_on.5), channel_id=1, source_target_pairs={{0,1},{1,2},{2,3},{4,5},{5,6},{6,7},{8,9},{9,10},{10,11},{12,13},{... | collective-permute-start | bytes 786440 | tf_op jit(solution)/shard_map/ppermute | solution.py:320
  51.6 1.0 %copy-start.1 = (f32[2048]{0:T(1024)S(1)}, f32[2048]{0:T(1024)}, u32[]{:S(2)}) copy-start(f32[2048]{0:T(1024)} %param.12) | copy-start | bytes 24580

commit v3 on v2

--- a/solution.py
+++ b/solution.py
@@ -11,8 +11,12 @@
 BF16 = jnp.bfloat16
 TILE = 16
 BLOCK = 64
+SPAN = 4
 GROUP = 4
 LAG = 2
+FINISH = 4
+AHEAD = 0
+COST = pl.CostEstimate(flops=1, transcendentals=0, bytes_accessed=1)
 
 
 def halves(x):
@@ -137,31 +141,47 @@
     return done
 
 
-def span_kernel(
-    group, lengths_ref, q_ref, k_ref, v_ref, beta_ref, g_ref, a_ref, b_ref, out_ref, reach_ref
-):
-    count = q_ref.shape[0]
-    width = a_ref.shape[1]
+def documents(lengths_ref, count, most, strict_ref, lower_ref, fresh_ref, flags_ref):
     first = lax.axis_index("ctx") * count
     ids_col, before = doc_ids(lengths_ref, first, (count, 1), 0)
     ids_row, _ = doc_ids(lengths_ref, first, (1, count), 1)
     row = lax.broadcasted_iota(jnp.int32, (count, count), 0)
     col = lanes_of((count, count))
     same = ids_col == ids_row
-    lower = same & (row >= col)
-    strict = same & (row > col)
-    sums = (row >= col).astype(F32).astype(BF16)
-    fresh = ids_col == before
-    tail = (ids_row == ids_row[:, count - 1 :]).astype(F32)
-    kept = (ids_row[:, count - 1 :] == before).astype(F32)
-    cumul_all = dot(sums, g_ref[...])
+    lower_ref[...] = (same & (row >= col)).astype(F32)
+    strict_ref[...] = (same & (row > col)).astype(F32)
+    fresh_ref[...] = jnp.broadcast_to((ids_col == before).astype(F32), fresh_ref.shape)
+    last = ids_row[:, count - 1 :]
+    start = jnp.int32(0)
+    latest = jnp.int32(0)
+    for d in range(lengths_ref.shape[0]):
+        latest = jnp.where(start < first, start, latest)
+        start = start + lengths_ref[d]
+    back = jnp.int32(0)
+    for i in range(1, most):
+        back = back + jnp.where(latest < first - i * count, 1, 0)
+    flags_ref[0:1, :] = (ids_row == last).astype(F32)
+    flags_ref[1:2, :] = jnp.broadcast_to((last == before).astype(F32), (1, count))
+    flags_ref[2:3, :] = jnp.full((1, count), back.astype(F32))
+
+
+def span_heads(head, q_ref, k_ref, v_ref, beta_ref, g_ref, strict_ref, lower_ref, fresh_ref, flags_ref, refs):
+    count = q_ref.shape[0]
+    out_ref, reach_ref = refs[0], refs[1]
+    a_refs, b_refs = refs[2::2], refs[3::2]
+    group, width, _ = a_refs[0].shape
+    heads = range(len(a_refs) * group)
+    here = [slice((head + h) * width, (head + h + 1) * width) for h in heads]
+    row = lax.broadcasted_iota(jnp.int32, (count, count), 0)
+    sums = (row >= lanes_of((count, count))).astype(F32).astype(BF16)
+    cumul_all = dot(sums, g_ref[:, here[0].start : here[-1].stop])
     eye = lax.broadcasted_iota(jnp.int32, (width, width), 0) == lanes_of((width, width))
-    heads = range(a_ref.shape[0])
-    here = [slice(h * width, (h + 1) * width) for h in heads]
-    strength = [beta_ref[group * len(heads) + h :][:1] for h in heads]
+    strength = [beta_ref[head + h : head + h + 1, :] for h in heads]
+    tail = flags_ref[0:1, :]
+    kept = flags_ref[1:2, :width]
     total, half, kneg, kpos, qpos = [], [], [], [], []
     for h in heads:
-        cumul = cumul_all[:, here[h]]
+        cumul = cumul_all[:, h * width : (h + 1) * width]
         total.append(cumul[count - 1 :, :])
         middle = total[h] * 0.5
         half.append(jnp.exp(middle))
@@ -175,6 +195,7 @@
         * strength[h]
         for h in heads
     ]
+    strict = strict_ref[...] > 0.0
     systems = [jnp.where(strict, x[:count], 0.0) for x in products]
     rights = []
     for h in heads:
@@ -187,57 +208,106 @@
             )
         )
     updates = solve(systems, rights, count)
+    lower = lower_ref[...] > 0.0
+    fresh = fresh_ref[...] > 0.0
     for h in heads:
         scores = jnp.where(lower, products[h][count:], 0.0)
         khat = (kneg[h] * half[h]).T * (strength[h] * tail)
         found = dot3(halves(jnp.concatenate([khat, scores], axis=0)), updates[h])
-        b_ref[h] = found[:width, :width]
-        a_ref[h] = (jnp.where(eye, jnp.exp(total[h]), 0.0) - found[:width, width:]) * kept
-        out_ref[:, here[h]] = found[width:, :width]
-        reach_ref[:, here[h]] = jnp.where(fresh, qpos[h] * half[h] - found[width:, width:], 0.0)
+        b_refs[h // group][h % group] = found[:width, :width]
+        a_refs[h // group][h % group] = (
+            jnp.where(eye, jnp.exp(total[h]), 0.0) - found[:width, width:]
+        ) * kept
+        at = slice(h * width, (h + 1) * width)
+        out_ref[:, at] = found[width:, :width]
+        reach_ref[:, at] = jnp.where(fresh, qpos[h] * half[h] - found[width:, width:], 0.0)
 
 
 VMEM = pl.BlockSpec(memory_space=pltpu.VMEM)
-SMEM = pl.BlockSpec(memory_space=pltpu.SMEM)
-
-
-def span(group, lengths, queries, keys, values, strength, log_decay):
+ANY = pl.BlockSpec(memory_space=pl.ANY)
+
+
+def opening_kernel(most, *refs):
+    lengths_hbm, beta_hbm, *sources = refs[:6]
+    beta_ref, *targets = refs[6:11]
+    masks = refs[11:15]
+    outs = refs[15:-2]
+    lengths_ref, sems = refs[-2:]
+    count = sources[0].shape[0]
+    cols = outs[0].shape[1]
+    first = [(lengths_hbm, lengths_ref), (beta_hbm, beta_ref)]
+    first += [(x.at[:, :cols], y.at[:, :cols]) for x, y in zip(sources, targets)]
+    rest = [(x.at[:, cols:], y.at[:, cols:]) for x, y in zip(sources, targets)]
+    copies = [pltpu.make_async_copy(x, y, sems.at[i]) for i, (x, y) in enumerate(first + rest)]
+    for copy in copies:
+        copy.start()
+    copies[0].wait()
+    documents(lengths_ref, count, most, *masks)
+    for copy in copies[1 : len(first)]:
+        copy.wait()
+    q_ref, k_ref, v_ref, g_ref = targets
+    span_heads(0, q_ref, k_ref, v_ref, beta_ref, g_ref, *masks, outs)
+    for copy in copies[len(first) :]:
+        copy.wait()
+
+
+def span_shapes(count, width):
+    part = jax.ShapeDtypeStruct((count, SPAN * width), F32)
+    square = jax.ShapeDtypeStruct((GROUP, width, width), F32)
+    return [part, part] + [square] * (2 * SPAN // GROUP)
+
+
+def opening(most, lengths, strength, queries, keys, values, log_decay):
     count, total = queries.shape
     heads = strength.shape[0]
     width = total // heads
-    cols = GROUP * width
-    rows = pl.BlockSpec((count, cols), lambda i: (0, group))
-    square = jax.ShapeDtypeStruct((GROUP, width, width), F32)
-    part = jax.ShapeDtypeStruct((count, cols), F32)
+    given = [lengths, strength, queries, keys, values, log_decay]
+    given = [pltpu.with_memory_space_constraint(x, pltpu.HBM) for x in given]
+    square = jax.ShapeDtypeStruct((count, count), F32)
+    kept = [jax.ShapeDtypeStruct(x.shape, x.dtype) for x in given[1:]]
+    kept += [
+        square,
+        square,
+        jax.ShapeDtypeStruct((count, width), F32),
+        jax.ShapeDtypeStruct((8, count), F32),
+    ]
+    shapes = kept + span_shapes(count, width)
+    results = pl.pallas_call(
+        functools.partial(opening_kernel, most),
+        in_specs=[ANY] * len(given),
+        out_specs=[VMEM] * len(shapes),
+        out_shape=shapes,
+        scratch_shapes=[pltpu.SMEM(lengths.shape, lengths.dtype), pltpu.SemaphoreType.DMA((10,))],
+        compiler_params=pltpu.CompilerParams(vmem_limit_bytes=32 << 20),
+        cost_estimate=COST,
+        name="opening",
+    )(*given)
+    return results[: len(kept)], results[len(kept) :]
+
+
+def span_kernel(head, beta_ref, q_ref, k_ref, v_ref, g_ref, *refs):
+    span_heads(head, q_ref, k_ref, v_ref, beta_ref, g_ref, *refs[:4], refs[4:])
+
+
+def span(head, shared):
+    count = shared[1].shape[0]
+    width = shared[1].shape[1] // shared[0].shape[0]
+    shapes = span_shapes(count, width)
     return pl.pallas_call(
-        functools.partial(span_kernel, group),
-        grid=(1,),
-        in_specs=[SMEM, rows, rows, rows, VMEM, rows],
-        out_specs=[VMEM] * 4,
-        out_shape=[square, square, part, part],
+        functools.partial(span_kernel, head),
+        in_specs=[VMEM] * len(shared),
+        out_specs=[VMEM] * len(shapes),
+        out_shape=shapes,
         compiler_params=pltpu.CompilerParams(vmem_limit_bytes=32 << 20),
+        cost_estimate=COST,
         name="span",
-    )(lengths, queries, keys, values, strength, log_decay)
-
-
-def spans_back(lengths_ref, count, most):
-    first = lax.axis_index("ctx") * count
-    start = jnp.int32(0)
-    latest = jnp.int32(0)
-    fresh = jnp.int32(0)
-    for d in range(lengths_ref.shape[0]):
-        latest = jnp.where(start < first, start, latest)
-        fresh = jnp.where((start >= first) & (start < first + count), 1, fresh)
-        start = start + lengths_ref[d]
-    back = jnp.int32(0)
-    for i in range(1, most):
-        back = back + jnp.where(latest < first - i * count, 1, 0)
-    return back, fresh
-
-
-def pass_kernel(count, most, own, low, late, lengths_ref, state_ref, *refs):
+    )(*shared)
+
+
+def pass_kernel(own, low, late, flags_ref, state_ref, *refs):
     out_ref = refs[-1]
-    before, fresh = spans_back(lengths_ref, count, most)
+    width = out_ref.shape[1]
+    before = flags_ref[2:3, :width]
     for h in range(out_ref.shape[0]):
         trans_a, trans_b = refs[own][h], refs[own + 1][h]
         for i in range(1, late):
@@ -245,10 +315,10 @@
             trans_a = jnp.where(here, refs[own + 2 * i][h], trans_a)
             trans_b = jnp.where(here, refs[own + 2 * i + 1][h], trans_b)
         sent = trans_b + dot3(halves(trans_a), halves(state_ref[h]))
-        out_ref[h] = jnp.where(fresh == 1, refs[0][h], sent) if own else sent
-
-
-def message(step, count, most, lengths, trans_a, trans_b, received):
+        out_ref[h] = jnp.where(flags_ref[1:2, :width] > 0.0, sent, refs[0][h]) if own else sent
+
+
+def message(step, most, flags, trans_a, trans_b, received):
     own = [trans_b[step]] if step < len(trans_b) else []
     if step < LAG:
         return own[0]
@@ -257,72 +327,113 @@
     late = [x for x in late if 0 <= x < len(trans_b)]
     carried = [x for g in late for x in (trans_a[g], trans_b[g])]
     return pl.pallas_call(
-        functools.partial(pass_kernel, count, most, len(own), low, len(late)),
-        in_specs=[SMEM] + [VMEM] * (1 + len(own) + len(carried)),
+        functools.partial(pass_kernel, len(own), low, len(late)),
+        in_specs=[VMEM] * (2 + len(own) + len(carried)),
         out_specs=VMEM,
         out_shape=jax.ShapeDtypeStruct(trans_b[0].shape, F32),
         compiler_params=pltpu.CompilerParams(vmem_limit_bytes=8 << 20),
+        cost_estimate=COST,
         name="pass_on",
-    )(lengths, received[step - LAG], *own, *carried)
-
-
-def finish_kernel(lengths_ref, out_ref, reach_ref, gain_ref, *refs):
-    states = refs[:-2]
+    )(flags, received[step - LAG], *own, *carried)
+
+
+def finish_kernel(head, most, spans, flags_ref, gain_ref, *refs):
     mixed_ref = refs[-1]
-    heads, width, _ = states[0].shape
-    before, _ = spans_back(lengths_ref, out_ref.shape[0], len(states))
-    for h in range(heads):
-        here = slice(h * width, (h + 1) * width)
-        state = states[0][h]
-        for i in range(1, len(states)):
-            state = jnp.where(before == i, states[i][h], state)
-        outs = out_ref[:, here] + dot3(halves(reach_ref[:, here]), halves(state))
-        scale = lax.rsqrt(jnp.mean(outs * outs, axis=-1, keepdims=True) + 1e-06)
-        mixed_ref[:, here] = (outs * scale * gain_ref[:, here]).astype(BF16)
-
-
-def finished(group, mixed, lengths, outs, reach, states, gain):
-    count, cols = outs.shape
+    outs, reach = refs[:spans], refs[spans : 2 * spans]
+    states = refs[2 * spans : -1]
+    group, width, _ = states[0].shape
+    before = flags_ref[2:3, :width]
+    for h in range(mixed_ref.shape[1] // width):
+        at = (head + h) % SPAN * width
+        here = slice(at, at + width)
+        state = states[h // group * most][h % group]
+        for i in range(1, most):
+            state = jnp.where(before == i, states[h // group * most + i][h % group], state)
+        of = h // SPAN
+        total = outs[of][:, here] + dot3(halves(reach[of][:, here]), halves(state))
+        scale = lax.rsqrt(jnp.mean(total * total, axis=-1, keepdims=True) + 1e-06)
+        gain = gain_ref[:, (head + h) * width : (head + h + 1) * width]
+        mixed_ref[:, h * width : (h + 1) * width] = (total * scale * gain).astype(BF16)
+
+
+def finish_first(*refs):
+    finish_kernel(*refs)
+
+
+def finish_next(head, most, spans, flags_ref, gain_ref, *refs):
+    finish_kernel(head, most, spans, flags_ref, gain_ref, *refs[:-2], refs[-1])
+
+
+def finished(head, mixed, flags, outs, reach, received, most, gain):
+    count = outs[0].shape[0]
+    width = received[0].shape[1]
+    low, high = head // SPAN, (head + FINISH - 1) // SPAN + 1
+    groups = range(head // GROUP, (head + FINISH) // GROUP)
+    states = [received[g + LAG * i] for g in groups for i in range(most)]
+    given = [flags, gain, *outs[low:high], *reach[low:high], *states]
+    specs = [VMEM] * len(given)
+    aliases = {}
+    if mixed is not None:
+        aliases = {len(given): 0}
+        given.append(mixed)
+        specs.append(ANY)
+    kernel = finish_first if mixed is None else finish_next
     return pl.pallas_call(
-        finish_kernel,
+        functools.partial(kernel, head, most, high - low),
         grid=(1,),
-        in_specs=[SMEM, VMEM, VMEM, pl.BlockSpec((1, cols), lambda i: (0, group))]
-        + [VMEM] * len(states)
-        + [pl.BlockSpec(memory_space=pl.ANY)],
-        out_specs=pl.BlockSpec((count, cols), lambda i: (0, group)),
-        out_shape=jax.ShapeDtypeStruct(mixed.shape, BF16),
-        input_output_aliases={4 + len(states): 0},
+        in_specs=specs,
+        out_specs=pl.BlockSpec((count, FINISH * width), lambda i: (0, head // FINISH)),
+        out_shape=jax.ShapeDtypeStruct((count, gain.shape[1]), BF16),
+        input_output_aliases=aliases,
         compiler_params=pltpu.CompilerParams(vmem_limit_bytes=8 << 20),
+        cost_estimate=COST,
         name="finish",
-    )(lengths, outs, reach, gain, *states, mixed)
+    )(*given)
+
+
+def then(flags, results):
+    flags, results = lax.optimization_barrier((flags, tuple(results)))
+    return flags, list(results)
 
 
 def local(queries, keys, values, beta, log_decay, out_gain, doc_lengths):
     devices = lax.axis_size("ctx")
-    pairs = [(i, i + 1) for i in range(devices - 1)]
-    count = queries.shape[0]
-    groups = beta.shape[1] // GROUP
+    ring = [(i, (i + 1) % devices) for i in range(devices)]
+    heads = beta.shape[1]
     most = devices // 2
-    queries, keys, values, log_decay = (
-        pltpu.with_memory_space_constraint(x, pltpu.HBM)
-        for x in (queries, keys, values, log_decay)
-    )
-    strength = beta.T
-    trans_a, trans_b, outs, reach = zip(
-        *(
-            span(g, doc_lengths, queries, keys, values, strength, log_decay)
-            for g in range(groups)
-        )
-    )
-    received = []
-    for step in range(groups + LAG * (most - 1)):
-        sent = message(step, count, most, doc_lengths, trans_a, trans_b, received)
-        received.append(lax.ppermute(sent, "ctx", pairs))
-    mixed = jnp.zeros(queries.shape, BF16)
+    shared, first = opening(most, doc_lengths, beta.T, queries, keys, values, log_decay)
+    shared, flags = shared[:-1], shared[-1]
+    flags, first = then(flags, first)
+    outs, reach, trans_a, trans_b, received = [], [], [], [], []
+    mixed = None
     gain = out_gain.reshape(1, -1)
-    for g in range(groups):
-        states = [received[g + LAG * i] for i in range(most)]
-        mixed = finished(g, mixed, doc_lengths, outs[g], reach[g], states, gain)
+    groups = heads // GROUP
+    steps = groups + LAG * (most - 1)
+    head = SPAN
+
+    def keep(found):
+        outs.append(found[0])
+        reach.append(found[1])
+        trans_a.extend(found[2::2])
+        trans_b.extend(found[3::2])
+
+    keep(first)
+    ended = 0
+    for step in range(steps):
+        while head < heads and head < (step + 1 + AHEAD * (step >= LAG)) * GROUP:
+            flags, found = then(flags, span(head, [*shared, flags]))
+            keep(found)
+            head += SPAN
+        sent = message(step, most, flags, trans_a, trans_b, received)
+        if step >= LAG:
+            flags, (sent,) = then(flags, [sent])
+        received.append(lax.ppermute(sent, "ctx", ring))
+        while head >= heads and ended + FINISH <= (step - 1 - LAG * (most - 1)) * GROUP:
+            mixed = finished(ended, mixed, flags, outs, reach, received, most, gain)
+            flags, (mixed,) = then(flags, [mixed])
+            ended += FINISH
+    for h in range(ended, heads, FINISH):
+        mixed = finished(h, mixed, flags, outs, reach, received, most, gain)
     return mixed
 
 

time: 59.7 us -> 45.7 us (0.77)
  starting transfers between devices: 22.8 us -> 6.48 us
  waiting for transfers between devices: 4.37 us -> 17.8 us
  Pallas kernels: 29.7 us -> 21.2 us
  local copies, waits for them, and re-layouts: 2.34 us -> 0.01 us
    ppermute x6, starting transfers between devices: 22.8 us -> 6.48 us  [local(): received.append(lax.ppermute(sent, 'ctx', ring))]
    ppermute x6, waiting for transfers between devices: 4.37 us -> 17.8 us  [local(): received.append(lax.ppermute(sent, 'ctx', ring))]
    pallas_call x12, Pallas kernels: 29.7 us -> 21.2 us  [the longest x3 10.8 us: span(): pl.pallas_call(functools.partial(span_kernel, head), in_specs=[VMEM] * le...]
    unnamed x6 -> x2, local copies, waits for them, and re-layouts: 1.38 us -> 0.01 us
    broadcast_in_dim x1 -> x0, local copies, waits for them, and re-layouts: 0.97 us -> none  [local(): mixed = jnp.zeros(queries.shape, BF16)]
  transfers between devices with their start and end apart: 6 -> 6, of which waited for: 2 -> 6; matrix products, arithmetic and copies ran while one was open for 2% -> 0% of each run, Pallas kernels for 39% -> 33%
where the time goes in v3:
time: 45.7 us; the launch traced here: 45.5 us
  Pallas kernels  21.2 us (46%)
  waiting for transfers between devices  17.8 us (39%)
  starting transfers between devices  6.48 us (14%)
    ppermute x6, waiting for transfers between devices, local(): received.append(lax.ppermute(sent, 'ctx', ring))  17.8 us
    pallas_call x3, Pallas kernels, span(): pl.pallas_call(functools.partial(span_kernel, head), in_specs=[VMEM] * le...  10.8 us
    ppermute x6, starting transfers between devices, local(): received.append(lax.ppermute(sent, 'ctx', ring))  6.48 us
    pallas_call x1, Pallas kernels, opening(): pl.pallas_call(functools.partial(opening_kernel, most), in_specs=[ANY] *...  4.9 us
    pallas_call x4, Pallas kernels, finished(): pl.pallas_call(functools.partial(kernel, head, most, high - low), grid=(1...  4.43 us
    pallas_call x4, Pallas kernels, message(): pl.pallas_call(functools.partial(pass_kernel, len(own), low, len(late)),...  1.05 us
  transfers between devices with their start and end apart: 6, of which 6 were waited for; matrix products, arithmetic and copies ran while one was open for 0% of the time, Pallas kernels for 33%

profile of v3, /device:TPU:0, one launch (start us, length us, event | category | flops | bytes accessed | tf_op | source)
XLA Modules:
  0.0 45.5 jit_solution(2454485152689416110)
XLA Ops:
  0.0 4.9 %opening.1 = (f32[16,192]{1,0:T(8,128)S(1)}, bf16[192,2048]{1,0:T(8,128)(2,1)S(1)}, bf16[192,2048]{1,0:T(8,128)(2,1)S(1)}, bf16[192,2048]{1,0:T(8,128)(2,1)S(1)}...) custom-call(s32[16]{0:T(128)} %refs_0_.1, ...), custom_call_target="tpu_custom_call" | custom-call | flops 1 | bytes 1 | tf_op jit(solution)/shard_map/opening/pallas_call | solution.py:275
  4.9 3.1 %collective-permute-start = (f32[4,128,128]{2,1,0:T(8,128)S(1)}, f32[4,128,128]{2,1,0:T(8,128)S(1)}, u32[]{:S(2)}, u32[]{:S(2)}) collective-permute-start(f32[4,128,128]{2,1,0:T(8,128)S(1)} %get-tuple-element.86.refs_2_), channel_id=1, source_target_pairs={{0,1},{1,2},{2,3},{3,0},{4,5},{5,6},{6,7},{7,4},{8,9},{9,10},{10,1... | collective-permute-start | bytes 786440 | tf_op jit(solution)/shard_map/ppermute | solution.py:430
  8.0 3.6 %span.3 = (f32[192,512]{1,0:T(8,128)S(1)}, f32[192,512]{1,0:T(8,128)S(1)}, f32[4,128,128]{2,1,0:T(8,128)S(1)}, f32[4,128,128]{2,1,0:T(8,128)S(1)}) custom-call(f32[16,192]{1,0:T(8,128)S(1)} %get-tuple-element.68.beta_ref, bf16[192,2048]{1,0:T(8,128)(2,1)S(1)} %get-tuple-element.69.q_ref, bf16[192,2048]{1,0:T(8,128)(2,1)S(1)} %get-tuple-element.70.k_ref, ...), custom_call_target="tpu_custom_call" | custom-call | flops 1 | bytes 1 | tf_op jit(solution)/shard_map/span/pallas_call | solution.py:296
  11.6 1.6 %collective-permute-start.1 = (f32[4,128,128]{2,1,0:T(8,128)S(1)}, f32[4,128,128]{2,1,0:T(8,128)S(1)}, u32[]{:S(2)}, u32[]{:S(2)}) collective-permute-start(f32[4,128,128]{2,1,0:T(8,128)S(1)} %get-tuple-element.95.refs_2_), channel_id=1, source_target_pairs={{0,1},{1,2},{2,3},{3,0},{4,5},{5,6},{6,7},{7,4},{8,9},{9,10},{10,1... | collective-permute-start | bytes 786440 | tf_op jit(solution)/shard_map/ppermute | solution.py:430
  13.2 3.6 %span.4 = (f32[192,512]{1,0:T(8,128)S(1)}, f32[192,512]{1,0:T(8,128)S(1)}, f32[4,128,128]{2,1,0:T(8,128)S(1)}, f32[4,128,128]{2,1,0:T(8,128)S(1)}) custom-call(f32[16,192]{1,0:T(8,128)S(1)} %get-tuple-element.68.beta_ref, bf16[192,2048]{1,0:T(8,128)(2,1)S(1)} %get-tuple-element.69.q_ref, bf16[192,2048]{1,0:T(8,128)(2,1)S(1)} %get-tuple-element.70.k_ref, ...), custom_call_target="tpu_custom_call" | custom-call | flops 1 | bytes 1 | tf_op jit(solution)/shard_map/span/pallas_call | solution.py:296
  16.8 0.2 collective-permute-done.state_ref.refs_4_
  17.0 0.3 pass_on.4
  17.3 1.7 %collective-permute-start.2 = (f32[4,128,128]{2,1,0:T(8,128)S(1)}, f32[4,128,128]{2,1,0:T(8,128)S(1)}, u32[]{:S(2)}, u32[]{:S(2)}) collective-permute-start(f32[4,128,128]{2,1,0:T(8,128)S(1)} %pass_on.4), channel_id=1, source_target_pairs={{0,1},{1,2},{2,3},{3,0},{4,5},{5,6},{6,7},{7,4},{8,9},{9,10},{10,1... | collective-permute-start | bytes 786440 | tf_op jit(solution)/shard_map/ppermute | solution.py:430
  18.9 3.6 %span.5 = (f32[192,512]{1,0:T(8,128)S(1)}, f32[192,512]{1,0:T(8,128)S(1)}, f32[4,128,128]{2,1,0:T(8,128)S(1)}, f32[4,128,128]{2,1,0:T(8,128)S(1)}) custom-call(f32[16,192]{1,0:T(8,128)S(1)} %get-tuple-element.68.beta_ref, bf16[192,2048]{1,0:T(8,128)(2,1)S(1)} %get-tuple-element.69.q_ref, bf16[192,2048]{1,0:T(8,128)(2,1)S(1)} %get-tuple-element.70.k_ref, ...), custom_call_target="tpu_custom_call" | custom-call | flops 1 | bytes 1 | tf_op jit(solution)/shard_map/span/pallas_call | solution.py:296
  22.5 0.2 collective-permute-done.1.state_ref.refs_2_
  22.7 0.3 pass_on.5
  22.9 0.0 copy-start
  23.0 0.1 collective-permute-start.3
  23.0 5.5 %collective-permute-done.2.state_ref.refs_5_.refs_2_ = f32[4,128,128]{2,1,0:T(8,128)S(1)} collective-permute-done((f32[4,128,128]{2,1,0:T(8,128)S(1)}, f32[4,128,128]{2,1,0:T(8,128)S(1)}, u32[]{:S(2)}, u32[]{:S(2)}) %collective-permute-start.2) | collective-permute-done | bytes 262176 | tf_op jit(solution)/shard_map/ppermute | solution.py:430
  28.5 0.3 pass_on.6
  28.8 1.1 %finish.4.refs_4_ = bf16[192,2048]{1,0:T(8,128)(2,1)} custom-call(f32[8,192]{1,0:T(8,128)S(1)} %get-tuple-element.111.refs_3_.flags_ref.refs_0_, f32[1,2048]{1,0:T(1,128)S(1)} %bitcast.2, f32[192,512]{1,0:T(8,128)S(1)} %get-tuple-element.102.refs_2_, f32[192,512]{1,0:T(8,128)S(1)} %get-tuple-element.103.refs_3_, ...), custom_call_target="tpu_custom_call" | custom-call | flops 1 | bytes 1 | tf_op jit(solution)/shard_map/finish/pallas_call | solution.py:381
  29.9 3.9 %collective-permute-done.3.state_ref.refs_3_.refs_2_ = f32[4,128,128]{2,1,0:T(8,128)S(1)} collective-permute-done((f32[4,128,128]{2,1,0:T(8,128)S(1)}, f32[4,128,128]{2,1,0:T(8,128)S(1)}, u32[]{:S(2)}, u32[]{:S(2)}) %collective-permute-start.3) | collective-permute-done | bytes 262176 | tf_op jit(solution)/shard_map/ppermute | solution.py:430
  33.8 0.3 pass_on.7
  34.1 0.1 collective-permute-start.4
  34.2 1.1 %finish.5.refs_4_ = bf16[192,2048]{1,0:T(8,128)(2,1)} custom-call(f32[8,192]{1,0:T(8,128)S(1)} %get-tuple-element.111.refs_3_.flags_ref.refs_0_, f32[1,2048]{1,0:T(1,128)S(1)} %bitcast.3, f32[192,512]{1,0:T(8,128)S(1)} %get-tuple-element.108.refs_0_, f32[192,512]{1,0:T(8,128)S(1)} %get-tuple-element.109.refs_1_, ...), custom_call_target="tpu_custom_call", output_to_operand_aliasing={{}: (6, {})} | custom-call | flops 1 | bytes 1 | tf_op jit(solution)/shard_map/finish/pallas_call | solution.py:381
  35.3 5.2 %collective-permute-done.5.refs_3_ = f32[4,128,128]{2,1,0:T(8,128)S(1)} collective-permute-done((f32[4,128,128]{2,1,0:T(8,128)S(1)}, f32[4,128,128]{2,1,0:T(8,128)S(1)}, u32[]{:S(2)}, u32[]{:S(2)}) %collective-permute-start.5) | collective-permute-done | bytes 262176 | tf_op jit(solution)/shard_map/ppermute | solution.py:430
  40.5 1.1 %finish.6.refs_4_ = bf16[192,2048]{1,0:T(8,128)(2,1)} custom-call(f32[8,192]{1,0:T(8,128)S(1)} %get-tuple-element.111.refs_3_.flags_ref.refs_0_, f32[1,2048]{1,0:T(1,128)S(1)} %bitcast.4, f32[192,512]{1,0:T(8,128)S(1)} %get-tuple-element.115.refs_0_, f32[192,512]{1,0:T(8,128)S(1)} %get-tuple-element.116.refs_1_, ...), custom_call_target="tpu_custom_call", output_to_operand_aliasing={{}: (6, {})} | custom-call | flops 1 | bytes 1 | tf_op jit(solution)/shard_map/finish/pallas_call | solution.py:381
  41.6 2.8 %collective-permute-done.4.refs_3_ = f32[4,128,128]{2,1,0:T(8,128)S(1)} collective-permute-done((f32[4,128,128]{2,1,0:T(8,128)S(1)}, f32[4,128,128]{2,1,0:T(8,128)S(1)}, u32[]{:S(2)}, u32[]{:S(2)}) %collective-permute-start.4) | collective-permute-done | bytes 262176 | tf_op jit(solution)/shard_map/ppermute | solution.py:430
  44.4 1.1 %finish.7 = bf16[192,2048]{1,0:T(8,128)(2,1)} custom-call(f32[8,192]{1,0:T(8,128)S(1)} %get-tuple-element.111.refs_3_.flags_ref.refs_0_, f32[1,2048]{1,0:T(1,128)S(1)} %bitcast.5, f32[192,512]{1,0:T(8,128)S(1)} %get-tuple-element.112.refs_0_, f32[192,512]{1,0:T(8,128)S(1)} %get-tuple-element.113.refs_1_, ...), custom_call_target="tpu_custom_call", output_to_operand_aliasing={{}: (6, {})} | custom-call | flops 1 | bytes 1 | tf_op jit(solution)/shard_map/finish/pallas_call | solution.py:381
  (2 shorter events, 0.0 us)
Async XLA Ops:
  4.9 12.1 %collective-permute-start = (f32[4,128,128]{2,1,0:T(8,128)S(1)}, f32[4,128,128]{2,1,0:T(8,128)S(1)}, u32[]{:S(2)}, u32[]{:S(2)}) collective-permute-start(f32[4,128,128]{2,1,0:T(8,128)S(1)} %get-tuple-element.86.refs_2_), channel_id=1, source_target_pairs={{0,1},{1,2},{2,3},{3,0},{4,5},{5,6},{6,7},{7,4},{8,9},{9,10},{10,1... | collective-permute-start | bytes 786440 | tf_op jit(solution)/shard_map/ppermute | solution.py:430
  11.6 11.1 %collective-permute-start.1 = (f32[4,128,128]{2,1,0:T(8,128)S(1)}, f32[4,128,128]{2,1,0:T(8,128)S(1)}, u32[]{:S(2)}, u32[]{:S(2)}) collective-permute-start(f32[4,128,128]{2,1,0:T(8,128)S(1)} %get-tuple-element.95.refs_2_), channel_id=1, source_target_pairs={{0,1},{1,2},{2,3},{3,0},{4,5},{5,6},{6,7},{7,4},{8,9},{9,10},{10,1... | collective-permute-start | bytes 786440 | tf_op jit(solution)/shard_map/ppermute | solution.py:430
  17.3 11.3 %collective-permute-start.2 = (f32[4,128,128]{2,1,0:T(8,128)S(1)}, f32[4,128,128]{2,1,0:T(8,128)S(1)}, u32[]{:S(2)}, u32[]{:S(2)}) collective-permute-start(f32[4,128,128]{2,1,0:T(8,128)S(1)} %pass_on.4), channel_id=1, source_target_pairs={{0,1},{1,2},{2,3},{3,0},{4,5},{5,6},{6,7},{7,4},{8,9},{9,10},{10,1... | collective-permute-start | bytes 786440 | tf_op jit(solution)/shard_map/ppermute | solution.py:430
  22.9 5.9 %copy-start = (f32[2048]{0:T(1024)S(1)}, f32[2048]{0:T(1024)}, u32[]{:S(2)}) copy-start(f32[2048]{0:T(1024)} %param.12) | copy-start | bytes 24580
  23.0 10.9 %collective-permute-start.3 = (f32[4,128,128]{2,1,0:T(8,128)S(1)}, f32[4,128,128]{2,1,0:T(8,128)S(1)}, u32[]{:S(2)}, u32[]{:S(2)}) collective-permute-start(f32[4,128,128]{2,1,0:T(8,128)S(1)} %pass_on.5), channel_id=1, source_target_pairs={{0,1},{1,2},{2,3},{3,0},{4,5},{5,6},{6,7},{7,4},{8,9},{9,10},{10,1... | collective-permute-start | bytes 786440 | tf_op jit(solution)/shard_map/ppermute | solution.py:430
  29.9 10.6 %collective-permute-start.5 = (f32[4,128,128]{2,1,0:T(8,128)S(1)}, f32[4,128,128]{2,1,0:T(8,128)S(1)}, u32[]{:S(2)}, u32[]{:S(2)}) collective-permute-start(f32[4,128,128]{2,1,0:T(8,128)S(1)} %pass_on.6), channel_id=1, source_target_pairs={{0,1},{1,2},{2,3},{3,0},{4,5},{5,6},{6,7},{7,4},{8,9},{9,10},{10,1... | collective-permute-start | bytes 786440 | tf_op jit(solution)/shard_map/ppermute | solution.py:430
  34.1 10.3 %collective-permute-start.4 = (f32[4,128,128]{2,1,0:T(8,128)S(1)}, f32[4,128,128]{2,1,0:T(8,128)S(1)}, u32[]{:S(2)}, u32[]{:S(2)}) collective-permute-start(f32[4,128,128]{2,1,0:T(8,128)S(1)} %pass_on.7), channel_id=1, source_target_pairs={{0,1},{1,2},{2,3},{3,0},{4,5},{5,6},{6,7},{7,4},{8,9},{9,10},{10,1... | collective-permute-start | bytes 786440 | tf_op jit(solution)/shard_map/ppermute | solution.py:430

commit v4 on v3

--- a/solution.py
+++ b/solution.py
@@ -11,12 +11,14 @@
 BF16 = jnp.bfloat16
 TILE = 16
 BLOCK = 64
-SPAN = 4
-GROUP = 4
-LAG = 2
-FINISH = 4
-AHEAD = 0
-COST = pl.CostEstimate(flops=1, transcendentals=0, bytes_accessed=1)
+SPANS = ((2,), (2, 2), (2, 2), (2, 2), (2,))
+LAG = 3
+FILL = (1,) * 99
+LATE = 2
+QUERY = pl.CostEstimate(flops=10**8, transcendentals=0, bytes_accessed=1)
+COST = pl.CostEstimate(flops=10**8, transcendentals=0, bytes_accessed=1)
+PASS = pl.CostEstimate(flops=10**6, transcendentals=0, bytes_accessed=1)
+END = pl.CostEstimate(flops=10**8, transcendentals=0, bytes_accessed=1)
 
 
 def halves(x):
@@ -165,13 +167,14 @@
     flags_ref[2:3, :] = jnp.full((1, count), back.astype(F32))
 
 
-def span_heads(head, q_ref, k_ref, v_ref, beta_ref, g_ref, strict_ref, lower_ref, fresh_ref, flags_ref, refs):
-    count = q_ref.shape[0]
-    out_ref, reach_ref = refs[0], refs[1]
-    a_refs, b_refs = refs[2::2], refs[3::2]
-    group, width, _ = a_refs[0].shape
-    heads = range(len(a_refs) * group)
+def span_heads(head, k_ref, v_ref, beta_ref, g_ref, strict_ref, flags_ref, refs):
+    count = k_ref.shape[0]
+    up_ref, half_ref, kneg_refs, update_refs = refs[0], refs[1], refs[2:4], refs[4:6]
+    width = refs[6].shape[1]
+    places = [(a, b, i) for a, b in zip(refs[6::2], refs[7::2]) for i in range(a.shape[0])]
+    heads = range(len(places))
     here = [slice((head + h) * width, (head + h + 1) * width) for h in heads]
+    own = [slice(h * width, (h + 1) * width) for h in heads]
     row = lax.broadcasted_iota(jnp.int32, (count, count), 0)
     sums = (row >= lanes_of((count, count))).astype(F32).astype(BF16)
     cumul_all = dot(sums, g_ref[:, here[0].start : here[-1].stop])
@@ -179,48 +182,90 @@
     strength = [beta_ref[head + h : head + h + 1, :] for h in heads]
     tail = flags_ref[0:1, :]
     kept = flags_ref[1:2, :width]
-    total, half, kneg, kpos, qpos = [], [], [], [], []
+    total, kneg, kpos, khat, parts = [], [], [], [], []
     for h in heads:
-        cumul = cumul_all[:, h * width : (h + 1) * width]
+        cumul = cumul_all[:, own[h]]
         total.append(cumul[count - 1 :, :])
         middle = total[h] * 0.5
-        half.append(jnp.exp(middle))
+        half = jnp.exp(middle)
         up = jnp.exp(cumul - middle)
+        up_ref[:, own[h]] = up
+        half_ref[0:1, own[h]] = half
         kn = unit_rows(k_ref[:, here[h]].astype(F32))
-        kneg.append(kn * jnp.exp(middle - cumul))
+        negative = kn * jnp.exp(middle - cumul)
+        kneg.append(halves(negative))
+        for ref, x in zip(kneg_refs, kneg[h]):
+            ref[:, own[h]] = x
         kpos.append(kn * up)
-        qpos.append(unit_rows(q_ref[:, here[h]].astype(F32)) * up)
-    products = [
-        dot3(halves(jnp.concatenate([kpos[h], qpos[h]], axis=0)), halves(kneg[h]), ((1,), (1,)))
-        * strength[h]
+        parts.append(halves(kpos[h] * half))
+        khat.append(halves((negative * half).T * (strength[h] * tail)))
+    strict = strict_ref[...] > 0.0
+    systems = [
+        jnp.where(strict, dot3(halves(kpos[h]), kneg[h], ((1,), (1,))) * strength[h], 0.0)
         for h in heads
     ]
-    strict = strict_ref[...] > 0.0
-    systems = [jnp.where(strict, x[:count], 0.0) for x in products]
     rights = []
     for h in heads:
-        high, low = halves(kpos[h] * half[h])
         value = v_ref[:, here[h]]
         rights.append(
             (
-                jnp.concatenate([value, high], axis=1),
-                jnp.concatenate([jnp.zeros_like(value), low], axis=1),
+                jnp.concatenate([value, parts[h][0]], axis=1),
+                jnp.concatenate([jnp.zeros_like(value), parts[h][1]], axis=1),
             )
         )
     updates = solve(systems, rights, count)
+    for h in heads:
+        for ref, x in zip(update_refs, updates[h]):
+            ref[:, 2 * h * width : 2 * (h + 1) * width] = x
+        found = dot3(khat[h], updates[h])
+        a_ref, b_ref, i = places[h]
+        b_ref[i] = found[:, :width]
+        a_ref[i] = (jnp.where(eye, jnp.exp(total[h]), 0.0) - found[:, width:]) * kept
+
+
+def query_kernel(head, q_ref, beta_ref, lower_ref, fresh_ref, flags_ref, *refs):
+    up_ref, half_ref, kneg_refs, update_refs = refs[0], refs[1], refs[2:4], refs[4:6]
+    out_ref, reach_ref = refs[6:]
+    count, width = fresh_ref.shape
+    heads = range(out_ref.shape[1] // width)
+    own = [slice(h * width, (h + 1) * width) for h in heads]
     lower = lower_ref[...] > 0.0
     fresh = fresh_ref[...] > 0.0
+    qpos = [
+        unit_rows(q_ref[:, (head + h) * width : (head + h + 1) * width].astype(F32))
+        * up_ref[:, own[h]]
+        for h in heads
+    ]
+    scores = []
     for h in heads:
-        scores = jnp.where(lower, products[h][count:], 0.0)
-        khat = (kneg[h] * half[h]).T * (strength[h] * tail)
-        found = dot3(halves(jnp.concatenate([khat, scores], axis=0)), updates[h])
-        b_refs[h // group][h % group] = found[:width, :width]
-        a_refs[h // group][h % group] = (
-            jnp.where(eye, jnp.exp(total[h]), 0.0) - found[:width, width:]
-        ) * kept
-        at = slice(h * width, (h + 1) * width)
-        out_ref[:, at] = found[width:, :width]
-        reach_ref[:, at] = jnp.where(fresh, qpos[h] * half[h] - found[width:, width:], 0.0)
+        kneg = tuple(x[:, own[h]] for x in kneg_refs)
+        product = dot3(halves(qpos[h]), kneg, ((1,), (1,)))
+        scores.append(
+            halves(jnp.where(lower, product * beta_ref[head + h : head + h + 1, :], 0.0))
+        )
+    for h in heads:
+        update = tuple(x[:, 2 * h * width : 2 * (h + 1) * width] for x in update_refs)
+        found = dot3(scores[h], update)
+        out_ref[:, own[h]] = found[:, :width]
+        reach_ref[:, own[h]] = jnp.where(
+            fresh, qpos[h] * half_ref[0:1, own[h]] - found[:, width:], 0.0
+        )
+
+
+def query(head, shared, flags, saved):
+    beta, queries, _, _, _, _, lower, fresh = shared
+    count = queries.shape[0]
+    part = jax.ShapeDtypeStruct(saved[0].shape, F32)
+    given = [queries, beta, lower, fresh, flags, *saved]
+    return pl.pallas_call(
+        functools.partial(query_kernel, head),
+        in_specs=[VMEM] * len(given),
+        out_specs=[VMEM] * 2,
+        out_shape=[part, part],
+        compiler_params=pltpu.CompilerParams(vmem_limit_bytes=32 << 20),
+        cost_estimate=QUERY,
+        name="query",
+    )(*given)
 
 
 VMEM = pl.BlockSpec(memory_space=pltpu.VMEM)
@@ -236,8 +281,9 @@
     count = sources[0].shape[0]
     cols = outs[0].shape[1]
     first = [(lengths_hbm, lengths_ref), (beta_hbm, beta_ref)]
-    first += [(x.at[:, :cols], y.at[:, :cols]) for x, y in zip(sources, targets)]
-    rest = [(x.at[:, cols:], y.at[:, cols:]) for x, y in zip(sources, targets)]
+    pairs = list(zip(sources, targets))
+    first += [(x.at[:, :cols], y.at[:, :cols]) for x, y in pairs[1:]]
+    rest = [(x.at[:, cols:], y.at[:, cols:]) for x, y in pairs[1:]] + pairs[:1]
     copies = [pltpu.make_async_copy(x, y, sems.at[i]) for i, (x, y) in enumerate(first + rest)]
     for copy in copies:
         copy.start()
@@ -245,19 +291,22 @@
     documents(lengths_ref, count, most, *masks)
     for copy in copies[1 : len(first)]:
         copy.wait()
-    q_ref, k_ref, v_ref, g_ref = targets
-    span_heads(0, q_ref, k_ref, v_ref, beta_ref, g_ref, *masks, outs)
+    _, k_ref, v_ref, g_ref = targets
+    strict_ref, _, _, flags_ref = masks
+    span_heads(0, k_ref, v_ref, beta_ref, g_ref, strict_ref, flags_ref, outs)
     for copy in copies[len(first) :]:
         copy.wait()
 
 
-def span_shapes(count, width):
-    part = jax.ShapeDtypeStruct((count, SPAN * width), F32)
-    square = jax.ShapeDtypeStruct((GROUP, width, width), F32)
-    return [part, part] + [square] * (2 * SPAN // GROUP)
-
-
-def opening(most, lengths, strength, queries, keys, values, log_decay):
+def span_shapes(groups, count, width):
+    cols = sum(groups) * width
+    shapes = [((count, cols), F32), ((8, cols), F32)]
+    shapes += [((count, cols), BF16)] * 2 + [((count, 2 * cols), BF16)] * 2
+    shapes += [((x, width, width), F32) for x in groups for _ in range(2)]
+    return [jax.ShapeDtypeStruct(*x) for x in shapes]
+
+
+def opening(groups, most, lengths, strength, queries, keys, values, log_decay):
     count, total = queries.shape
     heads = strength.shape[0]
     width = total // heads
@@ -271,13 +320,13 @@
         jax.ShapeDtypeStruct((count, width), F32),
         jax.ShapeDtypeStruct((8, count), F32),
     ]
-    shapes = kept + span_shapes(count, width)
+    shapes = kept + span_shapes(groups, count, width)
     results = pl.pallas_call(
         functools.partial(opening_kernel, most),
         in_specs=[ANY] * len(given),
         out_specs=[VMEM] * len(shapes),
         out_shape=shapes,
-        scratch_shapes=[pltpu.SMEM(lengths.shape, lengths.dtype), pltpu.SemaphoreType.DMA((10,))],
+        scratch_shapes=[pltpu.SMEM(lengths.shape, lengths.dtype), pltpu.SemaphoreType.DMA((9,))],
         compiler_params=pltpu.CompilerParams(vmem_limit_bytes=32 << 20),
         cost_estimate=COST,
         name="opening",
@@ -285,37 +334,44 @@
     return results[: len(kept)], results[len(kept) :]
 
 
-def span_kernel(head, beta_ref, q_ref, k_ref, v_ref, g_ref, *refs):
-    span_heads(head, q_ref, k_ref, v_ref, beta_ref, g_ref, *refs[:4], refs[4:])
-
-
-def span(head, shared):
-    count = shared[1].shape[0]
-    width = shared[1].shape[1] // shared[0].shape[0]
-    shapes = span_shapes(count, width)
+def span_kernel(head, k_ref, v_ref, beta_ref, g_ref, strict_ref, flags_ref, *refs):
+    span_heads(head, k_ref, v_ref, beta_ref, g_ref, strict_ref, flags_ref, refs)
+
+
+def span(head, groups, shared, flags):
+    beta, queries, keys, values, decay, strict, _, _ = shared
+    count = keys.shape[0]
+    given = [keys, values, beta, decay, strict, flags]
+    shapes = span_shapes(groups, count, keys.shape[1] // beta.shape[0])
     return pl.pallas_call(
         functools.partial(span_kernel, head),
-        in_specs=[VMEM] * len(shared),
+        in_specs=[VMEM] * len(given),
         out_specs=[VMEM] * len(shapes),
         out_shape=shapes,
         compiler_params=pltpu.CompilerParams(vmem_limit_bytes=32 << 20),
         cost_estimate=COST,
         name="span",
-    )(*shared)
+    )(*given)
 
 
 def pass_kernel(own, low, late, flags_ref, state_ref, *refs):
     out_ref = refs[-1]
     width = out_ref.shape[1]
     before = flags_ref[2:3, :width]
+    kept = flags_ref[1:2, :width] > 0.0
     for h in range(out_ref.shape[0]):
-        trans_a, trans_b = refs[own][h], refs[own + 1][h]
-        for i in range(1, late):
-            here = before == low + i
-            trans_a = jnp.where(here, refs[own + 2 * i][h], trans_a)
-            trans_b = jnp.where(here, refs[own + 2 * i + 1][h], trans_b)
-        sent = trans_b + dot3(halves(trans_a), halves(state_ref[h]))
-        out_ref[h] = jnp.where(flags_ref[1:2, :width] > 0.0, sent, refs[0][h]) if own else sent
+        there = [i for i in range(late) if h < refs[own + 2 * i].shape[0]]
+        sent = None
+        if there:
+            trans_a, trans_b = refs[own + 2 * there[0]][h], refs[own + 2 * there[0] + 1][h]
+            for i in there[1:]:
+                here = before == low + i
+                trans_a = jnp.where(here, refs[own + 2 * i][h], trans_a)
+                trans_b = jnp.where(here, refs[own + 2 * i + 1][h], trans_b)
+            sent = trans_b + dot3(halves(trans_a), halves(state_ref[h]))
+        if own and h < refs[0].shape[0]:
+            sent = refs[0][h] if sent is None else jnp.where(kept, sent, refs[0][h])
+        out_ref[h] = sent
 
 
 def message(step, most, flags, trans_a, trans_b, received):
@@ -326,69 +382,79 @@
     low = next(i for i, x in enumerate(late) if x < len(trans_b))
     late = [x for x in late if 0 <= x < len(trans_b)]
     carried = [x for g in late for x in (trans_a[g], trans_b[g])]
+    size = max(x.shape[0] for x in own + carried)
     return pl.pallas_call(
         functools.partial(pass_kernel, len(own), low, len(late)),
         in_specs=[VMEM] * (2 + len(own) + len(carried)),
         out_specs=VMEM,
-        out_shape=jax.ShapeDtypeStruct(trans_b[0].shape, F32),
+        out_shape=jax.ShapeDtypeStruct((size, *trans_b[0].shape[1:]), F32),
         compiler_params=pltpu.CompilerParams(vmem_limit_bytes=8 << 20),
-        cost_estimate=COST,
+        cost_estimate=PASS,
         name="pass_on",
     )(flags, received[step - LAG], *own, *carried)
 
 
-def finish_kernel(head, most, spans, flags_ref, gain_ref, *refs):
-    mixed_ref = refs[-1]
-    outs, reach = refs[:spans], refs[spans : 2 * spans]
-    states = refs[2 * spans : -1]
-    group, width, _ = states[0].shape
+def finish_kernel(parts, most, flags_ref, gain_ref, *refs):
+    mixed_hbm, buffer, sems = refs[-3:]
+    width = refs[2].shape[1]
     before = flags_ref[2:3, :width]
-    for h in range(mixed_ref.shape[1] // width):
-        at = (head + h) % SPAN * width
-        here = slice(at, at + width)
-        state = states[h // group * most][h % group]
-        for i in range(1, most):
-            state = jnp.where(before == i, states[h // group * most + i][h % group], state)
-        of = h // SPAN
-        total = outs[of][:, here] + dot3(halves(reach[of][:, here]), halves(state))
-        scale = lax.rsqrt(jnp.mean(total * total, axis=-1, keepdims=True) + 1e-06)
-        gain = gain_ref[:, (head + h) * width : (head + h + 1) * width]
-        mixed_ref[:, h * width : (h + 1) * width] = (total * scale * gain).astype(BF16)
-
-
-def finish_first(*refs):
-    finish_kernel(*refs)
-
-
-def finish_next(head, most, spans, flags_ref, gain_ref, *refs):
-    finish_kernel(head, most, spans, flags_ref, gain_ref, *refs[:-2], refs[-1])
-
-
-def finished(head, mixed, flags, outs, reach, received, most, gain):
-    count = outs[0].shape[0]
+    copies, filled = [], 0
+    for n, (head, at, size) in enumerate(parts):
+        outs_ref, reach_ref, *states = refs[n * (most + 2) : (n + 1) * (most + 2)]
+        for h in range(size):
+            here = slice((at + h) * width, (at + h + 1) * width)
+            state = states[0][h]
+            for i in range(1, most):
+                state = jnp.where(before == i, states[i][h], state)
+            total = outs_ref[:, here] + dot3(halves(reach_ref[:, here]), halves(state))
+            scale = lax.rsqrt(jnp.mean(total * total, axis=-1, keepdims=True) + 1e-06)
+            there = slice((head + h) * width, (head + h + 1) * width)
+            place = slice((filled + h) * width, (filled + h + 1) * width)
+            buffer[:, place] = (total * scale * gain_ref[:, there]).astype(BF16)
+        there = slice(head * width, (head + size) * width)
+        place = slice(filled * width, (filled + size) * width)
+        copies.append(
+            pltpu.make_async_copy(buffer.at[:, place], mixed_hbm.at[:, there], sems.at[n])
+        )
+        copies[-1].start()
+        filled += size
+    for copy in copies:
+        copy.wait()
+
+
+def finished(chosen, places, mixed, flags, answers, received, most, gain):
+    count = answers[0][0].shape[0]
     width = received[0].shape[1]
-    low, high = head // SPAN, (head + FINISH - 1) // SPAN + 1
-    groups = range(head // GROUP, (head + FINISH) // GROUP)
-    states = [received[g + LAG * i] for g in groups for i in range(most)]
-    given = [flags, gain, *outs[low:high], *reach[low:high], *states]
+    given = [flags, gain]
+    for g in chosen:
+        given += [*answers[g], *(received[g + LAG * i] for i in range(most))]
     specs = [VMEM] * len(given)
     aliases = {}
+    parts = [places[g] for g in chosen]
+    kernel = functools.partial(finish_kernel, parts, most)
     if mixed is not None:
         aliases = {len(given): 0}
         given.append(mixed)
         specs.append(ANY)
-    kernel = finish_first if mixed is None else finish_next
+        kernel = functools.partial(finish_more, parts, most)
     return pl.pallas_call(
-        functools.partial(kernel, head, most, high - low),
-        grid=(1,),
+        kernel,
         in_specs=specs,
-        out_specs=pl.BlockSpec((count, FINISH * width), lambda i: (0, head // FINISH)),
+        out_specs=pl.BlockSpec(memory_space=pltpu.HBM),
         out_shape=jax.ShapeDtypeStruct((count, gain.shape[1]), BF16),
+        scratch_shapes=[
+            pltpu.VMEM((count, sum(x[2] for x in parts) * width), BF16),
+            pltpu.SemaphoreType.DMA((len(parts),)),
+        ],
         input_output_aliases=aliases,
-        compiler_params=pltpu.CompilerParams(vmem_limit_bytes=8 << 20),
-        cost_estimate=COST,
+        compiler_params=pltpu.CompilerParams(vmem_limit_bytes=16 << 20),
+        cost_estimate=END,
         name="finish",
     )(*given)
+
+
+def finish_more(parts, most, *refs):
+    finish_kernel(parts, most, *refs[:-4], *refs[-3:])
 
 
 def then(flags, results):
@@ -399,41 +465,45 @@
 def local(queries, keys, values, beta, log_decay, out_gain, doc_lengths):
     devices = lax.axis_size("ctx")
     ring = [(i, (i + 1) % devices) for i in range(devices)]
-    heads = beta.shape[1]
     most = devices // 2
-    shared, first = opening(most, doc_lengths, beta.T, queries, keys, values, log_decay)
+    gain = out_gain.reshape(1, -1)
+    sizes = [x for s in SPANS for x in s]
+    groups = len(sizes)
+    places, spans, head = [], [], 0
+    for n, span_groups in enumerate(SPANS):
+        for i, size in enumerate(span_groups):
+            places.append((head + sum(span_groups[:i]), sum(span_groups[:i]), size))
+            spans.append(n)
+        head += sum(span_groups)
+    shared, first = opening(SPANS[0], most, doc_lengths, beta.T, queries, keys, values, log_decay)
     shared, flags = shared[:-1], shared[-1]
     flags, first = then(flags, first)
-    outs, reach, trans_a, trans_b, received = [], [], [], [], []
+    found = [first]
+    trans_a, trans_b = first[6::2], first[7::2]
+    received = []
     mixed = None
-    gain = out_gain.reshape(1, -1)
-    groups = heads // GROUP
-    steps = groups + LAG * (most - 1)
-    head = SPAN
-
-    def keep(found):
-        outs.append(found[0])
-        reach.append(found[1])
-        trans_a.extend(found[2::2])
-        trans_b.extend(found[3::2])
-
-    keep(first)
-    ended = 0
-    for step in range(steps):
-        while head < heads and head < (step + 1 + AHEAD * (step >= LAG)) * GROUP:
-            flags, found = then(flags, span(head, [*shared, flags]))
-            keep(found)
-            head += SPAN
+    answers = []
+    starts = [sum(map(sum, SPANS[:n])) for n in range(len(SPANS))]
+    for step in range(groups + LAG * (most - 1)):
+        if step < groups and spans[step] == len(found):
+            flags, results = then(flags, span(places[step][0], SPANS[spans[step]], shared, flags))
+            found.append(results)
+            trans_a, trans_b = trans_a + results[6::2], trans_b + results[7::2]
         sent = message(step, most, flags, trans_a, trans_b, received)
         if step >= LAG:
             flags, (sent,) = then(flags, [sent])
         received.append(lax.ppermute(sent, "ctx", ring))
-        while head >= heads and ended + FINISH <= (step - 1 - LAG * (most - 1)) * GROUP:
-            mixed = finished(ended, mixed, flags, outs, reach, received, most, gain)
-            flags, (mixed,) = then(flags, [mixed])
-            ended += FINISH
-    for h in range(ended, heads, FINISH):
-        mixed = finished(h, mixed, flags, outs, reach, received, most, gain)
+        for _ in range(FILL[max(0, step - groups + 1)] if step >= groups - 1 else 0):
+            if len(answers) < len(found):
+                n = len(answers)
+                flags, results = then(flags, query(starts[n], shared, flags, found[n][:6]))
+                answers.append(results)
+    for n in range(len(answers), len(found)):
+        flags, results = then(flags, query(starts[n], shared, flags, found[n][:6]))
+        answers.append(results)
+    answers = [answers[n] for n in spans]
+    for chosen in (range(groups - LATE), *([g] for g in range(groups - LATE, groups))):
+        mixed = finished(chosen, places, mixed, flags, answers, received, most, gain)
     return mixed
 
 

time: 45.7 us -> 44.7 us (0.978)
  waiting for transfers between devices: 17.8 us -> 6.45 us
  starting transfers between devices: 6.48 us -> 13.4 us
  Pallas kernels: 21.2 us -> 24.3 us
    ppermute x6 -> x11, waiting for transfers between devices: 17.8 us -> 6.45 us  [local(): received.append(lax.ppermute(sent, 'ctx', ring))]
    ppermute x6 -> x11, starting transfers between devices: 6.48 us -> 13.4 us  [local(): received.append(lax.ppermute(sent, 'ctx', ring))]
    pallas_call x4 -> x8, Pallas kernels: 4.43 us -> 7.39 us  [the longest x5 3.88 us: query(): pl.pallas_call(functools.partial(query_kernel, head), in_specs=[VMEM] * l...]
    pallas_call x1, Pallas kernels: 4.9 us -> 3.65 us  [opening(): pl.pallas_call(functools.partial(opening_kernel, most), in_specs=[ANY] *...]
    pallas_call x3 -> x4, Pallas kernels: 10.8 us -> 11.6 us  [span(): pl.pallas_call(functools.partial(span_kernel, head), in_specs=[VMEM] * le...]
    pallas_call x4 -> x8, Pallas kernels: 1.05 us -> 1.61 us  [message(): pl.pallas_call(functools.partial(pass_kernel, len(own), low, len(late)),...]
  transfers between devices with their start and end apart: 6 -> 11, of which waited for: 6 -> 7; matrix products, arithmetic and copies ran while one was open for 0% -> 0% of each run, Pallas kernels for 33% -> 44%
where the time goes in v4:
time: 44.7 us; the launch traced here: 44.5 us
  Pallas kernels  24.3 us (54%)
  starting transfers between devices  13.4 us (30%)
  waiting for transfers between devices  6.45 us (14%)
    ppermute x11, starting transfers between devices, local(): received.append(lax.ppermute(sent, 'ctx', ring))  13.4 us
    pallas_call x4, Pallas kernels, span(): pl.pallas_call(functools.partial(span_kernel, head), in_specs=[VMEM] * le...  11.6 us
    ppermute x11, waiting for transfers between devices, local(): received.append(lax.ppermute(sent, 'ctx', ring))  6.45 us
    pallas_call x5, Pallas kernels, query(): pl.pallas_call(functools.partial(query_kernel, head), in_specs=[VMEM] * l...  3.88 us
    pallas_call x1, Pallas kernels, opening(): pl.pallas_call(functools.partial(opening_kernel, most), in_specs=[ANY] *...  3.65 us
    pallas_call x3, Pallas kernels, finished(): pl.pallas_call(kernel, in_specs=specs, out_specs=pl.BlockSpec(memory_spac...  3.51 us
    pallas_call x8, Pallas kernels, message(): pl.pallas_call(functools.partial(pass_kernel, len(own), low, len(late)),...  1.61 us
  transfers between devices with their start and end apart: 11, of which 7 were waited for; matrix products, arithmetic and copies ran while one was open for 0% of the time, Pallas kernels for 44%

profile of v4, /device:TPU:0, one launch (start us, length us, event | category | flops | bytes accessed | tf_op | source)
XLA Modules:
  0.0 44.5 jit_solution(9893933294968976041)
XLA Ops:
  0.0 3.7 %opening.1 = (f32[16,192]{1,0:T(8,128)S(1)}, bf16[192,2048]{1,0:T(8,128)(2,1)S(1)}, bf16[192,2048]{1,0:T(8,128)(2,1)S(1)}, bf16[192,2048]{1,0:T(8,128)(2,1)S(1)}...) custom-call(s32[16]{0:T(128)} %refs_0_.1, ...), custom_call_target="tpu_custom_call" | custom-call | flops 100000000 | bytes 1 | tf_op jit(solution)/shard_map/opening/pallas_call | solution.py:324
  3.7 3.1 %collective-permute-start = (f32[2,128,128]{2,1,0:T(8,128)S(1)}, f32[2,128,128]{2,1,0:T(8,128)S(1)}, u32[]{:S(2)}, u32[]{:S(2)}) collective-permute-start(f32[2,128,128]{2,1,0:T(8,128)S(1)} %get-tuple-element.189.refs_2_), channel_id=1, source_target_pairs={{0,1},{1,2},{2,3},{3,0},{4,5},{5,6},{6,7},{7,4},{8,9},{9,10},{10,1... | collective-permute-start | bytes 393224 | tf_op jit(solution)/shard_map/ppermute | solution.py:495
  6.7 3.0 %span.4 = (f32[192,512]{1,0:T(8,128)S(1)}, f32[8,512]{1,0:T(8,128)S(1)}, bf16[192,512]{1,0:T(8,128)(2,1)S(1)}, bf16[192,512]{1,0:T(8,128)(2,1)S(1)}, bf16[192,10...) custom-call(bf16[192,2048]{1,0:T(8,128)(2,1)S(1)} %get-tuple-element, ...), custom_call_target="tpu_custom_call" | custom-call | flops 100000000 | bytes 1 | tf_op jit(solution)/shard_map/span/pallas_call | solution.py:346
  9.8 1.6 %collective-permute-start.1 = (f32[2,128,128]{2,1,0:T(8,128)S(1)}, f32[2,128,128]{2,1,0:T(8,128)S(1)}, u32[]{:S(2)}, u32[]{:S(2)}) collective-permute-start(f32[2,128,128]{2,1,0:T(8,128)S(1)} %get-tuple-element.193.refs_2_), channel_id=1, source_target_pairs={{0,1},{1,2},{2,3},{3,0},{4,5},{5,6},{6,7},{7,4},{8,9},{9,10},{10,1... | collective-permute-start | bytes 393224 | tf_op jit(solution)/shard_map/ppermute | solution.py:495
  11.4 1.6 %collective-permute-start.2 = (f32[2,128,128]{2,1,0:T(8,128)S(1)}, f32[2,128,128]{2,1,0:T(8,128)S(1)}, u32[]{:S(2)}, u32[]{:S(2)}) collective-permute-start(f32[2,128,128]{2,1,0:T(8,128)S(1)} %get-tuple-element.208.refs_2_), channel_id=1, source_target_pairs={{0,1},{1,2},{2,3},{3,0},{4,5},{5,6},{6,7},{7,4},{8,9},{9,10},{10,1... | collective-permute-start | bytes 393224 | tf_op jit(solution)/shard_map/ppermute | solution.py:495
  13.0 3.0 %span.5 = (f32[192,512]{1,0:T(8,128)S(1)}, f32[8,512]{1,0:T(8,128)S(1)}, bf16[192,512]{1,0:T(8,128)(2,1)S(1)}, bf16[192,512]{1,0:T(8,128)(2,1)S(1)}, bf16[192,10...) custom-call(bf16[192,2048]{1,0:T(8,128)(2,1)S(1)} %get-tuple-element, ...), custom_call_target="tpu_custom_call" | custom-call | flops 100000000 | bytes 1 | tf_op jit(solution)/shard_map/span/pallas_call | solution.py:346
  16.4 1.6 %collective-permute-done.1.state_ref.refs_6_ = f32[2,128,128]{2,1,0:T(8,128)S(1)} collective-permute-done((f32[2,128,128]{2,1,0:T(8,128)S(1)}, f32[2,128,128]{2,1,0:T(8,128)S(1)}, u32[]{:S(2)}, u32[]{:S(2)}) %collective-permute-start.1) | collective-permute-done | bytes 131104 | tf_op jit(solution)/shard_map/ppermute | solution.py:495
  18.4 3.0 %span.6 = (f32[192,512]{1,0:T(8,128)S(1)}, f32[8,512]{1,0:T(8,128)S(1)}, bf16[192,512]{1,0:T(8,128)(2,1)S(1)}, bf16[192,512]{1,0:T(8,128)(2,1)S(1)}, bf16[192,10...) custom-call(bf16[192,2048]{1,0:T(8,128)(2,1)S(1)} %get-tuple-element, ...), custom_call_target="tpu_custom_call" | custom-call | flops 100000000 | bytes 1 | tf_op jit(solution)/shard_map/span/pallas_call | solution.py:346
  21.6 1.6 %collective-permute-start.5 = (f32[2,128,128]{2,1,0:T(8,128)S(1)}, f32[2,128,128]{2,1,0:T(8,128)S(1)}, u32[]{:S(2)}, u32[]{:S(2)}) collective-permute-start(f32[2,128,128]{2,1,0:T(8,128)S(1)} %pass_on.10), channel_id=1, source_target_pairs={{0,1},{1,2},{2,3},{3,0},{4,5},{5,6},{6,7},{7,4},{8,9},{9,10},{10,1... | collective-permute-start | bytes 393224 | tf_op jit(solution)/shard_map/ppermute | solution.py:495
  23.2 0.6 %collective-permute-done.3.state_ref.refs_3_.refs_14_ = f32[2,128,128]{2,1,0:T(8,128)S(1)} collective-permute-done((f32[2,128,128]{2,1,0:T(8,128)S(1)}, f32[2,128,128]{2,1,0:T(8,128)S(1)}, u32[]{:S(2)}, u32[]{:S(2)}) %collective-permute-start.3) | collective-permute-done | bytes 131104 | tf_op jit(solution)/shard_map/ppermute | solution.py:495
  24.1 1.2 %collective-permute-start.6 = (f32[2,128,128]{2,1,0:T(8,128)S(1)}, f32[2,128,128]{2,1,0:T(8,128)S(1)}, u32[]{:S(2)}, u32[]{:S(2)}) collective-permute-start(f32[2,128,128]{2,1,0:T(8,128)S(1)} %pass_on.11), channel_id=1, source_target_pairs={{0,1},{1,2},{2,3},{3,0},{4,5},{5,6},{6,7},{7,4},{8,9},{9,10},{10,1... | collective-permute-start | bytes 393224 | tf_op jit(solution)/shard_map/ppermute | solution.py:495
  25.3 2.5 %span.7 = (f32[192,256]{1,0:T(8,128)S(1)}, f32[8,256]{1,0:T(8,128)S(1)}, bf16[192,256]{1,0:T(8,128)(2,1)S(1)}, bf16[192,256]{1,0:T(8,128)(2,1)S(1)}, bf16[192,51...) custom-call(bf16[192,2048]{1,0:T(8,128)(2,1)S(1)} %get-tuple-element., ...), custom_call_target="tpu_custom_call" | custom-call | flops 100000000 | bytes 1 | tf_op jit(solution)/shard_map/span/pallas_call | solution.py:346
  28.0 1.7 %collective-permute-start.7 = (f32[2,128,128]{2,1,0:T(8,128)S(1)}, f32[2,128,128]{2,1,0:T(8,128)S(1)}, u32[]{:S(2)}, u32[]{:S(2)}) collective-permute-start(f32[2,128,128]{2,1,0:T(8,128)S(1)} %pass_on.12), channel_id=1, source_target_pairs={{0,1},{1,2},{2,3},{3,0},{4,5},{5,6},{6,7},{7,4},{8,9},{9,10},{10,1... | collective-permute-start | bytes 393224 | tf_op jit(solution)/shard_map/ppermute | solution.py:495
  30.8 0.9 %query.6 = (f32[192,512]{1,0:T(8,128)S(1)}, f32[192,512]{1,0:T(8,128)S(1)}) custom-call(bf16[192,2048]{1,0:T(8,128)(2,1)S(1)} %get-tuple-element.229.q_ref, f32[16,192]{1,0:T(8,128)S(1)} %get-tuple-element.164.beta_ref, f32[192,192]{1,0:T(8,128)S(1)} %get-tuple-element.230.lower_ref, f32[192,128]{1,0:T(8,128)S(1)} %get-tuple-element.231.fresh_ref, ...), custom_call_target="tpu_custom_call" | custom-call | flops 100000000 | bytes 1 | tf_op jit(solution)/shard_map/query/pallas_call | solution.py:260
  32.1 2.1 %collective-permute-start.9 = (f32[2,128,128]{2,1,0:T(8,128)S(1)}, f32[2,128,128]{2,1,0:T(8,128)S(1)}, u32[]{:S(2)}, u32[]{:S(2)}) collective-permute-start(f32[2,128,128]{2,1,0:T(8,128)S(1)} %pass_on.14), channel_id=1, source_target_pairs={{0,1},{1,2},{2,3},{3,0},{4,5},{5,6},{6,7},{7,4},{8,9},{9,10},{10,1... | collective-permute-start | bytes 393224 | tf_op jit(solution)/shard_map/ppermute | solution.py:495
  34.2 0.9 %query.7 = (f32[192,512]{1,0:T(8,128)S(1)}, f32[192,512]{1,0:T(8,128)S(1)}) custom-call(bf16[192,2048]{1,0:T(8,128)(2,1)S(1)} %get-tuple-element.229.q_ref, f32[16,192]{1,0:T(8,128)S(1)} %get-tuple-element.164.beta_ref, f32[192,192]{1,0:T(8,128)S(1)} %get-tuple-element.230.lower_ref, f32[192,128]{1,0:T(8,128)S(1)} %get-tuple-element.231.fresh_ref, ...), custom_call_target="tpu_custom_call" | custom-call | flops 100000000 | bytes 1 | tf_op jit(solution)/shard_map/query/pallas_call | solution.py:260
  35.0 1.3 %collective-permute-done.7.state_ref.refs_19_.refs_4_ = f32[2,128,128]{2,1,0:T(8,128)S(1)} collective-permute-done((f32[2,128,128]{2,1,0:T(8,128)S(1)}, f32[2,128,128]{2,1,0:T(8,128)S(1)}, u32[]{:S(2)}, u32[]{:S(2)}) %collective-permute-start.7) | collective-permute-done | bytes 131104 | tf_op jit(solution)/shard_map/ppermute | solution.py:495
  36.6 0.9 %query.8 = (f32[192,512]{1,0:T(8,128)S(1)}, f32[192,512]{1,0:T(8,128)S(1)}) custom-call(bf16[192,2048]{1,0:T(8,128)(2,1)S(1)} %get-tuple-element.229.q_ref, f32[16,192]{1,0:T(8,128)S(1)} %get-tuple-element.164.beta_ref, f32[192,192]{1,0:T(8,128)S(1)} %get-tuple-element.230.lower_ref, f32[192,128]{1,0:T(8,128)S(1)} %get-tuple-element.231.fresh_ref, ...), custom_call_target="tpu_custom_call" | custom-call | flops 100000000 | bytes 1 | tf_op jit(solution)/shard_map/query/pallas_call | solution.py:260
  37.5 0.6 %query.9 = (f32[192,256]{1,0:T(8,128)S(1)}, f32[192,256]{1,0:T(8,128)S(1)}) custom-call(bf16[192,2048]{1,0:T(8,128)(2,1)S(1)} %get-tuple-element.229.q_ref, f32[16,192]{1,0:T(8,128)S(1)} %get-tuple-element.164.beta_ref, f32[192,192]{1,0:T(8,128)S(1)} %get-tuple-element.230.lower_ref, f32[192,128]{1,0:T(8,128)S(1)} %get-tuple-element.231.fresh_ref, ...), custom_call_target="tpu_custom_call" | custom-call | flops 100000000 | bytes 1 | tf_op jit(solution)/shard_map/query/pallas_call | solution.py:260
  38.1 1.0 %collective-permute-done.10.refs_23_ = f32[2,128,128]{2,1,0:T(8,128)S(1)} collective-permute-done((f32[2,128,128]{2,1,0:T(8,128)S(1)}, f32[2,128,128]{2,1,0:T(8,128)S(1)}, u32[]{:S(2)}, u32[]{:S(2)}) %collective-permute-start.10) | collective-permute-done | bytes 131104 | tf_op jit(solution)/shard_map/ppermute | solution.py:495
  39.1 1.5 %finish.3.refs_6_ = bf16[192,2048]{1,0:T(8,128)(2,1)} custom-call(f32[8,192]{1,0:T(8,128)S(1)} %get-tuple-element.285.flags_ref.refs_0_, f32[1,2048]{1,0:T(1,128)S(1)} %bitcast.2, f32[192,256]{1,0:T(8,128)S(1)} %get-tuple-element.292.refs_0_, f32[192,256]{1,0:T(8,128)S(1)} %get-tuple-element.293.refs_1_, ...), custom_call_target="tpu_custom_call" | custom-call | flops 100000000 | bytes 1 | tf_op jit(solution)/shard_map/finish/pallas_call | solution.py:440
  40.9 1.0 %finish.4.refs_6_ = bf16[192,2048]{1,0:T(8,128)(2,1)} custom-call(f32[8,192]{1,0:T(8,128)S(1)} %get-tuple-element.285.flags_ref.refs_0_, f32[1,2048]{1,0:T(1,128)S(1)} %bitcast.3, f32[192,512]{1,0:T(8,128)S(1)} %get-tuple-element.289.refs_20_.refs_2_, f32[192,512]{1,0:T(8,128)S(1)} %get-tuple-element.290.refs_21_.refs_3_, ...), custom_call_target="tpu_custom_call", output_to_operand_aliasing={{}: (6, {})} | custom-call | flops 100000000 | bytes 1 | tf_op jit(solution)/shard_map/finish/pallas_call | solution.py:440
  41.9 1.4 %collective-permute-done.8.refs_5_ = f32[2,128,128]{2,1,0:T(8,128)S(1)} collective-permute-done((f32[2,128,128]{2,1,0:T(8,128)S(1)}, f32[2,128,128]{2,1,0:T(8,128)S(1)}, u32[]{:S(2)}, u32[]{:S(2)}) %collective-permute-start.8) | collective-permute-done | bytes 131104 | tf_op jit(solution)/shard_map/ppermute | solution.py:495
  43.4 1.0 %finish.5 = bf16[192,2048]{1,0:T(8,128)(2,1)} custom-call(f32[8,192]{1,0:T(8,128)S(1)} %get-tuple-element.285.flags_ref.refs_0_, f32[1,2048]{1,0:T(1,128)S(1)} %bitcast.4, f32[192,256]{1,0:T(8,128)S(1)} %get-tuple-element.286.refs_2_, f32[192,256]{1,0:T(8,128)S(1)} %get-tuple-element.287.refs_3_, ...), custom_call_target="tpu_custom_call", output_to_operand_aliasing={{}: (6, {})} | custom-call | flops 100000000 | bytes 1 | tf_op jit(solution)/shard_map/finish/pallas_call | solution.py:440
  (21 shorter events, 3.2 us)
Async XLA Ops:
  3.7 12.4 %collective-permute-start = (f32[2,128,128]{2,1,0:T(8,128)S(1)}, f32[2,128,128]{2,1,0:T(8,128)S(1)}, u32[]{:S(2)}, u32[]{:S(2)}) collective-permute-start(f32[2,128,128]{2,1,0:T(8,128)S(1)} %get-tuple-element.189.refs_2_), channel_id=1, source_target_pairs={{0,1},{1,2},{2,3},{3,0},{4,5},{5,6},{6,7},{7,4},{8,9},{9,10},{10,1... | collective-permute-start | bytes 393224 | tf_op jit(solution)/shard_map/ppermute | solution.py:495
  9.8 8.2 %collective-permute-start.1 = (f32[2,128,128]{2,1,0:T(8,128)S(1)}, f32[2,128,128]{2,1,0:T(8,128)S(1)}, u32[]{:S(2)}, u32[]{:S(2)}) collective-permute-start(f32[2,128,128]{2,1,0:T(8,128)S(1)} %get-tuple-element.193.refs_2_), channel_id=1, source_target_pairs={{0,1},{1,2},{2,3},{3,0},{4,5},{5,6},{6,7},{7,4},{8,9},{9,10},{10,1... | collective-permute-start | bytes 393224 | tf_op jit(solution)/shard_map/ppermute | solution.py:495
  11.4 10.0 %collective-permute-start.2 = (f32[2,128,128]{2,1,0:T(8,128)S(1)}, f32[2,128,128]{2,1,0:T(8,128)S(1)}, u32[]{:S(2)}, u32[]{:S(2)}) collective-permute-start(f32[2,128,128]{2,1,0:T(8,128)S(1)} %get-tuple-element.208.refs_2_), channel_id=1, source_target_pairs={{0,1},{1,2},{2,3},{3,0},{4,5},{5,6},{6,7},{7,4},{8,9},{9,10},{10,1... | collective-permute-start | bytes 393224 | tf_op jit(solution)/shard_map/ppermute | solution.py:495
  16.2 7.6 %collective-permute-start.3 = (f32[2,128,128]{2,1,0:T(8,128)S(1)}, f32[2,128,128]{2,1,0:T(8,128)S(1)}, u32[]{:S(2)}, u32[]{:S(2)}) collective-permute-start(f32[2,128,128]{2,1,0:T(8,128)S(1)} %pass_on.8), channel_id=1, source_target_pairs={{0,1},{1,2},{2,3},{3,0},{4,5},{5,6},{6,7},{7,4},{8,9},{9,10},{10,1... | collective-permute-start | bytes 393224 | tf_op jit(solution)/shard_map/ppermute | solution.py:495
  18.2 9.6 %collective-permute-start.4 = (f32[2,128,128]{2,1,0:T(8,128)S(1)}, f32[2,128,128]{2,1,0:T(8,128)S(1)}, u32[]{:S(2)}, u32[]{:S(2)}) collective-permute-start(f32[2,128,128]{2,1,0:T(8,128)S(1)} %pass_on.9), channel_id=1, source_target_pairs={{0,1},{1,2},{2,3},{3,0},{4,5},{5,6},{6,7},{7,4},{8,9},{9,10},{10,1... | collective-permute-start | bytes 393224 | tf_op jit(solution)/shard_map/ppermute | solution.py:495
  21.6 8.8 %collective-permute-start.5 = (f32[2,128,128]{2,1,0:T(8,128)S(1)}, f32[2,128,128]{2,1,0:T(8,128)S(1)}, u32[]{:S(2)}, u32[]{:S(2)}) collective-permute-start(f32[2,128,128]{2,1,0:T(8,128)S(1)} %pass_on.10), channel_id=1, source_target_pairs={{0,1},{1,2},{2,3},{3,0},{4,5},{5,6},{6,7},{7,4},{8,9},{9,10},{10,1... | collective-permute-start | bytes 393224 | tf_op jit(solution)/shard_map/ppermute | solution.py:495
  24.1 7.8 %collective-permute-start.6 = (f32[2,128,128]{2,1,0:T(8,128)S(1)}, f32[2,128,128]{2,1,0:T(8,128)S(1)}, u32[]{:S(2)}, u32[]{:S(2)}) collective-permute-start(f32[2,128,128]{2,1,0:T(8,128)S(1)} %pass_on.11), channel_id=1, source_target_pairs={{0,1},{1,2},{2,3},{3,0},{4,5},{5,6},{6,7},{7,4},{8,9},{9,10},{10,1... | collective-permute-start | bytes 393224 | tf_op jit(solution)/shard_map/ppermute | solution.py:495
  28.0 8.3 %collective-permute-start.7 = (f32[2,128,128]{2,1,0:T(8,128)S(1)}, f32[2,128,128]{2,1,0:T(8,128)S(1)}, u32[]{:S(2)}, u32[]{:S(2)}) collective-permute-start(f32[2,128,128]{2,1,0:T(8,128)S(1)} %pass_on.12), channel_id=1, source_target_pairs={{0,1},{1,2},{2,3},{3,0},{4,5},{5,6},{6,7},{7,4},{8,9},{9,10},{10,1... | collective-permute-start | bytes 393224 | tf_op jit(solution)/shard_map/ppermute | solution.py:495
  30.7 8.5 %collective-permute-start.10 = (f32[2,128,128]{2,1,0:T(8,128)S(1)}, f32[2,128,128]{2,1,0:T(8,128)S(1)}, u32[]{:S(2)}, u32[]{:S(2)}) collective-permute-start(f32[2,128,128]{2,1,0:T(8,128)S(1)} %pass_on.13), channel_id=1, source_target_pairs={{0,1},{1,2},{2,3},{3,0},{4,5},{5,6},{6,7},{7,4},{8,9},{9,10},{10,1... | collective-permute-start | bytes 393224 | tf_op jit(solution)/shard_map/ppermute | solution.py:495
  32.1 8.8 %collective-permute-start.9 = (f32[2,128,128]{2,1,0:T(8,128)S(1)}, f32[2,128,128]{2,1,0:T(8,128)S(1)}, u32[]{:S(2)}, u32[]{:S(2)}) collective-permute-start(f32[2,128,128]{2,1,0:T(8,128)S(1)} %pass_on.14), channel_id=1, source_target_pairs={{0,1},{1,2},{2,3},{3,0},{4,5},{5,6},{6,7},{7,4},{8,9},{9,10},{10,1... | collective-permute-start | bytes 393224 | tf_op jit(solution)/shard_map/ppermute | solution.py:495
  36.5 6.8 %collective-permute-start.8 = (f32[2,128,128]{2,1,0:T(8,128)S(1)}, f32[2,128,128]{2,1,0:T(8,128)S(1)}, u32[]{:S(2)}, u32[]{:S(2)}) collective-permute-start(f32[2,128,128]{2,1,0:T(8,128)S(1)} %pass_on.15), channel_id=1, source_target_pairs={{0,1},{1,2},{2,3},{3,0},{4,5},{5,6},{6,7},{7,4},{8,9},{9,10},{10,1... | collective-permute-start | bytes 393224 | tf_op jit(solution)/shard_map/ppermute | solution.py:495
  37.5 1.7 %copy-start = (f32[2048]{0:T(1024)S(1)}, f32[2048]{0:T(1024)}, u32[]{:S(2)}) copy-start(f32[2048]{0:T(1024)} %param.12) | copy-start | bytes 24580

commit v5 on v4

--- a/solution.py
+++ b/solution.py
@@ -31,7 +31,9 @@
 
 
 def dot3(a, b, dims=((1,), (0,))):
-    return dot(a[0], b[0], dims) + (dot(a[0], b[1], dims) + dot(a[1], b[0], dims))
+    rows = a[0].shape[0]
+    both = dot(jnp.concatenate(a, axis=0), b[0], dims)
+    return both[:rows] + (dot(a[0], b[1], dims) + both[rows:])
 
 
 def rows_of(pair, low, high):

time: 44.7 us -> 44.1 us (0.987)
  starting transfers between devices: 13.4 us -> 12.8 us
  waiting for transfers between devices: 6.45 us -> 6.98 us
  Pallas kernels: 24.3 us -> 23.8 us
    ppermute x11, starting transfers between devices: 13.4 us -> 12.8 us  [local(): received.append(lax.ppermute(sent, 'ctx', ring))]
    ppermute x11, waiting for transfers between devices: 6.45 us -> 6.98 us  [local(): received.append(lax.ppermute(sent, 'ctx', ring))]
where the time goes in v5:
time: 44.1 us; the launch traced here: 44 us
  Pallas kernels  23.8 us (54%)
  starting transfers between devices  12.8 us (29%)
  waiting for transfers between devices  6.98 us (16%)
    ppermute x11, starting transfers between devices, local(): received.append(lax.ppermute(sent, 'ctx', ring))  12.8 us
    pallas_call x4, Pallas kernels, span(): pl.pallas_call(functools.partial(span_kernel, head), in_specs=[VMEM] * le...  11.2 us
    ppermute x11, waiting for transfers between devices, local(): received.append(lax.ppermute(sent, 'ctx', ring))  6.98 us
    pallas_call x5, Pallas kernels, query(): pl.pallas_call(functools.partial(query_kernel, head), in_specs=[VMEM] * l...  3.93 us
    pallas_call x1, Pallas kernels, opening(): pl.pallas_call(functools.partial(opening_kernel, most), in_specs=[ANY] *...  3.54 us
    pallas_call x3, Pallas kernels, finished(): pl.pallas_call(kernel, in_specs=specs, out_specs=pl.BlockSpec(memory_spac...  3.48 us
    pallas_call x8, Pallas kernels, message(): pl.pallas_call(functools.partial(pass_kernel, len(own), low, len(late)),...  1.6 us
  transfers between devices with their start and end apart: 11, of which 7 were waited for; matrix products, arithmetic and copies ran while one was open for 0% of the time, Pallas kernels for 44%

profile of v5, /device:TPU:0, one launch (start us, length us, event | category | flops | bytes accessed | tf_op | source)
XLA Modules:
  0.0 44.0 jit_solution(10128965261862933791)
XLA Ops:
  0.0 3.5 %opening.1 = (f32[16,192]{1,0:T(8,128)S(1)}, bf16[192,2048]{1,0:T(8,128)(2,1)S(1)}, bf16[192,2048]{1,0:T(8,128)(2,1)S(1)}, bf16[192,2048]{1,0:T(8,128)(2,1)S(1)}...) custom-call(s32[16]{0:T(128)} %refs_0_.1, ...), custom_call_target="tpu_custom_call" | custom-call | flops 100000000 | bytes 1 | tf_op jit(solution)/shard_map/opening/pallas_call | solution.py:326
  3.5 3.1 %collective-permute-start = (f32[2,128,128]{2,1,0:T(8,128)S(1)}, f32[2,128,128]{2,1,0:T(8,128)S(1)}, u32[]{:S(2)}, u32[]{:S(2)}) collective-permute-start(f32[2,128,128]{2,1,0:T(8,128)S(1)} %get-tuple-element.189.refs_2_), channel_id=1, source_target_pairs={{0,1},{1,2},{2,3},{3,0},{4,5},{5,6},{6,7},{7,4},{8,9},{9,10},{10,1... | collective-permute-start | bytes 393224 | tf_op jit(solution)/shard_map/ppermute | solution.py:497
  6.6 2.9 %span.4 = (f32[192,512]{1,0:T(8,128)S(1)}, f32[8,512]{1,0:T(8,128)S(1)}, bf16[192,512]{1,0:T(8,128)(2,1)S(1)}, bf16[192,512]{1,0:T(8,128)(2,1)S(1)}, bf16[192,10...) custom-call(bf16[192,2048]{1,0:T(8,128)(2,1)S(1)} %get-tuple-element, ...), custom_call_target="tpu_custom_call" | custom-call | flops 100000000 | bytes 1 | tf_op jit(solution)/shard_map/span/pallas_call | solution.py:348
  9.6 1.6 %collective-permute-start.1 = (f32[2,128,128]{2,1,0:T(8,128)S(1)}, f32[2,128,128]{2,1,0:T(8,128)S(1)}, u32[]{:S(2)}, u32[]{:S(2)}) collective-permute-start(f32[2,128,128]{2,1,0:T(8,128)S(1)} %get-tuple-element.193.refs_2_), channel_id=1, source_target_pairs={{0,1},{1,2},{2,3},{3,0},{4,5},{5,6},{6,7},{7,4},{8,9},{9,10},{10,1... | collective-permute-start | bytes 393224 | tf_op jit(solution)/shard_map/ppermute | solution.py:497
  11.2 1.6 %collective-permute-start.2 = (f32[2,128,128]{2,1,0:T(8,128)S(1)}, f32[2,128,128]{2,1,0:T(8,128)S(1)}, u32[]{:S(2)}, u32[]{:S(2)}) collective-permute-start(f32[2,128,128]{2,1,0:T(8,128)S(1)} %get-tuple-element.208.refs_2_), channel_id=1, source_target_pairs={{0,1},{1,2},{2,3},{3,0},{4,5},{5,6},{6,7},{7,4},{8,9},{9,10},{10,1... | collective-permute-start | bytes 393224 | tf_op jit(solution)/shard_map/ppermute | solution.py:497
  12.8 2.9 %span.5 = (f32[192,512]{1,0:T(8,128)S(1)}, f32[8,512]{1,0:T(8,128)S(1)}, bf16[192,512]{1,0:T(8,128)(2,1)S(1)}, bf16[192,512]{1,0:T(8,128)(2,1)S(1)}, bf16[192,10...) custom-call(bf16[192,2048]{1,0:T(8,128)(2,1)S(1)} %get-tuple-element, ...), custom_call_target="tpu_custom_call" | custom-call | flops 100000000 | bytes 1 | tf_op jit(solution)/shard_map/span/pallas_call | solution.py:348
  16.0 1.7 %collective-permute-done.1.state_ref.refs_6_ = f32[2,128,128]{2,1,0:T(8,128)S(1)} collective-permute-done((f32[2,128,128]{2,1,0:T(8,128)S(1)}, f32[2,128,128]{2,1,0:T(8,128)S(1)}, u32[]{:S(2)}, u32[]{:S(2)}) %collective-permute-start.1) | collective-permute-done | bytes 131104 | tf_op jit(solution)/shard_map/ppermute | solution.py:497
  18.0 2.9 %span.6 = (f32[192,512]{1,0:T(8,128)S(1)}, f32[8,512]{1,0:T(8,128)S(1)}, bf16[192,512]{1,0:T(8,128)(2,1)S(1)}, bf16[192,512]{1,0:T(8,128)(2,1)S(1)}, bf16[192,10...) custom-call(bf16[192,2048]{1,0:T(8,128)(2,1)S(1)} %get-tuple-element, ...), custom_call_target="tpu_custom_call" | custom-call | flops 100000000 | bytes 1 | tf_op jit(solution)/shard_map/span/pallas_call | solution.py:348
  21.2 1.6 %collective-permute-start.5 = (f32[2,128,128]{2,1,0:T(8,128)S(1)}, f32[2,128,128]{2,1,0:T(8,128)S(1)}, u32[]{:S(2)}, u32[]{:S(2)}) collective-permute-start(f32[2,128,128]{2,1,0:T(8,128)S(1)} %pass_on.10), channel_id=1, source_target_pairs={{0,1},{1,2},{2,3},{3,0},{4,5},{5,6},{6,7},{7,4},{8,9},{9,10},{10,1... | collective-permute-start | bytes 393224 | tf_op jit(solution)/shard_map/ppermute | solution.py:497
  22.8 0.7 %collective-permute-done.3.state_ref.refs_3_.refs_14_ = f32[2,128,128]{2,1,0:T(8,128)S(1)} collective-permute-done((f32[2,128,128]{2,1,0:T(8,128)S(1)}, f32[2,128,128]{2,1,0:T(8,128)S(1)}, u32[]{:S(2)}, u32[]{:S(2)}) %collective-permute-start.3) | collective-permute-done | bytes 131104 | tf_op jit(solution)/shard_map/ppermute | solution.py:497
  23.8 1.1 %collective-permute-start.6 = (f32[2,128,128]{2,1,0:T(8,128)S(1)}, f32[2,128,128]{2,1,0:T(8,128)S(1)}, u32[]{:S(2)}, u32[]{:S(2)}) collective-permute-start(f32[2,128,128]{2,1,0:T(8,128)S(1)} %pass_on.11), channel_id=1, source_target_pairs={{0,1},{1,2},{2,3},{3,0},{4,5},{5,6},{6,7},{7,4},{8,9},{9,10},{10,1... | collective-permute-start | bytes 393224 | tf_op jit(solution)/shard_map/ppermute | solution.py:497
  24.8 2.4 %span.7 = (f32[192,256]{1,0:T(8,128)S(1)}, f32[8,256]{1,0:T(8,128)S(1)}, bf16[192,256]{1,0:T(8,128)(2,1)S(1)}, bf16[192,256]{1,0:T(8,128)(2,1)S(1)}, bf16[192,51...) custom-call(bf16[192,2048]{1,0:T(8,128)(2,1)S(1)} %get-tuple-element., ...), custom_call_target="tpu_custom_call" | custom-call | flops 100000000 | bytes 1 | tf_op jit(solution)/shard_map/span/pallas_call | solution.py:348
  27.5 1.8 %collective-permute-start.7 = (f32[2,128,128]{2,1,0:T(8,128)S(1)}, f32[2,128,128]{2,1,0:T(8,128)S(1)}, u32[]{:S(2)}, u32[]{:S(2)}) collective-permute-start(f32[2,128,128]{2,1,0:T(8,128)S(1)} %pass_on.12), channel_id=1, source_target_pairs={{0,1},{1,2},{2,3},{3,0},{4,5},{5,6},{6,7},{7,4},{8,9},{9,10},{10,1... | collective-permute-start | bytes 393224 | tf_op jit(solution)/shard_map/ppermute | solution.py:497
  30.3 0.9 %query.6 = (f32[192,512]{1,0:T(8,128)S(1)}, f32[192,512]{1,0:T(8,128)S(1)}) custom-call(bf16[192,2048]{1,0:T(8,128)(2,1)S(1)} %get-tuple-element.229.q_ref, f32[16,192]{1,0:T(8,128)S(1)} %get-tuple-element.164.beta_ref, f32[192,192]{1,0:T(8,128)S(1)} %get-tuple-element.230.lower_ref, f32[192,128]{1,0:T(8,128)S(1)} %get-tuple-element.231.fresh_ref, ...), custom_call_target="tpu_custom_call" | custom-call | flops 100000000 | bytes 1 | tf_op jit(solution)/shard_map/query/pallas_call | solution.py:262
  31.2 0.7 %collective-permute-done.6.state_ref.refs_15_.refs_4_ = f32[2,128,128]{2,1,0:T(8,128)S(1)} collective-permute-done((f32[2,128,128]{2,1,0:T(8,128)S(1)}, f32[2,128,128]{2,1,0:T(8,128)S(1)}, u32[]{:S(2)}, u32[]{:S(2)}) %collective-permute-start.6) | collective-permute-done | bytes 131104 | tf_op jit(solution)/shard_map/ppermute | solution.py:497
  32.0 1.7 %collective-permute-start.9 = (f32[2,128,128]{2,1,0:T(8,128)S(1)}, f32[2,128,128]{2,1,0:T(8,128)S(1)}, u32[]{:S(2)}, u32[]{:S(2)}) collective-permute-start(f32[2,128,128]{2,1,0:T(8,128)S(1)} %pass_on.14), channel_id=1, source_target_pairs={{0,1},{1,2},{2,3},{3,0},{4,5},{5,6},{6,7},{7,4},{8,9},{9,10},{10,1... | collective-permute-start | bytes 393224 | tf_op jit(solution)/shard_map/ppermute | solution.py:497
  33.7 0.9 %query.7 = (f32[192,512]{1,0:T(8,128)S(1)}, f32[192,512]{1,0:T(8,128)S(1)}) custom-call(bf16[192,2048]{1,0:T(8,128)(2,1)S(1)} %get-tuple-element.229.q_ref, f32[16,192]{1,0:T(8,128)S(1)} %get-tuple-element.164.beta_ref, f32[192,192]{1,0:T(8,128)S(1)} %get-tuple-element.230.lower_ref, f32[192,128]{1,0:T(8,128)S(1)} %get-tuple-element.231.fresh_ref, ...), custom_call_target="tpu_custom_call" | custom-call | flops 100000000 | bytes 1 | tf_op jit(solution)/shard_map/query/pallas_call | solution.py:262
  34.6 1.1 %collective-permute-done.7.state_ref.refs_19_.refs_4_ = f32[2,128,128]{2,1,0:T(8,128)S(1)} collective-permute-done((f32[2,128,128]{2,1,0:T(8,128)S(1)}, f32[2,128,128]{2,1,0:T(8,128)S(1)}, u32[]{:S(2)}, u32[]{:S(2)}) %collective-permute-start.7) | collective-permute-done | bytes 131104 | tf_op jit(solution)/shard_map/ppermute | solution.py:497
  36.1 0.9 %query.8 = (f32[192,512]{1,0:T(8,128)S(1)}, f32[192,512]{1,0:T(8,128)S(1)}) custom-call(bf16[192,2048]{1,0:T(8,128)(2,1)S(1)} %get-tuple-element.229.q_ref, f32[16,192]{1,0:T(8,128)S(1)} %get-tuple-element.164.beta_ref, f32[192,192]{1,0:T(8,128)S(1)} %get-tuple-element.230.lower_ref, f32[192,128]{1,0:T(8,128)S(1)} %get-tuple-element.231.fresh_ref, ...), custom_call_target="tpu_custom_call" | custom-call | flops 100000000 | bytes 1 | tf_op jit(solution)/shard_map/query/pallas_call | solution.py:262
  37.6 1.0 %collective-permute-done.10.refs_23_ = f32[2,128,128]{2,1,0:T(8,128)S(1)} collective-permute-done((f32[2,128,128]{2,1,0:T(8,128)S(1)}, f32[2,128,128]{2,1,0:T(8,128)S(1)}, u32[]{:S(2)}, u32[]{:S(2)}) %collective-permute-start.10) | collective-permute-done | bytes 131104 | tf_op jit(solution)/shard_map/ppermute | solution.py:497
  38.6 1.5 %finish.3.refs_6_ = bf16[192,2048]{1,0:T(8,128)(2,1)} custom-call(f32[8,192]{1,0:T(8,128)S(1)} %get-tuple-element.285.flags_ref.refs_0_, f32[1,2048]{1,0:T(1,128)S(1)} %bitcast.2, f32[192,256]{1,0:T(8,128)S(1)} %get-tuple-element.292.refs_0_, f32[192,256]{1,0:T(8,128)S(1)} %get-tuple-element.293.refs_1_, ...), custom_call_target="tpu_custom_call" | custom-call | flops 100000000 | bytes 1 | tf_op jit(solution)/shard_map/finish/pallas_call | solution.py:442
  40.6 1.0 %finish.4.refs_6_ = bf16[192,2048]{1,0:T(8,128)(2,1)} custom-call(f32[8,192]{1,0:T(8,128)S(1)} %get-tuple-element.285.flags_ref.refs_0_, f32[1,2048]{1,0:T(1,128)S(1)} %bitcast.3, f32[192,512]{1,0:T(8,128)S(1)} %get-tuple-element.289.refs_20_.refs_2_, f32[192,512]{1,0:T(8,128)S(1)} %get-tuple-element.290.refs_21_.refs_3_, ...), custom_call_target="tpu_custom_call", output_to_operand_aliasing={{}: (6, {})} | custom-call | flops 100000000 | bytes 1 | tf_op jit(solution)/shard_map/finish/pallas_call | solution.py:442
  41.6 1.2 %collective-permute-done.8.refs_5_ = f32[2,128,128]{2,1,0:T(8,128)S(1)} collective-permute-done((f32[2,128,128]{2,1,0:T(8,128)S(1)}, f32[2,128,128]{2,1,0:T(8,128)S(1)}, u32[]{:S(2)}, u32[]{:S(2)}) %collective-permute-start.8) | collective-permute-done | bytes 131104 | tf_op jit(solution)/shard_map/ppermute | solution.py:497
  42.8 1.0 %finish.5 = bf16[192,2048]{1,0:T(8,128)(2,1)} custom-call(f32[8,192]{1,0:T(8,128)S(1)} %get-tuple-element.285.flags_ref.refs_0_, f32[1,2048]{1,0:T(1,128)S(1)} %bitcast.4, f32[192,256]{1,0:T(8,128)S(1)} %get-tuple-element.286.refs_2_, f32[192,256]{1,0:T(8,128)S(1)} %get-tuple-element.287.refs_3_, ...), custom_call_target="tpu_custom_call", output_to_operand_aliasing={{}: (6, {})} | custom-call | flops 100000000 | bytes 1 | tf_op jit(solution)/shard_map/finish/pallas_call | solution.py:442
  (21 shorter events, 3.7 us)
Async XLA Ops:
  3.5 12.2 %collective-permute-start = (f32[2,128,128]{2,1,0:T(8,128)S(1)}, f32[2,128,128]{2,1,0:T(8,128)S(1)}, u32[]{:S(2)}, u32[]{:S(2)}) collective-permute-start(f32[2,128,128]{2,1,0:T(8,128)S(1)} %get-tuple-element.189.refs_2_), channel_id=1, source_target_pairs={{0,1},{1,2},{2,3},{3,0},{4,5},{5,6},{6,7},{7,4},{8,9},{9,10},{10,1... | collective-permute-start | bytes 393224 | tf_op jit(solution)/shard_map/ppermute | solution.py:497
  9.6 8.2 %collective-permute-start.1 = (f32[2,128,128]{2,1,0:T(8,128)S(1)}, f32[2,128,128]{2,1,0:T(8,128)S(1)}, u32[]{:S(2)}, u32[]{:S(2)}) collective-permute-start(f32[2,128,128]{2,1,0:T(8,128)S(1)} %get-tuple-element.193.refs_2_), channel_id=1, source_target_pairs={{0,1},{1,2},{2,3},{3,0},{4,5},{5,6},{6,7},{7,4},{8,9},{9,10},{10,1... | collective-permute-start | bytes 393224 | tf_op jit(solution)/shard_map/ppermute | solution.py:497
  11.2 9.8 %collective-permute-start.2 = (f32[2,128,128]{2,1,0:T(8,128)S(1)}, f32[2,128,128]{2,1,0:T(8,128)S(1)}, u32[]{:S(2)}, u32[]{:S(2)}) collective-permute-start(f32[2,128,128]{2,1,0:T(8,128)S(1)} %get-tuple-element.208.refs_2_), channel_id=1, source_target_pairs={{0,1},{1,2},{2,3},{3,0},{4,5},{5,6},{6,7},{7,4},{8,9},{9,10},{10,1... | collective-permute-start | bytes 393224 | tf_op jit(solution)/shard_map/ppermute | solution.py:497
  15.9 7.6 %collective-permute-start.3 = (f32[2,128,128]{2,1,0:T(8,128)S(1)}, f32[2,128,128]{2,1,0:T(8,128)S(1)}, u32[]{:S(2)}, u32[]{:S(2)}) collective-permute-start(f32[2,128,128]{2,1,0:T(8,128)S(1)} %pass_on.8), channel_id=1, source_target_pairs={{0,1},{1,2},{2,3},{3,0},{4,5},{5,6},{6,7},{7,4},{8,9},{9,10},{10,1... | collective-permute-start | bytes 393224 | tf_op jit(solution)/shard_map/ppermute | solution.py:497
  18.0 9.3 %collective-permute-start.4 = (f32[2,128,128]{2,1,0:T(8,128)S(1)}, f32[2,128,128]{2,1,0:T(8,128)S(1)}, u32[]{:S(2)}, u32[]{:S(2)}) collective-permute-start(f32[2,128,128]{2,1,0:T(8,128)S(1)} %pass_on.9), channel_id=1, source_target_pairs={{0,1},{1,2},{2,3},{3,0},{4,5},{5,6},{6,7},{7,4},{8,9},{9,10},{10,1... | collective-permute-start | bytes 393224 | tf_op jit(solution)/shard_map/ppermute | solution.py:497
  21.2 8.8 %collective-permute-start.5 = (f32[2,128,128]{2,1,0:T(8,128)S(1)}, f32[2,128,128]{2,1,0:T(8,128)S(1)}, u32[]{:S(2)}, u32[]{:S(2)}) collective-permute-start(f32[2,128,128]{2,1,0:T(8,128)S(1)} %pass_on.10), channel_id=1, source_target_pairs={{0,1},{1,2},{2,3},{3,0},{4,5},{5,6},{6,7},{7,4},{8,9},{9,10},{10,1... | collective-permute-start | bytes 393224 | tf_op jit(solution)/shard_map/ppermute | solution.py:497
  23.8 8.1 %collective-permute-start.6 = (f32[2,128,128]{2,1,0:T(8,128)S(1)}, f32[2,128,128]{2,1,0:T(8,128)S(1)}, u32[]{:S(2)}, u32[]{:S(2)}) collective-permute-start(f32[2,128,128]{2,1,0:T(8,128)S(1)} %pass_on.11), channel_id=1, source_target_pairs={{0,1},{1,2},{2,3},{3,0},{4,5},{5,6},{6,7},{7,4},{8,9},{9,10},{10,1... | collective-permute-start | bytes 393224 | tf_op jit(solution)/shard_map/ppermute | solution.py:497
  27.5 8.3 %collective-permute-start.7 = (f32[2,128,128]{2,1,0:T(8,128)S(1)}, f32[2,128,128]{2,1,0:T(8,128)S(1)}, u32[]{:S(2)}, u32[]{:S(2)}) collective-permute-start(f32[2,128,128]{2,1,0:T(8,128)S(1)} %pass_on.12), channel_id=1, source_target_pairs={{0,1},{1,2},{2,3},{3,0},{4,5},{5,6},{6,7},{7,4},{8,9},{9,10},{10,1... | collective-permute-start | bytes 393224 | tf_op jit(solution)/shard_map/ppermute | solution.py:497
  30.2 8.4 %collective-permute-start.10 = (f32[2,128,128]{2,1,0:T(8,128)S(1)}, f32[2,128,128]{2,1,0:T(8,128)S(1)}, u32[]{:S(2)}, u32[]{:S(2)}) collective-permute-start(f32[2,128,128]{2,1,0:T(8,128)S(1)} %pass_on.13), channel_id=1, source_target_pairs={{0,1},{1,2},{2,3},{3,0},{4,5},{5,6},{6,7},{7,4},{8,9},{9,10},{10,1... | collective-permute-start | bytes 393224 | tf_op jit(solution)/shard_map/ppermute | solution.py:497
  32.0 8.6 %collective-permute-start.9 = (f32[2,128,128]{2,1,0:T(8,128)S(1)}, f32[2,128,128]{2,1,0:T(8,128)S(1)}, u32[]{:S(2)}, u32[]{:S(2)}) collective-permute-start(f32[2,128,128]{2,1,0:T(8,128)S(1)} %pass_on.14), channel_id=1, source_target_pairs={{0,1},{1,2},{2,3},{3,0},{4,5},{5,6},{6,7},{7,4},{8,9},{9,10},{10,1... | collective-permute-start | bytes 393224 | tf_op jit(solution)/shard_map/ppermute | solution.py:497
  36.0 6.8 %collective-permute-start.8 = (f32[2,128,128]{2,1,0:T(8,128)S(1)}, f32[2,128,128]{2,1,0:T(8,128)S(1)}, u32[]{:S(2)}, u32[]{:S(2)}) collective-permute-start(f32[2,128,128]{2,1,0:T(8,128)S(1)} %pass_on.15), channel_id=1, source_target_pairs={{0,1},{1,2},{2,3},{3,0},{4,5},{5,6},{6,7},{7,4},{8,9},{9,10},{10,1... | collective-permute-start | bytes 393224 | tf_op jit(solution)/shard_map/ppermute | solution.py:497
  36.9 1.7 %copy-start = (f32[2048]{0:T(1024)S(1)}, f32[2048]{0:T(1024)}, u32[]{:S(2)}) copy-start(f32[2048]{0:T(1024)} %param.12) | copy-start | bytes 24580

commit v6 on v5

--- a/solution.py
+++ b/solution.py
@@ -11,7 +11,7 @@
 BF16 = jnp.bfloat16
 TILE = 16
 BLOCK = 64
-SPANS = ((2,), (2, 2), (2, 2), (2, 2), (2,))
+SPANS = ((2,), (2, 2, 2), (2, 2, 2, 2))
 LAG = 3
 FILL = (1,) * 99
 LATE = 2

time: 44.1 us -> 43.9 us (level)
  waiting for transfers between devices: 6.98 us -> 12 us
  Pallas kernels: 23.8 us -> 20.3 us
  starting transfers between devices: 12.8 us -> 11.1 us
    ppermute x11, waiting for transfers between devices: 6.98 us -> 12 us  [local(): received.append(lax.ppermute(sent, 'ctx', ring))]
    pallas_call x4 -> x2, Pallas kernels: 11.2 us -> 8.37 us  [span(): pl.pallas_call(functools.partial(span_kernel, head), in_specs=[VMEM] * le...]
    ppermute x11, starting transfers between devices: 12.8 us -> 11.1 us  [local(): received.append(lax.ppermute(sent, 'ctx', ring))]
    pallas_call x5 -> x3, Pallas kernels: 3.93 us -> 3.36 us  [query(): pl.pallas_call(functools.partial(query_kernel, head), in_specs=[VMEM] * l...]
  transfers between devices with their start and end apart: 11 -> 11, of which waited for: 7 -> 10; matrix products, arithmetic and copies ran while one was open for 0% -> 0% of each run, Pallas kernels for 44% -> 36%
where the time goes in v6:
time: 43.9 us; the launch traced here: 43.8 us
  Pallas kernels  20.3 us (46%)
  waiting for transfers between devices  12 us (27%)
  starting transfers between devices  11.1 us (25%)
    ppermute x11, waiting for transfers between devices, local(): received.append(lax.ppermute(sent, 'ctx', ring))  12 us
    ppermute x11, starting transfers between devices, local(): received.append(lax.ppermute(sent, 'ctx', ring))  11.1 us
    pallas_call x2, Pallas kernels, span(): pl.pallas_call(functools.partial(span_kernel, head), in_specs=[VMEM] * le...  8.37 us
    pallas_call x1, Pallas kernels, opening(): pl.pallas_call(functools.partial(opening_kernel, most), in_specs=[ANY] *...  3.54 us
    pallas_call x3, Pallas kernels, finished(): pl.pallas_call(kernel, in_specs=specs, out_specs=pl.BlockSpec(memory_spac...  3.5 us
    pallas_call x3, Pallas kernels, query(): pl.pallas_call(functools.partial(query_kernel, head), in_specs=[VMEM] * l...  3.36 us
    pallas_call x8, Pallas kernels, message(): pl.pallas_call(functools.partial(pass_kernel, len(own), low, len(late)),...  1.58 us
  transfers between devices with their start and end apart: 11, of which 10 were waited for; matrix products, arithmetic and copies ran while one was open for 0% of the time, Pallas kernels for 36%

profile of v6, /device:TPU:0, one launch (start us, length us, event | category | flops | bytes accessed | tf_op | source)
XLA Modules:
  0.0 43.8 jit_solution(10192347315944472019)
XLA Ops:
  0.0 3.5 %opening.1 = (f32[16,192]{1,0:T(8,128)S(1)}, bf16[192,2048]{1,0:T(8,128)(2,1)S(1)}, bf16[192,2048]{1,0:T(8,128)(2,1)S(1)}, bf16[192,2048]{1,0:T(8,128)(2,1)S(1)}...) custom-call(s32[16]{0:T(128)} %refs_0_.1, ...), custom_call_target="tpu_custom_call" | custom-call | flops 100000000 | bytes 1 | tf_op jit(solution)/shard_map/opening/pallas_call | solution.py:326
  3.5 3.1 %collective-permute-start = (f32[2,128,128]{2,1,0:T(8,128)S(1)}, f32[2,128,128]{2,1,0:T(8,128)S(1)}, u32[]{:S(2)}, u32[]{:S(2)}) collective-permute-start(f32[2,128,128]{2,1,0:T(8,128)S(1)} %get-tuple-element.144.refs_2_), channel_id=1, source_target_pairs={{0,1},{1,2},{2,3},{3,0},{4,5},{5,6},{6,7},{7,4},{8,9},{9,10},{10,1... | collective-permute-start | bytes 393224 | tf_op jit(solution)/shard_map/ppermute | solution.py:497
  6.6 3.7 %span.2 = (f32[192,768]{1,0:T(8,128)S(1)}, f32[8,768]{1,0:T(8,128)S(1)}, bf16[192,768]{1,0:T(8,128)(2,1)S(1)}, bf16[192,768]{1,0:T(8,128)(2,1)S(1)}, bf16[192,15...) custom-call(bf16[192,2048]{1,0:T(8,128)(2,1)S(1)} %get-tuple-element, ...), custom_call_target="tpu_custom_call" | custom-call | flops 100000000 | bytes 1 | tf_op jit(solution)/shard_map/span/pallas_call | solution.py:348
  10.3 1.6 %collective-permute-start.1 = (f32[2,128,128]{2,1,0:T(8,128)S(1)}, f32[2,128,128]{2,1,0:T(8,128)S(1)}, u32[]{:S(2)}, u32[]{:S(2)}) collective-permute-start(f32[2,128,128]{2,1,0:T(8,128)S(1)} %get-tuple-element.163.refs_2_), channel_id=1, source_target_pairs={{0,1},{1,2},{2,3},{3,0},{4,5},{5,6},{6,7},{7,4},{8,9},{9,10},{10,1... | collective-permute-start | bytes 393224 | tf_op jit(solution)/shard_map/ppermute | solution.py:497
  12.0 1.6 %collective-permute-start.2 = (f32[2,128,128]{2,1,0:T(8,128)S(1)}, f32[2,128,128]{2,1,0:T(8,128)S(1)}, u32[]{:S(2)}, u32[]{:S(2)}) collective-permute-start(f32[2,128,128]{2,1,0:T(8,128)S(1)} %get-tuple-element.167.refs_2_), channel_id=1, source_target_pairs={{0,1},{1,2},{2,3},{3,0},{4,5},{5,6},{6,7},{7,4},{8,9},{9,10},{10,1... | collective-permute-start | bytes 393224 | tf_op jit(solution)/shard_map/ppermute | solution.py:497
  13.9 4.7 %span.3 = (f32[192,1024]{1,0:T(8,128)S(1)}, f32[8,1024]{1,0:T(8,128)S(1)}, bf16[192,1024]{1,0:T(8,128)(2,1)S(1)}, bf16[192,1024]{1,0:T(8,128)(2,1)S(1)}, bf16[19...) custom-call(bf16[192,2048]{1,0:T(8,128)(2,1)S(1)} %get-tuple-element, ...), custom_call_target="tpu_custom_call" | custom-call | flops 100000000 | bytes 1 | tf_op jit(solution)/shard_map/span/pallas_call | solution.py:348
  18.8 1.7 %collective-permute-start.4 = (f32[2,128,128]{2,1,0:T(8,128)S(1)}, f32[2,128,128]{2,1,0:T(8,128)S(1)}, u32[]{:S(2)}, u32[]{:S(2)}) collective-permute-start(f32[2,128,128]{2,1,0:T(8,128)S(1)} %pass_on.9), channel_id=1, source_target_pairs={{0,1},{1,2},{2,3},{3,0},{4,5},{5,6},{6,7},{7,4},{8,9},{9,10},{10,1... | collective-permute-start | bytes 393224 | tf_op jit(solution)/shard_map/ppermute | solution.py:497
  20.5 0.8 %collective-permute-done.2.state_ref.refs_10_ = f32[2,128,128]{2,1,0:T(8,128)S(1)} collective-permute-done((f32[2,128,128]{2,1,0:T(8,128)S(1)}, f32[2,128,128]{2,1,0:T(8,128)S(1)}, u32[]{:S(2)}, u32[]{:S(2)}) %collective-permute-start.2) | collective-permute-done | bytes 131104 | tf_op jit(solution)/shard_map/ppermute | solution.py:497
  21.6 0.8 %collective-permute-start.5 = (f32[2,128,128]{2,1,0:T(8,128)S(1)}, f32[2,128,128]{2,1,0:T(8,128)S(1)}, u32[]{:S(2)}, u32[]{:S(2)}) collective-permute-start(f32[2,128,128]{2,1,0:T(8,128)S(1)} %pass_on.10), channel_id=1, source_target_pairs={{0,1},{1,2},{2,3},{3,0},{4,5},{5,6},{6,7},{7,4},{8,9},{9,10},{10,1... | collective-permute-start | bytes 393224 | tf_op jit(solution)/shard_map/ppermute | solution.py:497
  22.4 0.9 %collective-permute-done.3.state_ref.refs_3_.refs_14_ = f32[2,128,128]{2,1,0:T(8,128)S(1)} collective-permute-done((f32[2,128,128]{2,1,0:T(8,128)S(1)}, f32[2,128,128]{2,1,0:T(8,128)S(1)}, u32[]{:S(2)}, u32[]{:S(2)}) %collective-permute-start.3) | collective-permute-done | bytes 131104 | tf_op jit(solution)/shard_map/ppermute | solution.py:497
  23.5 0.7 %collective-permute-start.6 = (f32[2,128,128]{2,1,0:T(8,128)S(1)}, f32[2,128,128]{2,1,0:T(8,128)S(1)}, u32[]{:S(2)}, u32[]{:S(2)}) collective-permute-start(f32[2,128,128]{2,1,0:T(8,128)S(1)} %pass_on.11), channel_id=1, source_target_pairs={{0,1},{1,2},{2,3},{3,0},{4,5},{5,6},{6,7},{7,4},{8,9},{9,10},{10,1... | collective-permute-start | bytes 393224 | tf_op jit(solution)/shard_map/ppermute | solution.py:497
  24.2 2.9 %collective-permute-done.4.state_ref.refs_7_.refs_18_ = f32[2,128,128]{2,1,0:T(8,128)S(1)} collective-permute-done((f32[2,128,128]{2,1,0:T(8,128)S(1)}, f32[2,128,128]{2,1,0:T(8,128)S(1)}, u32[]{:S(2)}, u32[]{:S(2)}) %collective-permute-start.4) | collective-permute-done | bytes 131104 | tf_op jit(solution)/shard_map/ppermute | solution.py:497
  27.4 0.7 %query.3 = (f32[192,256]{1,0:T(8,128)S(1)}, f32[192,256]{1,0:T(8,128)S(1)}) custom-call(bf16[192,2048]{1,0:T(8,128)(2,1)S(1)} %get-tuple-element.179.q_ref, f32[16,192]{1,0:T(8,128)S(1)} %get-tuple-element.128.beta_ref, f32[192,192]{1,0:T(8,128)S(1)} %get-tuple-element.180.lower_ref, f32[192,128]{1,0:T(8,128)S(1)} %get-tuple-element.181.fresh_ref, ...), custom_call_target="tpu_custom_call" | custom-call | flops 100000000 | bytes 1 | tf_op jit(solution)/shard_map/query/pallas_call | solution.py:262
  28.1 1.9 %collective-permute-done.5.state_ref.refs_11_.refs_22_ = f32[2,128,128]{2,1,0:T(8,128)S(1)} collective-permute-done((f32[2,128,128]{2,1,0:T(8,128)S(1)}, f32[2,128,128]{2,1,0:T(8,128)S(1)}, u32[]{:S(2)}, u32[]{:S(2)}) %collective-permute-start.5) | collective-permute-done | bytes 131104 | tf_op jit(solution)/shard_map/ppermute | solution.py:497
  30.4 1.2 %query.4 = (f32[192,768]{1,0:T(8,128)S(1)}, f32[192,768]{1,0:T(8,128)S(1)}) custom-call(bf16[192,2048]{1,0:T(8,128)(2,1)S(1)} %get-tuple-element.179.q_ref, f32[16,192]{1,0:T(8,128)S(1)} %get-tuple-element.128.beta_ref, f32[192,192]{1,0:T(8,128)S(1)} %get-tuple-element.180.lower_ref, f32[192,128]{1,0:T(8,128)S(1)} %get-tuple-element.181.fresh_ref, ...), custom_call_target="tpu_custom_call" | custom-call | flops 100000000 | bytes 1 | tf_op jit(solution)/shard_map/query/pallas_call | solution.py:262
  31.6 1.2 %collective-permute-done.6.state_ref.refs_15_.refs_4_ = f32[2,128,128]{2,1,0:T(8,128)S(1)} collective-permute-done((f32[2,128,128]{2,1,0:T(8,128)S(1)}, f32[2,128,128]{2,1,0:T(8,128)S(1)}, u32[]{:S(2)}, u32[]{:S(2)}) %collective-permute-start.6) | collective-permute-done | bytes 131104 | tf_op jit(solution)/shard_map/ppermute | solution.py:497
  33.2 1.5 %query.5 = (f32[192,1024]{1,0:T(8,128)S(1)}, f32[192,1024]{1,0:T(8,128)S(1)}) custom-call(bf16[192,2048]{1,0:T(8,128)(2,1)S(1)} %get-tuple-element.179.q_ref, f32[16,192]{1,0:T(8,128)S(1)} %get-tuple-element.128.beta_ref, f32[192,192]{1,0:T(8,128)S(1)} %get-tuple-element.180.lower_ref, f32[192,128]{1,0:T(8,128)S(1)} %get-tuple-element.181.fresh_ref, ...), custom_call_target="tpu_custom_call" | custom-call | flops 100000000 | bytes 1 | tf_op jit(solution)/shard_map/query/pallas_call | solution.py:262
  34.8 0.8 %collective-permute-done.7.state_ref.refs_19_.refs_4_ = f32[2,128,128]{2,1,0:T(8,128)S(1)} collective-permute-done((f32[2,128,128]{2,1,0:T(8,128)S(1)}, f32[2,128,128]{2,1,0:T(8,128)S(1)}, u32[]{:S(2)}, u32[]{:S(2)}) %collective-permute-start.7) | collective-permute-done | bytes 131104 | tf_op jit(solution)/shard_map/ppermute | solution.py:497
  35.8 0.9 %collective-permute-start.8 = (f32[2,128,128]{2,1,0:T(8,128)S(1)}, f32[2,128,128]{2,1,0:T(8,128)S(1)}, u32[]{:S(2)}, u32[]{:S(2)}) collective-permute-start(f32[2,128,128]{2,1,0:T(8,128)S(1)} %pass_on.15), channel_id=1, source_target_pairs={{0,1},{1,2},{2,3},{3,0},{4,5},{5,6},{6,7},{7,4},{8,9},{9,10},{10,1... | collective-permute-start | bytes 393224 | tf_op jit(solution)/shard_map/ppermute | solution.py:497
  36.7 1.9 %collective-permute-done.10.refs_23_ = f32[2,128,128]{2,1,0:T(8,128)S(1)} collective-permute-done((f32[2,128,128]{2,1,0:T(8,128)S(1)}, f32[2,128,128]{2,1,0:T(8,128)S(1)}, u32[]{:S(2)}, u32[]{:S(2)}) %collective-permute-start.10) | collective-permute-done | bytes 131104 | tf_op jit(solution)/shard_map/ppermute | solution.py:497
  38.6 1.5 %finish.3.refs_6_ = bf16[192,2048]{1,0:T(8,128)(2,1)} custom-call(f32[8,192]{1,0:T(8,128)S(1)} %get-tuple-element.217.flags_ref.refs_0_, f32[1,2048]{1,0:T(1,128)S(1)} %bitcast.2, f32[192,256]{1,0:T(8,128)S(1)} %get-tuple-element.222.refs_0_, f32[192,256]{1,0:T(8,128)S(1)} %get-tuple-element.223.refs_1_, ...), custom_call_target="tpu_custom_call" | custom-call | flops 100000000 | bytes 1 | tf_op jit(solution)/shard_map/finish/pallas_call | solution.py:442
  40.1 0.9 %collective-permute-done.9.refs_5_ = f32[2,128,128]{2,1,0:T(8,128)S(1)} collective-permute-done((f32[2,128,128]{2,1,0:T(8,128)S(1)}, f32[2,128,128]{2,1,0:T(8,128)S(1)}, u32[]{:S(2)}, u32[]{:S(2)}) %collective-permute-start.9) | collective-permute-done | bytes 131104 | tf_op jit(solution)/shard_map/ppermute | solution.py:497
  41.0 1.0 %finish.4.refs_6_ = bf16[192,2048]{1,0:T(8,128)(2,1)} custom-call(f32[8,192]{1,0:T(8,128)S(1)} %get-tuple-element.217.flags_ref.refs_0_, f32[1,2048]{1,0:T(1,128)S(1)} %bitcast.3, f32[192,1024]{1,0:T(8,128)S(1)} %get-tuple-element.218.refs_16_.refs_20_.refs_2_, ...), custom_call_target="tpu_custom_call", output_to_operand_aliasing={{}: (6, {})} | custom-call | flops 100000000 | bytes 1 | tf_op jit(solution)/shard_map/finish/pallas_call | solution.py:442
  42.6 1.0 %finish.5 = bf16[192,2048]{1,0:T(8,128)(2,1)} custom-call(f32[8,192]{1,0:T(8,128)S(1)} %get-tuple-element.217.flags_ref.refs_0_, f32[1,2048]{1,0:T(1,128)S(1)} %bitcast.4, f32[192,1024]{1,0:T(8,128)S(1)} %get-tuple-element.218.refs_16_.refs_20_.refs_2_, f32[192,1024]{1,0:T(8,128)S(1)} %get-tuple-element.219.refs_17_.refs_21_.refs_3_, ...), custom_call_target="tpu_custom_call", output_to_operand_aliasing={{}: (6, {})} | custom-call | flops 100000000 | bytes 1 | tf_op jit(solution)/shard_map/finish/pallas_call | solution.py:442
  (17 shorter events, 3.0 us)
Async XLA Ops:
  3.5 10.0 %collective-permute-start = (f32[2,128,128]{2,1,0:T(8,128)S(1)}, f32[2,128,128]{2,1,0:T(8,128)S(1)}, u32[]{:S(2)}, u32[]{:S(2)}) collective-permute-start(f32[2,128,128]{2,1,0:T(8,128)S(1)} %get-tuple-element.144.refs_2_), channel_id=1, source_target_pairs={{0,1},{1,2},{2,3},{3,0},{4,5},{5,6},{6,7},{7,4},{8,9},{9,10},{10,1... | collective-permute-start | bytes 393224 | tf_op jit(solution)/shard_map/ppermute | solution.py:497
  10.3 8.3 %collective-permute-start.1 = (f32[2,128,128]{2,1,0:T(8,128)S(1)}, f32[2,128,128]{2,1,0:T(8,128)S(1)}, u32[]{:S(2)}, u32[]{:S(2)}) collective-permute-start(f32[2,128,128]{2,1,0:T(8,128)S(1)} %get-tuple-element.163.refs_2_), channel_id=1, source_target_pairs={{0,1},{1,2},{2,3},{3,0},{4,5},{5,6},{6,7},{7,4},{8,9},{9,10},{10,1... | collective-permute-start | bytes 393224 | tf_op jit(solution)/shard_map/ppermute | solution.py:497
  12.0 9.4 %collective-permute-start.2 = (f32[2,128,128]{2,1,0:T(8,128)S(1)}, f32[2,128,128]{2,1,0:T(8,128)S(1)}, u32[]{:S(2)}, u32[]{:S(2)}) collective-permute-start(f32[2,128,128]{2,1,0:T(8,128)S(1)} %get-tuple-element.167.refs_2_), channel_id=1, source_target_pairs={{0,1},{1,2},{2,3},{3,0},{4,5},{5,6},{6,7},{7,4},{8,9},{9,10},{10,1... | collective-permute-start | bytes 393224 | tf_op jit(solution)/shard_map/ppermute | solution.py:497
  13.8 9.5 %collective-permute-start.3 = (f32[2,128,128]{2,1,0:T(8,128)S(1)}, f32[2,128,128]{2,1,0:T(8,128)S(1)}, u32[]{:S(2)}, u32[]{:S(2)}) collective-permute-start(f32[2,128,128]{2,1,0:T(8,128)S(1)} %pass_on.8), channel_id=1, source_target_pairs={{0,1},{1,2},{2,3},{3,0},{4,5},{5,6},{6,7},{7,4},{8,9},{9,10},{10,1... | collective-permute-start | bytes 393224 | tf_op jit(solution)/shard_map/ppermute | solution.py:497
  18.8 8.3 %collective-permute-start.4 = (f32[2,128,128]{2,1,0:T(8,128)S(1)}, f32[2,128,128]{2,1,0:T(8,128)S(1)}, u32[]{:S(2)}, u32[]{:S(2)}) collective-permute-start(f32[2,128,128]{2,1,0:T(8,128)S(1)} %pass_on.9), channel_id=1, source_target_pairs={{0,1},{1,2},{2,3},{3,0},{4,5},{5,6},{6,7},{7,4},{8,9},{9,10},{10,1... | collective-permute-start | bytes 393224 | tf_op jit(solution)/shard_map/ppermute | solution.py:497
  21.6 8.4 %collective-permute-start.5 = (f32[2,128,128]{2,1,0:T(8,128)S(1)}, f32[2,128,128]{2,1,0:T(8,128)S(1)}, u32[]{:S(2)}, u32[]{:S(2)}) collective-permute-start(f32[2,128,128]{2,1,0:T(8,128)S(1)} %pass_on.10), channel_id=1, source_target_pairs={{0,1},{1,2},{2,3},{3,0},{4,5},{5,6},{6,7},{7,4},{8,9},{9,10},{10,1... | collective-permute-start | bytes 393224 | tf_op jit(solution)/shard_map/ppermute | solution.py:497
  23.5 9.3 %collective-permute-start.6 = (f32[2,128,128]{2,1,0:T(8,128)S(1)}, f32[2,128,128]{2,1,0:T(8,128)S(1)}, u32[]{:S(2)}, u32[]{:S(2)}) collective-permute-start(f32[2,128,128]{2,1,0:T(8,128)S(1)} %pass_on.11), channel_id=1, source_target_pairs={{0,1},{1,2},{2,3},{3,0},{4,5},{5,6},{6,7},{7,4},{8,9},{9,10},{10,1... | collective-permute-start | bytes 393224 | tf_op jit(solution)/shard_map/ppermute | solution.py:497
  27.3 8.3 %collective-permute-start.7 = (f32[2,128,128]{2,1,0:T(8,128)S(1)}, f32[2,128,128]{2,1,0:T(8,128)S(1)}, u32[]{:S(2)}, u32[]{:S(2)}) collective-permute-start(f32[2,128,128]{2,1,0:T(8,128)S(1)} %pass_on.12), channel_id=1, source_target_pairs={{0,1},{1,2},{2,3},{3,0},{4,5},{5,6},{6,7},{7,4},{8,9},{9,10},{10,1... | collective-permute-start | bytes 393224 | tf_op jit(solution)/shard_map/ppermute | solution.py:497
  30.1 8.5 %collective-permute-start.10 = (f32[2,128,128]{2,1,0:T(8,128)S(1)}, f32[2,128,128]{2,1,0:T(8,128)S(1)}, u32[]{:S(2)}, u32[]{:S(2)}) collective-permute-start(f32[2,128,128]{2,1,0:T(8,128)S(1)} %pass_on.13), channel_id=1, source_target_pairs={{0,1},{1,2},{2,3},{3,0},{4,5},{5,6},{6,7},{7,4},{8,9},{9,10},{10,1... | collective-permute-start | bytes 393224 | tf_op jit(solution)/shard_map/ppermute | solution.py:497
  32.9 8.1 %collective-permute-start.9 = (f32[2,128,128]{2,1,0:T(8,128)S(1)}, f32[2,128,128]{2,1,0:T(8,128)S(1)}, u32[]{:S(2)}, u32[]{:S(2)}) collective-permute-start(f32[2,128,128]{2,1,0:T(8,128)S(1)} %pass_on.14), channel_id=1, source_target_pairs={{0,1},{1,2},{2,3},{3,0},{4,5},{5,6},{6,7},{7,4},{8,9},{9,10},{10,1... | collective-permute-start | bytes 393224 | tf_op jit(solution)/shard_map/ppermute | solution.py:497
  34.8 3.8 %copy-start = (f32[2048]{0:T(1024)S(1)}, f32[2048]{0:T(1024)}, u32[]{:S(2)}) copy-start(f32[2048]{0:T(1024)} %param.12) | copy-start | bytes 24580
  35.8 6.8 %collective-permute-start.8 = (f32[2,128,128]{2,1,0:T(8,128)S(1)}, f32[2,128,128]{2,1,0:T(8,128)S(1)}, u32[]{:S(2)}, u32[]{:S(2)}) collective-permute-start(f32[2,128,128]{2,1,0:T(8,128)S(1)} %pass_on.15), channel_id=1, source_target_pairs={{0,1},{1,2},{2,3},{3,0},{4,5},{5,6},{6,7},{7,4},{8,9},{9,10},{10,1... | collective-permute-start | bytes 393224 | tf_op jit(solution)/shard_map/ppermute | solution.py:497
